TPU v7x, 512 devices: a whole 4x4x16 slice. The times are simulated.
512 devices in a mesh: blk: 8 (over x, z_hi), grp: 64 (over y, z_lo, core).
Axes of the slice: x: 4, y: 4, z: 16 (z_hi: 2, z_lo: 8; z = z_hi * 8 + z_lo), core: 2. Of those that a mesh axis runs over, the one named last changes fastest.
Arguments:
- images: bfloat16 [8192, 1152], P(('blk', 'grp')), may hold values from -6 to 6
- texts: bfloat16 [8192, 1152], P(('blk', 'grp')), may hold values from -6 to 6
- scale: float32 [], replicated, may hold values from 8 to 16
- shift: float32 [], replicated, may hold values from -5 to -3
Outputs:
- image_loss: float32 [8192], P(('blk', 'grp'))
- image_grad: float32 [8192, 1152], P(('blk', 'grp'))
- text_grad: float32 [8192, 1152], P(('blk', 'grp'))
All inputs are finite; a program needn't handle non-finite values.
Results may differ from a plain program's by a relative error of at most 0.0045.
Values may be sent and summed in bfloat16 or wider, within the bound.
A program may use at most 64 MiB of HBM per device.

v0:
```python
import jax
import jax.numpy as jnp
from jax import lax
from jax.sharding import PartitionSpec as P


def passed_along(value, axis, steps):
    count = lax.axis_size(axis)
    pairs = [(source, (source + steps) % count) for source in range(count)]
    return lax.ppermute(value, axis, pairs)


def unit_rows(values):
    floats = values.astype(jnp.float32)
    norms = jnp.sqrt(jnp.sum(floats * floats, 1, keepdims=True) + 1e-06)
    return (floats / norms, norms)


def back_rows(grads, units, norms):
    return (grads - units * jnp.sum(units * grads, 1, keepdims=True)) / norms


def local(images, texts, scale, shift):
    rows = images.shape[0]
    image_unit, image_norm = unit_rows(images)
    text_unit, text_norm = unit_rows(texts)
    image_emb = image_unit.astype(jnp.bfloat16)
    text_emb = text_unit.astype(jnp.bfloat16)
    gathered = lax.all_gather(image_emb, "grp", axis=0, tiled=True)
    groups = lax.axis_size("grp")
    loops = lax.axis_size("blk")
    total = loops * groups * rows
    place = lax.axis_index("grp")
    image_ids = jnp.arange(groups * rows, dtype=jnp.int32)[:, None]
    column_ids = place * rows + jnp.arange(rows, dtype=jnp.int32)[None, :]
    own_label = (image_ids == column_ids).astype(jnp.float32)
    zero_label = jnp.zeros_like(own_label)
    text_now = text_emb
    loss_sum = jnp.zeros((groups * rows,), jnp.float32)
    carried = jnp.zeros((rows, images.shape[1]), jnp.float32)
    coefs = []
    seen = []
    for step in range(loops):
        label = own_label if step == 0 else zero_label
        logit = (
            scale
            * lax.dot_general(
                gathered, text_now, (((1,), (1,)), ((), ())), preferred_element_type=jnp.float32
            )
            + shift
        )
        loss = jnp.sum(jax.nn.softplus(logit * (1.0 - 2.0 * label)), 1) / total
        coef = ((jax.nn.sigmoid(logit) - label) * scale).astype(jnp.bfloat16)
        grad_text = lax.dot_general(
            coef, gathered, (((0,), (0,)), ((), ())), preferred_element_type=jnp.float32
        )
        loss, coef, grad_text = (loss, coef, grad_text)
        loss_sum = loss_sum + loss
        coefs.append(coef)
        seen.append(text_now)
        carried = passed_along(carried + grad_text, "blk", 1)
        if step + 1 < loops:
            text_now = passed_along(text_now, "blk", 1)
    left_side = jnp.concatenate(coefs, 1)
    right_side = jnp.concatenate(seen, 0)
    image_part = jnp.dot(left_side, right_side, preferred_element_type=jnp.float32)
    received = (
        lax.all_to_all(
            image_part.reshape(groups, rows, -1), "grp", split_axis=0, concat_axis=0, tiled=True
        ),
        lax.all_to_all(
            loss_sum.reshape(groups, rows), "grp", split_axis=0, concat_axis=0, tiled=True
        ),
    )
    image_sum = jnp.sum(received[0], 0)
    image_loss = jnp.sum(received[1], 0)
    image_grad = back_rows(image_sum, image_unit, image_norm)
    text_grad = back_rows(carried, text_unit, text_norm)
    return (image_loss, image_grad, text_grad)


def solution(mesh):
    in_specs = (P(("blk", "grp"), None), P(("blk", "grp"), None), P(), P())
    out_specs = (P(("blk", "grp")), P(("blk", "grp"), None), P(("blk", "grp"), None))
    return jax.shard_map(local, mesh=mesh, in_specs=in_specs, out_specs=out_specs, check_vma=False)
```

profile of v0, /device:TPU:64, one launch (start us, length us, event | category | flops | bytes accessed | tf_op | source)
XLA Modules:
  0.0 534.5 jit_solution(2764309689778662927)
XLA Ops:
  11.4 13.9 %collective-permute-start = (bf16[16,1152]{1,0:T(8,128)(2,1)S(1)}, bf16[16,1152]{1,0:T(8,128)(2,1)S(1)}, u32[]{:S(2)}, u32[]{:S(2)}) collective-permute-start(bf16[16,1152]{1,0:T(8,128)(2,1)S(1)} %get-tuple-element.4), channel_id=1, source_target_pairs={{0,64},{64,128},{128,192},{192,256},{256,320},{320,384},{384,448},... | collective-permute-start | bytes 110600 | tf_op jit(solution)/shard_map/ppermute | solution.py:10
  29.9 10.2 %collective-permute-start.1 = (bf16[16,1152]{1,0:T(8,128)(2,1)S(1)}, bf16[16,1152]{1,0:T(8,128)(2,1)S(1)}, u32[]{:S(2)}, u32[]{:S(2)}) collective-permute-start(bf16[16,1152]{1,0:T(8,128)(2,1)S(1)} %collective-permute-done), channel_id=1, source_target_pairs={{0,64},{64,128},{128,192},{192,256},{256,320},{320,384},{384,448},... | collective-permute-start | bytes 110600 | tf_op jit(solution)/shard_map/ppermute | solution.py:10
  40.2 6.4 %collective-permute-done.1 = bf16[16,1152]{1,0:T(8,128)(2,1)S(1)} collective-permute-done((bf16[16,1152]{1,0:T(8,128)(2,1)S(1)}, bf16[16,1152]{1,0:T(8,128)(2,1)S(1)}, u32[]{:S(2)}, u32[]{:S(2)}) %collective-permute-start.1) | collective-permute-done | bytes 36896 | tf_op jit(solution)/shard_map/ppermute | solution.py:10
  46.6 8.1 %collective-permute-start.2 = (bf16[16,1152]{1,0:T(8,128)(2,1)S(1)}, bf16[16,1152]{1,0:T(8,128)(2,1)S(1)}, u32[]{:S(2)}, u32[]{:S(2)}) collective-permute-start(bf16[16,1152]{1,0:T(8,128)(2,1)S(1)} %collective-permute-done.1), channel_id=1, source_target_pairs={{0,64},{64,128},{128,192},{192,256},{256,320},{320,384},{384,448},... | collective-permute-start | bytes 110600 | tf_op jit(solution)/shard_map/ppermute | solution.py:10
  54.8 9.1 %collective-permute-done.2 = bf16[16,1152]{1,0:T(8,128)(2,1)S(1)} collective-permute-done((bf16[16,1152]{1,0:T(8,128)(2,1)S(1)}, bf16[16,1152]{1,0:T(8,128)(2,1)S(1)}, u32[]{:S(2)}, u32[]{:S(2)}) %collective-permute-start.2) | collective-permute-done | bytes 36896 | tf_op jit(solution)/shard_map/ppermute | solution.py:10
  63.9 5.5 %collective-permute-start.3 = (bf16[16,1152]{1,0:T(8,128)(2,1)S(1)}, bf16[16,1152]{1,0:T(8,128)(2,1)S(1)}, u32[]{:S(2)}, u32[]{:S(2)}) collective-permute-start(bf16[16,1152]{1,0:T(8,128)(2,1)S(1)} %collective-permute-done.2), channel_id=1, source_target_pairs={{0,64},{64,128},{128,192},{192,256},{256,320},{320,384},{384,448},... | collective-permute-start | bytes 110600 | tf_op jit(solution)/shard_map/ppermute | solution.py:10
  69.4 11.2 %collective-permute-done.3 = bf16[16,1152]{1,0:T(8,128)(2,1)S(1)} collective-permute-done((bf16[16,1152]{1,0:T(8,128)(2,1)S(1)}, bf16[16,1152]{1,0:T(8,128)(2,1)S(1)}, u32[]{:S(2)}, u32[]{:S(2)}) %collective-permute-start.3) | collective-permute-done | bytes 36896 | tf_op jit(solution)/shard_map/ppermute | solution.py:10
  80.6 3.4 collective-permute-start.4
  84.0 13.5 %collective-permute-done.4 = bf16[16,1152]{1,0:T(8,128)(2,1)S(1)} collective-permute-done((bf16[16,1152]{1,0:T(8,128)(2,1)S(1)}, bf16[16,1152]{1,0:T(8,128)(2,1)S(1)}, u32[]{:S(2)}, u32[]{:S(2)}) %collective-permute-start.4) | collective-permute-done | bytes 36896 | tf_op jit(solution)/shard_map/ppermute | solution.py:10
  99.5 14.9 %collective-permute-done.5 = bf16[16,1152]{1,0:T(8,128)(2,1)S(1)} collective-permute-done((bf16[16,1152]{1,0:T(8,128)(2,1)S(1)}, bf16[16,1152]{1,0:T(8,128)(2,1)S(1)}, u32[]{:S(2)}, u32[]{:S(2)}) %collective-permute-start.5) | collective-permute-done | bytes 36896 | tf_op jit(solution)/shard_map/ppermute | solution.py:10
  116.3 14.8 %collective-permute-done.6 = bf16[16,1152]{1,0:T(8,128)(2,1)S(1)} collective-permute-done((bf16[16,1152]{1,0:T(8,128)(2,1)S(1)}, bf16[16,1152]{1,0:T(8,128)(2,1)S(1)}, u32[]{:S(2)}, u32[]{:S(2)}) %collective-permute-start.6) | collective-permute-done | bytes 36896 | tf_op jit(solution)/shard_map/ppermute | solution.py:10
  131.1 5.8 %all-gather.2.cloned.1.call-done = bf16[1024,1152]{1,0:T(8,128)(2,1)} async-done(((bf16[16,1152]{1,0:T(8,128)(2,1)}), bf16[1024,1152]{1,0:T(8,128)(2,1)}) %all-gather.2.cloned.1.call-update) | async-done | bytes 2359312 | tf_op jit(solution)/shard_map/all_gather | solution.py:29
  145.5 8.8 %all-to-all-start = ((f32[64,1,16]{2,1,0:T(1,128)}), f32[64,1,16]{2,1,0:T(1,128)S(1)}, u32[]{:S(2)}, u32[]{:S(2)}) async-start(f32[64,1,16]{2,1,0:T(1,128)} %bitcast), calls=%async_computation | async-start | bytes 65536 | tf_op jit(solution)/shard_map/all_to_all | solution.py:71
  157.6 7.0 %all-to-all-done = f32[64,1,16]{2,1,0:T(1,128)S(1)} async-done(((f32[64,1,16]{2,1,0:T(1,128)}), f32[64,1,16]{2,1,0:T(1,128)S(1)}, u32[]{:S(2)}, u32[]{:S(2)}) %all-to-all-start) | async-done | bytes 4128 | tf_op jit(solution)/shard_map/all_to_all | solution.py:71
  164.6 7.6 %all-to-all-start.1 = ((f32[64,16,1152]{2,1,0:T(8,128)}), f32[64,16,1152]{2,1,0:T(8,128)}, u32[]{:S(2)}, u32[]{:S(2)}) async-start(f32[64,16,1152]{2,1,0:T(8,128)} %bitcast.28), calls=%async_computation.1 | async-start | bytes 9437184 | tf_op jit(solution)/shard_map/all_to_all | solution.py:68
  172.7 8.2 %collective-permute-start.7 = (f32[16,1152]{1,0:T(8,128)S(1)}, f32[16,1152]{1,0:T(8,128)S(1)}, u32[]{:S(2)}, u32[]{:S(2)}) collective-permute-start(f32[16,1152]{1,0:T(8,128)S(1)} %fusion.26), channel_id=1, source_target_pairs={{0,64},{64,128},{128,192},{192,256},{256,320},{320,384},{384,448},... | collective-permute-start | bytes 221192 | tf_op jit(solution)/shard_map/ppermute | solution.py:10
  180.9 221.4 %collective-permute-done.7 = f32[16,1152]{1,0:T(8,128)S(1)} collective-permute-done((f32[16,1152]{1,0:T(8,128)S(1)}, f32[16,1152]{1,0:T(8,128)S(1)}, u32[]{:S(2)}, u32[]{:S(2)}) %collective-permute-start.7) | collective-permute-done | bytes 73760 | tf_op jit(solution)/shard_map/ppermute | solution.py:10
  406.2 13.6 %collective-permute-done.8 = f32[16,1152]{1,0:T(8,128)S(1)} collective-permute-done((f32[16,1152]{1,0:T(8,128)S(1)}, f32[16,1152]{1,0:T(8,128)S(1)}, u32[]{:S(2)}, u32[]{:S(2)}) %collective-permute-start.8) | collective-permute-done | bytes 73760 | tf_op jit(solution)/shard_map/ppermute | solution.py:10
  422.1 15.5 %collective-permute-done.9 = f32[16,1152]{1,0:T(8,128)S(1)} collective-permute-done((f32[16,1152]{1,0:T(8,128)S(1)}, f32[16,1152]{1,0:T(8,128)S(1)}, u32[]{:S(2)}, u32[]{:S(2)}) %collective-permute-start.9) | collective-permute-done | bytes 73760 | tf_op jit(solution)/shard_map/ppermute | solution.py:10
  440.0 14.8 %collective-permute-done.10 = f32[16,1152]{1,0:T(8,128)S(1)} collective-permute-done((f32[16,1152]{1,0:T(8,128)S(1)}, f32[16,1152]{1,0:T(8,128)S(1)}, u32[]{:S(2)}, u32[]{:S(2)}) %collective-permute-start.10) | collective-permute-done | bytes 73760 | tf_op jit(solution)/shard_map/ppermute | solution.py:10
  457.2 14.8 %collective-permute-done.11 = f32[16,1152]{1,0:T(8,128)S(1)} collective-permute-done((f32[16,1152]{1,0:T(8,128)S(1)}, f32[16,1152]{1,0:T(8,128)S(1)}, u32[]{:S(2)}, u32[]{:S(2)}) %collective-permute-start.11) | collective-permute-done | bytes 73760 | tf_op jit(solution)/shard_map/ppermute | solution.py:10
  474.4 14.7 %collective-permute-done.12 = f32[16,1152]{1,0:T(8,128)S(1)} collective-permute-done((f32[16,1152]{1,0:T(8,128)S(1)}, f32[16,1152]{1,0:T(8,128)S(1)}, u32[]{:S(2)}, u32[]{:S(2)}) %collective-permute-start.12) | collective-permute-done | bytes 73760 | tf_op jit(solution)/shard_map/ppermute | solution.py:10
  491.4 14.7 %collective-permute-done.13 = f32[16,1152]{1,0:T(8,128)S(1)} collective-permute-done((f32[16,1152]{1,0:T(8,128)S(1)}, f32[16,1152]{1,0:T(8,128)S(1)}, u32[]{:S(2)}, u32[]{:S(2)}) %collective-permute-start.13) | collective-permute-done | bytes 73760 | tf_op jit(solution)/shard_map/ppermute | solution.py:10
  508.7 14.5 %collective-permute-done.14 = f32[16,1152]{1,0:T(8,128)S(1)} collective-permute-done((f32[16,1152]{1,0:T(8,128)S(1)}, f32[16,1152]{1,0:T(8,128)S(1)}, u32[]{:S(2)}, u32[]{:S(2)}) %collective-permute-start.14) | collective-permute-done | bytes 73760 | tf_op jit(solution)/shard_map/ppermute | solution.py:10
  (72 shorter events, 46.3 us)
Async XLA Ops:
  7.2 129.7 %all-gather.2.cloned.1.call-start = ((), (), s32[]{:S(2)}) async-start(), calls=%async_computation.2 | async-start | bytes 2396160 | tf_op jit(solution)/shard_map/all_gather | solution.py:29
  11.4 18.6 %collective-permute-start = (bf16[16,1152]{1,0:T(8,128)(2,1)S(1)}, bf16[16,1152]{1,0:T(8,128)(2,1)S(1)}, u32[]{:S(2)}, u32[]{:S(2)}) collective-permute-start(bf16[16,1152]{1,0:T(8,128)(2,1)S(1)} %get-tuple-element.4), channel_id=1, source_target_pairs={{0,64},{64,128},{128,192},{192,256},{256,320},{320,384},{384,448},... | collective-permute-start | bytes 110600 | tf_op jit(solution)/shard_map/ppermute | solution.py:10
  29.9 16.7 %collective-permute-start.1 = (bf16[16,1152]{1,0:T(8,128)(2,1)S(1)}, bf16[16,1152]{1,0:T(8,128)(2,1)S(1)}, u32[]{:S(2)}, u32[]{:S(2)}) collective-permute-start(bf16[16,1152]{1,0:T(8,128)(2,1)S(1)} %collective-permute-done), channel_id=1, source_target_pairs={{0,64},{64,128},{128,192},{192,256},{256,320},{320,384},{384,448},... | collective-permute-start | bytes 110600 | tf_op jit(solution)/shard_map/ppermute | solution.py:10
  46.6 17.3 %collective-permute-start.2 = (bf16[16,1152]{1,0:T(8,128)(2,1)S(1)}, bf16[16,1152]{1,0:T(8,128)(2,1)S(1)}, u32[]{:S(2)}, u32[]{:S(2)}) collective-permute-start(bf16[16,1152]{1,0:T(8,128)(2,1)S(1)} %collective-permute-done.1), channel_id=1, source_target_pairs={{0,64},{64,128},{128,192},{192,256},{256,320},{320,384},{384,448},... | collective-permute-start | bytes 110600 | tf_op jit(solution)/shard_map/ppermute | solution.py:10
  63.9 16.7 %collective-permute-start.3 = (bf16[16,1152]{1,0:T(8,128)(2,1)S(1)}, bf16[16,1152]{1,0:T(8,128)(2,1)S(1)}, u32[]{:S(2)}, u32[]{:S(2)}) collective-permute-start(bf16[16,1152]{1,0:T(8,128)(2,1)S(1)} %collective-permute-done.2), channel_id=1, source_target_pairs={{0,64},{64,128},{128,192},{192,256},{256,320},{320,384},{384,448},... | collective-permute-start | bytes 110600 | tf_op jit(solution)/shard_map/ppermute | solution.py:10
  80.6 16.9 %collective-permute-start.4 = (bf16[16,1152]{1,0:T(8,128)(2,1)S(1)}, bf16[16,1152]{1,0:T(8,128)(2,1)S(1)}, u32[]{:S(2)}, u32[]{:S(2)}) collective-permute-start(bf16[16,1152]{1,0:T(8,128)(2,1)S(1)} %collective-permute-done.3), channel_id=1, source_target_pairs={{0,64},{64,128},{128,192},{192,256},{256,320},{320,384},{384,448},... | collective-permute-start | bytes 110600 | tf_op jit(solution)/shard_map/ppermute | solution.py:10
  97.5 16.8 %collective-permute-start.5 = (bf16[16,1152]{1,0:T(8,128)(2,1)S(1)}, bf16[16,1152]{1,0:T(8,128)(2,1)S(1)}, u32[]{:S(2)}, u32[]{:S(2)}) collective-permute-start(bf16[16,1152]{1,0:T(8,128)(2,1)S(1)} %collective-permute-done.4), channel_id=1, source_target_pairs={{0,64},{64,128},{128,192},{192,256},{256,320},{320,384},{384,448},... | collective-permute-start | bytes 110600 | tf_op jit(solution)/shard_map/ppermute | solution.py:10
  114.3 16.7 %collective-permute-start.6 = (bf16[16,1152]{1,0:T(8,128)(2,1)S(1)}, bf16[16,1152]{1,0:T(8,128)(2,1)S(1)}, u32[]{:S(2)}, u32[]{:S(2)}) collective-permute-start(bf16[16,1152]{1,0:T(8,128)(2,1)S(1)} %collective-permute-done.5), channel_id=1, source_target_pairs={{0,64},{64,128},{128,192},{192,256},{256,320},{320,384},{384,448},... | collective-permute-start | bytes 110600 | tf_op jit(solution)/shard_map/ppermute | solution.py:10
  136.9 2.6 copy-start
  145.5 19.1 %all-to-all-start = ((f32[64,1,16]{2,1,0:T(1,128)}), f32[64,1,16]{2,1,0:T(1,128)S(1)}, u32[]{:S(2)}, u32[]{:S(2)}) async-start(f32[64,1,16]{2,1,0:T(1,128)} %bitcast), calls=%async_computation | async-start | bytes 65536 | tf_op jit(solution)/shard_map/all_to_all | solution.py:71
  164.6 359.6 %all-to-all-start.1 = ((f32[64,16,1152]{2,1,0:T(8,128)}), f32[64,16,1152]{2,1,0:T(8,128)}, u32[]{:S(2)}, u32[]{:S(2)}) async-start(f32[64,16,1152]{2,1,0:T(8,128)} %bitcast.28), calls=%async_computation.1 | async-start | bytes 9437184 | tf_op jit(solution)/shard_map/all_to_all | solution.py:68
  172.7 229.6 %collective-permute-start.7 = (f32[16,1152]{1,0:T(8,128)S(1)}, f32[16,1152]{1,0:T(8,128)S(1)}, u32[]{:S(2)}, u32[]{:S(2)}) collective-permute-start(f32[16,1152]{1,0:T(8,128)S(1)} %fusion.26), channel_id=1, source_target_pairs={{0,64},{64,128},{128,192},{192,256},{256,320},{320,384},{384,448},... | collective-permute-start | bytes 221192 | tf_op jit(solution)/shard_map/ppermute | solution.py:10
  402.7 17.1 %collective-permute-start.8 = (f32[16,1152]{1,0:T(8,128)S(1)}, f32[16,1152]{1,0:T(8,128)S(1)}, u32[]{:S(2)}, u32[]{:S(2)}) collective-permute-start(f32[16,1152]{1,0:T(8,128)S(1)} %convolution_add_fusion), channel_id=1, source_target_pairs={{0,64},{64,128},{128,192},{192,256},{256,320},{320,384},{384,448},... | collective-permute-start | bytes 221192 | tf_op jit(solution)/shard_map/ppermute | solution.py:10
  419.8 17.9 %collective-permute-start.9 = (f32[16,1152]{1,0:T(8,128)S(1)}, f32[16,1152]{1,0:T(8,128)S(1)}, u32[]{:S(2)}, u32[]{:S(2)}) collective-permute-start(f32[16,1152]{1,0:T(8,128)S(1)} %add.259), channel_id=1, source_target_pairs={{0,64},{64,128},{128,192},{192,256},{256,320},{320,384},{384,448},... | collective-permute-start | bytes 221192 | tf_op jit(solution)/shard_map/ppermute | solution.py:10
  437.7 17.2 %collective-permute-start.10 = (f32[16,1152]{1,0:T(8,128)S(1)}, f32[16,1152]{1,0:T(8,128)S(1)}, u32[]{:S(2)}, u32[]{:S(2)}) collective-permute-start(f32[16,1152]{1,0:T(8,128)S(1)} %add.260), channel_id=1, source_target_pairs={{0,64},{64,128},{128,192},{192,256},{256,320},{320,384},{384,448},... | collective-permute-start | bytes 221192 | tf_op jit(solution)/shard_map/ppermute | solution.py:10
  454.9 17.1 %collective-permute-start.11 = (f32[16,1152]{1,0:T(8,128)S(1)}, f32[16,1152]{1,0:T(8,128)S(1)}, u32[]{:S(2)}, u32[]{:S(2)}) collective-permute-start(f32[16,1152]{1,0:T(8,128)S(1)} %add.261), channel_id=1, source_target_pairs={{0,64},{64,128},{128,192},{192,256},{256,320},{320,384},{384,448},... | collective-permute-start | bytes 221192 | tf_op jit(solution)/shard_map/ppermute | solution.py:10
  472.0 51.3 %copy-start.1 = (bf16[16,1152]{1,0:T(8,128)(2,1)S(1)}, bf16[16,1152]{1,0:T(8,128)(2,1)}, u32[]{:S(2)}) copy-start(bf16[16,1152]{1,0:T(8,128)(2,1)} %param.5) | copy-start | bytes 110596
  472.0 17.1 %collective-permute-start.12 = (f32[16,1152]{1,0:T(8,128)S(1)}, f32[16,1152]{1,0:T(8,128)S(1)}, u32[]{:S(2)}, u32[]{:S(2)}) collective-permute-start(f32[16,1152]{1,0:T(8,128)S(1)} %add.262), channel_id=1, source_target_pairs={{0,64},{64,128},{128,192},{192,256},{256,320},{320,384},{384,448},... | collective-permute-start | bytes 221192 | tf_op jit(solution)/shard_map/ppermute | solution.py:10
  489.1 17.1 %collective-permute-start.13 = (f32[16,1152]{1,0:T(8,128)S(1)}, f32[16,1152]{1,0:T(8,128)S(1)}, u32[]{:S(2)}, u32[]{:S(2)}) collective-permute-start(f32[16,1152]{1,0:T(8,128)S(1)} %add.263), channel_id=1, source_target_pairs={{0,64},{64,128},{128,192},{192,256},{256,320},{320,384},{384,448},... | collective-permute-start | bytes 221192 | tf_op jit(solution)/shard_map/ppermute | solution.py:10
  506.2 17.1 %collective-permute-start.14 = (f32[16,1152]{1,0:T(8,128)S(1)}, f32[16,1152]{1,0:T(8,128)S(1)}, u32[]{:S(2)}, u32[]{:S(2)}) collective-permute-start(f32[16,1152]{1,0:T(8,128)S(1)} %add.264), channel_id=1, source_target_pairs={{0,64},{64,128},{128,192},{192,256},{256,320},{320,384},{384,448},... | collective-permute-start | bytes 221192 | tf_op jit(solution)/shard_map/ppermute | solution.py:10
  524.2 2.6 copy-start.2
Sparse Core Ops, SparseCore 0:
  10.7 126.1 all-gather.1
where the time goes:
time: 536 us; the launch traced here: 535 us
  waiting for transfers between devices  410 us (76%)
  starting transfers between devices  84.1 us (16%)
  between operations  15.7 us (3%)
  matrix products  14.1 us (3%)
  other arithmetic  9.51 us (2%)
    ppermute x15, waiting for transfers between devices, passed_along(): return lax.ppermute(value, axis, pairs)  398 us
    ppermute x15, starting transfers between devices, passed_along(): return lax.ppermute(value, axis, pairs)  67.7 us
  transfers between devices with their start and end apart: 18, of which 17 were waited for; matrix products, arithmetic and copies ran while one was open for 2% of the time, Pallas kernels for 0%

commit v1 on v0

v1 whole, which is shorter than its diff:
```python
import jax
import jax.numpy as jnp
from jax import lax
from jax.sharding import PartitionSpec as P


def unit_rows(values):
    floats = values.astype(jnp.float32)
    norms = jnp.sqrt(jnp.sum(floats * floats, 1, keepdims=True) + 1e-06)
    return (floats / norms, norms)


def back_rows(grads, units, norms):
    return (grads - units * jnp.sum(units * grads, 1, keepdims=True)) / norms


def local(images, texts, scale, shift):
    rows = images.shape[0]
    image_unit, image_norm = unit_rows(images)
    text_unit, text_norm = unit_rows(texts)
    image_emb = image_unit.astype(jnp.bfloat16)
    text_emb = text_unit.astype(jnp.bfloat16)
    groups = lax.axis_size("grp")
    loops = lax.axis_size("blk")
    total = loops * groups * rows
    gathered = lax.all_gather(image_emb, "grp", axis=0, tiled=True)
    seen = lax.all_gather(text_emb, "blk", axis=0, tiled=True)
    place = lax.axis_index("grp")
    here = lax.axis_index("blk")
    image_ids = jnp.arange(groups * rows, dtype=jnp.int32)[:, None]
    column_ids = place * rows + (jnp.arange(loops * rows, dtype=jnp.int32) % rows)[None, :]
    column_blk = (jnp.arange(loops * rows, dtype=jnp.int32) // rows)[None, :]
    label = ((image_ids == column_ids) & (column_blk == here)).astype(jnp.float32)
    logit = (
        scale
        * lax.dot_general(gathered, seen, (((1,), (1,)), ((), ())), preferred_element_type=jnp.float32)
        + shift
    )
    loss = jnp.sum(jax.nn.softplus(logit * (1.0 - 2.0 * label)), 1) / total
    coef = ((jax.nn.sigmoid(logit) - label) * scale).astype(jnp.bfloat16)
    image_part = jnp.dot(coef, seen, preferred_element_type=jnp.float32)
    text_part = lax.dot_general(coef, gathered, (((0,), (0,)), ((), ())), preferred_element_type=jnp.float32)
    image_sum = lax.psum_scatter(image_part, "grp", scatter_dimension=0, tiled=True)
    image_loss = lax.psum_scatter(loss, "grp", scatter_dimension=0, tiled=True)
    text_sum = lax.psum_scatter(text_part, "blk", scatter_dimension=0, tiled=True)
    image_grad = back_rows(image_sum, image_unit, image_norm)
    text_grad = back_rows(text_sum, text_unit, text_norm)
    return (image_loss, image_grad, text_grad)


def solution(mesh):
    in_specs = (P(("blk", "grp"), None), P(("blk", "grp"), None), P(), P())
    out_specs = (P(("blk", "grp")), P(("blk", "grp"), None), P(("blk", "grp"), None))
    return jax.shard_map(local, mesh=mesh, in_specs=in_specs, out_specs=out_specs, check_vma=False)
```

time: 536 us -> 707 us (1.32)
  the two profiles are of different devices: /device:TPU:64 before, /device:TPU:4 now
where the time goes in v1:
time: 707 us; the launch traced here: 706 us
  waiting for transfers between devices  385 us (54%)
  blocking collectives  286 us (40%)
  between operations  15.7 us (2%)
  other arithmetic  9.52 us (1%)
  matrix products  7.54 us (1%)
    reduce_scatter x1, waiting for transfers between devices, local(): lax.psum_scatter(image_part, 'grp', scatter_dimension=0, tiled=True)  326 us
    unnamed x1, blocking collectives  216 us
    all_gather x1, blocking collectives, local(): seen = lax.all_gather(text_emb, 'blk', axis=0, tiled=True)  70.1 us
    all_gather x1, waiting for transfers between devices, local(): gathered = lax.all_gather(image_emb, 'grp', axis=0, tiled=True)  59.4 us
  transfers between devices with their start and end apart: 3, of which 2 were waited for; matrix products, arithmetic and copies ran while one was open for 1% of the time, Pallas kernels for 0%

profile of v1, /device:TPU:4, one launch (start us, length us, event | category | flops | bytes accessed | tf_op | source)
XLA Modules:
  0.0 706.1 jit_solution(12393039619672209299)
XLA Ops:
  7.2 0.0 all-gather.2.cloned.1.call-start
  7.2 0.9 fusion.3
  8.1 1.5 fusion.7
  9.6 0.0 all-gather.2.cloned.1.call-update
  9.6 0.0 reduce-scatter.5.cloned.1.call-start
  11.0 0.9 fusion.4
  11.9 0.9 fusion.8
  12.7 70.1 %all_gather.7 = bf16[128,1152]{1,0:T(8,128)(2,1)S(1)} all-gather(bf16[16,1152]{1,0:T(8,128)(2,1)S(1)} %fusion.8), channel_id=1, replica_groups=mesh['blk'=8,'grp'=64] {'blk'}, dimensions={0}, use_global_device_ids=true | all-gather | bytes 331776 | tf_op jit(solution)/shard_map/all_gather | solution.py:27
  82.8 59.4 %all-gather.2.cloned.1.call-done = bf16[1024,1152]{1,0:T(8,128)(2,1)} async-done(((bf16[16,1152]{1,0:T(8,128)(2,1)}), bf16[1024,1152]{1,0:T(8,128)(2,1)}) %all-gather.2.cloned.1.call-update) | async-done | bytes 2359312 | tf_op jit(solution)/shard_map/all_gather | solution.py:26
  142.2 3.0 fusion.1
  145.2 0.0 copy-done.2
  145.2 1.5 fusion.9
  146.7 0.0 reduce-scatter.5.cloned.1.call-update
  146.7 0.0 reduce-scatter.3.cloned.1.call-start
  146.8 3.1 fusion.10
  149.9 0.0 reduce-scatter.3.cloned.1.call-update
  149.9 1.3 dynamic-slice
  151.8 216.2 %all-reduce = f32[1024]{0:T(1024)S(1)} all-reduce(f32[1024]{0:T(1024)S(1)} %broadcast_multiply_fusion), channel_id=2, replica_groups=mesh['blk'=8,'grp'=64] {'grp'}, use_global_device_ids=true, to_apply=%region_3.4.clone | all-reduce | flops 1024 | bytes 8192
  368.0 0.6 dynamic-slice.1
  368.6 1.1 multiply_reduce_fusion
  369.6 1.6 subtract_divide_fusion
  371.2 325.6 %reduce-scatter.3.cloned.1.call-done = f32[16,1152]{1,0:T(8,128)} async-done(((f32[1024,1152]{1,0:T(8,128)}), f32[16,1152]{1,0:T(8,128)}) %reduce-scatter.3.cloned.1.call-update) | async-done | bytes 73744 | tf_op jit(solution)/shard_map/reduce_scatter | solution.py:43
  696.9 1.1 multiply_reduce_fusion.1
  698.0 1.6 subtract_divide_fusion.1
  (11 shorter events, 0.0 us)
Async XLA Ops:
  7.2 135.1 %all-gather.2.cloned.1.call-start = ((), (), s32[]{:S(2)}) async-start(), calls=%async_computation.2 | async-start | bytes 2396160 | tf_op jit(solution)/shard_map/all_gather | solution.py:26
  9.6 359.0 %reduce-scatter.5.cloned.1.call-start = ((), (), s32[]{:S(2)}) async-start(), calls=%async_computation.4 | async-start | bytes 663552 | tf_op jit(solution)/shard_map/reduce_scatter | solution.py:45
  142.2 3.0 copy-start.2
  146.7 550.1 %reduce-scatter.3.cloned.1.call-start = ((), (), s32[]{:S(2)}) async-start(), calls=%async_computation.3 | async-start | bytes 4792320 | tf_op jit(solution)/shard_map/reduce_scatter | solution.py:43
  149.9 218.7 %copy-start = (bf16[16,1152]{1,0:T(8,128)(2,1)S(1)}, bf16[16,1152]{1,0:T(8,128)(2,1)}, u32[]{:S(2)}) copy-start(bf16[16,1152]{1,0:T(8,128)(2,1)} %param.5) | copy-start | bytes 110596
  149.9 547.0 %copy-start.1 = (bf16[16,1152]{1,0:T(8,128)(2,1)S(1)}, bf16[16,1152]{1,0:T(8,128)(2,1)}, u32[]{:S(2)}) copy-start(bf16[16,1152]{1,0:T(8,128)(2,1)} %param.4) | copy-start | bytes 110596
Sparse Core Ops, SparseCore 0:
  10.7 131.4 all-gather.1
  146.9 109.8 reduce-scatter.4
  259.6 437.2 reduce-scatter.2

commit v2 on v1

--- a/solution.py
+++ b/solution.py
@@ -14,6 +14,16 @@
     return (grads - units * jnp.sum(units * grads, 1, keepdims=True)) / norms
 
 
+def spread(block, axis, count):
+    copies = jnp.tile(block, (count,) + (1,) * (block.ndim - 1))
+    return lax.all_to_all(copies, axis, 0, 0, tiled=True)
+
+
+def gather_sum(parts, axis, count):
+    received = lax.all_to_all(parts, axis, 0, 0, tiled=True)
+    return jnp.sum(received.reshape((count, -1) + parts.shape[1:]), 0)
+
+
 def local(images, texts, scale, shift):
     rows = images.shape[0]
     image_unit, image_norm = unit_rows(images)
@@ -23,8 +33,8 @@
     groups = lax.axis_size("grp")
     loops = lax.axis_size("blk")
     total = loops * groups * rows
-    gathered = lax.all_gather(image_emb, "grp", axis=0, tiled=True)
-    seen = lax.all_gather(text_emb, "blk", axis=0, tiled=True)
+    gathered = spread(image_emb, "grp", groups)
+    seen = spread(text_emb, "blk", loops)
     place = lax.axis_index("grp")
     here = lax.axis_index("blk")
     image_ids = jnp.arange(groups * rows, dtype=jnp.int32)[:, None]
@@ -40,9 +50,9 @@
     coef = ((jax.nn.sigmoid(logit) - label) * scale).astype(jnp.bfloat16)
     image_part = jnp.dot(coef, seen, preferred_element_type=jnp.float32)
     text_part = lax.dot_general(coef, gathered, (((0,), (0,)), ((), ())), preferred_element_type=jnp.float32)
-    image_sum = lax.psum_scatter(image_part, "grp", scatter_dimension=0, tiled=True)
-    image_loss = lax.psum_scatter(loss, "grp", scatter_dimension=0, tiled=True)
-    text_sum = lax.psum_scatter(text_part, "blk", scatter_dimension=0, tiled=True)
+    image_sum = gather_sum(image_part, "grp", groups)
+    image_loss = gather_sum(loss, "grp", groups)
+    text_sum = gather_sum(text_part, "blk", loops)
     image_grad = back_rows(image_sum, image_unit, image_norm)
     text_grad = back_rows(text_sum, text_unit, text_norm)
     return (image_loss, image_grad, text_grad)

time: 707 us -> 446 us (0.63)
  the two profiles are of different devices: /device:TPU:4 before, /device:TPU:24 now
where the time goes in v2:
time: 446 us; the launch traced here: 440 us
  waiting for transfers between devices  358 us (80%)
  starting transfers between devices  62 us (14%)
  other arithmetic  8.83 us (2%)
  matrix products  5.57 us (1%)
    all_to_all x3, waiting for transfers between devices, gather_sum(): received = lax.all_to_all(parts, axis, 0, 0, tiled=True)  239 us
    all_to_all x2, waiting for transfers between devices, spread(): return lax.all_to_all(copies, axis, 0, 0, tiled=True)  119 us
    all_to_all x2, starting transfers between devices, spread(): return lax.all_to_all(copies, axis, 0, 0, tiled=True)  34.7 us
    all_to_all x3, starting transfers between devices, gather_sum(): received = lax.all_to_all(parts, axis, 0, 0, tiled=True)  27.3 us
  transfers between devices with their start and end apart: 5, of which 5 were waited for; matrix products, arithmetic and copies ran while one was open for 2% of the time, Pallas kernels for 0%

profile of v2, /device:TPU:24, one launch (start us, length us, event | category | flops | bytes accessed | tf_op | source)
XLA Modules:
  0.0 439.7 jit_solution(18109259993610458904)
XLA Ops:
  0.6 0.9 fusion.7
  1.5 0.9 fusion.11
  2.4 0.7 tile.5
  3.1 17.6 %all-to-all-start.1 = ((bf16[8,16,1152]{2,1,0:T(8,128)(2,1)}), bf16[8,16,1152]{2,1,0:T(8,128)(2,1)S(1)}, u32[]{:S(2)}, u32[]{:S(2)}) async-start(bf16[8,16,1152]{2,1,0:T(8,128)(2,1)} %tile.5), calls=%async_computation.1 | async-start | bytes 589824 | tf_op jit(solution)/shard_map/all_to_all | solution.py:19
  20.7 0.9 fusion.6
  21.6 0.9 fusion.10
  22.4 15.1 %all-to-all-done.1 = bf16[8,16,1152]{2,1,0:T(8,128)(2,1)S(1)} async-done(((bf16[8,16,1152]{2,1,0:T(8,128)(2,1)}), bf16[8,16,1152]{2,1,0:T(8,128)(2,1)S(1)}, u32[]{:S(2)}, u32[]{:S(2)}) %all-to-all-start.1) | async-done | bytes 294944 | tf_op jit(solution)/shard_map/all_to_all | solution.py:19
  37.5 1.6 tile.4
  39.1 17.1 %all-to-all-start = ((bf16[64,16,1152]{2,1,0:T(8,128)(2,1)}), bf16[64,16,1152]{2,1,0:T(8,128)(2,1)S(1)}, u32[]{:S(2)}, u32[]{:S(2)}) async-start(bf16[64,16,1152]{2,1,0:T(8,128)(2,1)} %tile.4), calls=%async_computation | async-start | bytes 4718592 | tf_op jit(solution)/shard_map/all_to_all | solution.py:19
  57.6 104.2 %all-to-all-done = bf16[64,16,1152]{2,1,0:T(8,128)(2,1)S(1)} async-done(((bf16[64,16,1152]{2,1,0:T(8,128)(2,1)}), bf16[64,16,1152]{2,1,0:T(8,128)(2,1)S(1)}, u32[]{:S(2)}, u32[]{:S(2)}) %all-to-all-start) | async-done | bytes 2359328 | tf_op jit(solution)/shard_map/all_to_all | solution.py:19
  161.7 1.3 multiply_convert_fusion
  163.1 0.7 div.58
  163.8 10.2 %all-to-all-start.2 = ((f32[64,16,1]{1,2,0:T(1,128)}), f32[64,16,1]{1,2,0:T(1,128)S(1)}, u32[]{:S(2)}, u32[]{:S(2)}) async-start(f32[64,16,1]{1,2,0:T(1,128)} %bitcast.2), calls=%async_computation.2 | async-start | bytes 65536 | tf_op jit(solution)/shard_map/all_to_all | solution.py:23
  174.2 1.4 fusion.13
  175.6 8.8 %all-to-all-done.2 = f32[64,16,1]{1,2,0:T(1,128)S(1)} async-done(((f32[64,16,1]{1,2,0:T(1,128)}), f32[64,16,1]{1,2,0:T(1,128)S(1)}, u32[]{:S(2)}, u32[]{:S(2)}) %all-to-all-start.2) | async-done | bytes 4128 | tf_op jit(solution)/shard_map/all_to_all | solution.py:23
  184.4 3.5 all-to-all-start.4
  188.1 2.9 fusion.12
  191.0 27.4 %all-to-all-done.4 = f32[8,16,1152]{2,1,0:T(8,128)S(1)} async-done(((f32[8,16,1152]{2,1,0:T(8,128)}), f32[8,16,1152]{2,1,0:T(8,128)S(1)}, u32[]{:S(2)}, u32[]{:S(2)}) %all-to-all-start.4) | async-done | bytes 589856 | tf_op jit(solution)/shard_map/all_to_all | solution.py:23
  218.4 13.6 %all-to-all-start.3 = ((f32[64,16,1152]{2,1,0:T(8,128)}), f32[64,16,1152]{2,1,0:T(8,128)}, u32[]{:S(2)}, u32[]{:S(2)}) async-start(f32[64,16,1152]{2,1,0:T(8,128)} %fusion.12), calls=%async_computation.3 | async-start | bytes 9437184 | tf_op jit(solution)/shard_map/all_to_all | solution.py:23
  232.0 0.6 reduce_sum.75
  232.8 0.7 subtract_divide_fusion
  233.5 202.7 %all-to-all-done.3 = f32[64,16,1152]{2,1,0:T(8,128)} async-done(((f32[64,16,1152]{2,1,0:T(8,128)}), f32[64,16,1152]{2,1,0:T(8,128)}, u32[]{:S(2)}, u32[]{:S(2)}) %all-to-all-start.3) | async-done | bytes 4718624 | tf_op jit(solution)/shard_map/all_to_all | solution.py:23
  436.2 2.6 reduce_sum.76
  439.0 0.7 subtract_divide_fusion.1
  (14 shorter events, 0.9 us)
Async XLA Ops:
  3.1 34.4 %all-to-all-start.1 = ((bf16[8,16,1152]{2,1,0:T(8,128)(2,1)}), bf16[8,16,1152]{2,1,0:T(8,128)(2,1)S(1)}, u32[]{:S(2)}, u32[]{:S(2)}) async-start(bf16[8,16,1152]{2,1,0:T(8,128)(2,1)} %tile.5), calls=%async_computation.1 | async-start | bytes 589824 | tf_op jit(solution)/shard_map/all_to_all | solution.py:19
  39.1 122.6 %all-to-all-start = ((bf16[64,16,1152]{2,1,0:T(8,128)(2,1)}), bf16[64,16,1152]{2,1,0:T(8,128)(2,1)S(1)}, u32[]{:S(2)}, u32[]{:S(2)}) async-start(bf16[64,16,1152]{2,1,0:T(8,128)(2,1)} %tile.4), calls=%async_computation | async-start | bytes 4718592 | tf_op jit(solution)/shard_map/all_to_all | solution.py:19
  163.8 20.6 %all-to-all-start.2 = ((f32[64,16,1]{1,2,0:T(1,128)}), f32[64,16,1]{1,2,0:T(1,128)S(1)}, u32[]{:S(2)}, u32[]{:S(2)}) async-start(f32[64,16,1]{1,2,0:T(1,128)} %bitcast.2), calls=%async_computation.2 | async-start | bytes 65536 | tf_op jit(solution)/shard_map/all_to_all | solution.py:23
  184.4 34.0 %all-to-all-start.4 = ((f32[8,16,1152]{2,1,0:T(8,128)}), f32[8,16,1152]{2,1,0:T(8,128)S(1)}, u32[]{:S(2)}, u32[]{:S(2)}) async-start(f32[8,16,1152]{2,1,0:T(8,128)} %fusion.13), calls=%async_computation.4 | async-start | bytes 1179648 | tf_op jit(solution)/shard_map/all_to_all | solution.py:23
  191.0 41.6 %copy-start = (bf16[16,1152]{1,0:T(8,128)(2,1)S(1)}, bf16[16,1152]{1,0:T(8,128)(2,1)}, u32[]{:S(2)}) copy-start(bf16[16,1152]{1,0:T(8,128)(2,1)} %param.5) | copy-start | bytes 110596
  218.4 217.9 %all-to-all-start.3 = ((f32[64,16,1152]{2,1,0:T(8,128)}), f32[64,16,1152]{2,1,0:T(8,128)}, u32[]{:S(2)}, u32[]{:S(2)}) async-start(f32[64,16,1152]{2,1,0:T(8,128)} %fusion.12), calls=%async_computation.3 | async-start | bytes 9437184 | tf_op jit(solution)/shard_map/all_to_all | solution.py:23
  233.5 205.3 %copy-start.1 = (bf16[16,1152]{1,0:T(8,128)(2,1)S(1)}, bf16[16,1152]{1,0:T(8,128)(2,1)}, u32[]{:S(2)}) copy-start(bf16[16,1152]{1,0:T(8,128)(2,1)} %param.4) | copy-start | bytes 110596

commit v3 on v1

v3 whole, which is shorter than its diff:
```python
import jax
import jax.numpy as jnp
from jax import lax
from jax.sharding import Mesh, PartitionSpec as P

ROWS_AXES = ("x", "zh", "y", "zl", "c")
IMAGE_AXES = ("x", "y", "c")
TEXT_AXES = ("zh", "zl")


def unit_rows(values):
    floats = values.astype(jnp.float32)
    norms = jnp.sqrt(jnp.sum(floats * floats, 1, keepdims=True) + 1e-06)
    return (floats / norms, norms)


def back_rows(grads, units, norms):
    return (grads - units * jnp.sum(units * grads, 1, keepdims=True)) / norms


def linear_index(axes):
    index = 0
    for name in axes:
        index = index * lax.axis_size(name) + lax.axis_index(name)
    return index


def group_size(axes):
    size = 1
    for name in axes:
        size *= lax.axis_size(name)
    return size


def spread(block, axes, count):
    copies = jnp.tile(block, (count,) + (1,) * (block.ndim - 1))
    return lax.all_to_all(copies, axes, 0, 0, tiled=True)


def gather_sum(parts, axes, count):
    received = lax.all_to_all(parts, axes, 0, 0, tiled=True)
    return jnp.sum(received.reshape((count, -1) + parts.shape[1:]), 0)


def local(images, texts, scale, shift):
    rows = images.shape[0]
    image_unit, image_norm = unit_rows(images)
    text_unit, text_norm = unit_rows(texts)
    image_emb = image_unit.astype(jnp.bfloat16)
    text_emb = text_unit.astype(jnp.bfloat16)
    image_count = group_size(IMAGE_AXES)
    text_count = group_size(TEXT_AXES)
    total = image_count * text_count * rows
    gathered = spread(image_emb, IMAGE_AXES, image_count)
    seen = spread(text_emb, TEXT_AXES, text_count)
    image_ids = jnp.arange(image_count * rows, dtype=jnp.int32)[:, None]
    text_ids = jnp.arange(text_count * rows, dtype=jnp.int32)[None, :]
    mine_i = linear_index(IMAGE_AXES)
    mine_t = linear_index(TEXT_AXES)
    label = (
        (image_ids // rows == mine_i) & (text_ids // rows == mine_t) & (image_ids % rows == text_ids % rows)
    ).astype(jnp.float32)
    logit = (
        scale
        * lax.dot_general(gathered, seen, (((1,), (1,)), ((), ())), preferred_element_type=jnp.float32)
        + shift
    )
    loss = jnp.sum(jax.nn.softplus(logit * (1.0 - 2.0 * label)), 1) / total
    coef = ((jax.nn.sigmoid(logit) - label) * scale).astype(jnp.bfloat16)
    image_part = jnp.dot(coef, seen, preferred_element_type=jnp.float32)
    text_part = lax.dot_general(coef, gathered, (((0,), (0,)), ((), ())), preferred_element_type=jnp.float32)
    image_sum = gather_sum(image_part, IMAGE_AXES, image_count)
    image_loss = gather_sum(loss, IMAGE_AXES, image_count)
    text_sum = gather_sum(text_part, TEXT_AXES, text_count)
    image_grad = back_rows(image_sum, image_unit, image_norm)
    text_grad = back_rows(text_sum, text_unit, text_norm)
    return (image_loss, image_grad, text_grad)


def solution(mesh):
    blk, grp = mesh.devices.shape
    fine = Mesh(mesh.devices.reshape(blk // 2, 2, grp // 16, 8, 2), ROWS_AXES)
    in_specs = (P(ROWS_AXES, None), P(ROWS_AXES, None), P(), P())
    out_specs = (P(ROWS_AXES), P(ROWS_AXES, None), P(ROWS_AXES, None))
    return jax.shard_map(local, mesh=fine, in_specs=in_specs, out_specs=out_specs, check_vma=False)
```

time: 707 us -> 190 us (0.27)
  the two profiles are of different devices: /device:TPU:4 before, /device:TPU:24 now
where the time goes in v3:
time: 190 us; the launch traced here: 188 us
  waiting for transfers between devices  128 us (67%)
  starting transfers between devices  41.2 us (22%)
  other arithmetic  8.31 us (4%)
  matrix products  5.29 us (3%)
  local copies, waits for them, and re-layouts  3.29 us (2%)
  between operations  2.11 us (1%)
    all_to_all x3, waiting for transfers between devices, gather_sum(): received = lax.all_to_all(parts, axes, 0, 0, tiled=True)  81.6 us
    all_to_all x2, waiting for transfers between devices, spread(): return lax.all_to_all(copies, axes, 0, 0, tiled=True)  45.9 us
    all_to_all x2, starting transfers between devices, spread(): return lax.all_to_all(copies, axes, 0, 0, tiled=True)  22.6 us
    all_to_all x3, starting transfers between devices, gather_sum(): received = lax.all_to_all(parts, axes, 0, 0, tiled=True)  18.7 us
  transfers between devices with their start and end apart: 5, of which 5 were waited for; matrix products, arithmetic and copies ran while one was open for 5% of the time, Pallas kernels for 0%

profile of v3, /device:TPU:24, one launch (start us, length us, event | category | flops | bytes accessed | tf_op | source)
XLA Modules:
  0.0 187.7 jit_solution(6507789146432697808)
XLA Ops:
  0.6 0.9 fusion.4
  1.5 0.8 fusion.17
  2.4 1.1 tile.4
  3.5 9.4 %all-to-all-start = ((bf16[32,16,1152]{2,1,0:T(8,128)(2,1)}), bf16[32,16,1152]{2,1,0:T(8,128)(2,1)S(1)}, u32[]{:S(2)}, u32[]{:S(2)}) async-start(bf16[32,16,1152]{2,1,0:T(8,128)(2,1)} %tile.4), calls=%async_computation | async-start | bytes 2359296 | tf_op jit(solution)/shard_map/all_to_all | solution.py:37
  13.6 16.1 %all-to-all-done = bf16[32,16,1152]{2,1,0:T(8,128)(2,1)S(1)} async-done(((bf16[32,16,1152]{2,1,0:T(8,128)(2,1)}), bf16[32,16,1152]{2,1,0:T(8,128)(2,1)S(1)}, u32[]{:S(2)}, u32[]{:S(2)}) %all-to-all-start) | async-done | bytes 1179680 | tf_op jit(solution)/shard_map/all_to_all | solution.py:37
  29.7 0.8 tile.5
  30.5 13.2 %all-to-all-start.1 = ((bf16[16,16,1152]{2,1,0:T(8,128)(2,1)}), bf16[16,16,1152]{2,1,0:T(8,128)(2,1)S(1)}, u32[]{:S(2)}, u32[]{:S(2)}) async-start(bf16[16,16,1152]{2,1,0:T(8,128)(2,1)} %tile.5), calls=%async_computation.1 | async-start | bytes 1179648 | tf_op jit(solution)/shard_map/all_to_all | solution.py:37
  45.1 29.8 %all-to-all-done.1 = bf16[16,16,1152]{2,1,0:T(8,128)(2,1)S(1)} async-done(((bf16[16,16,1152]{2,1,0:T(8,128)(2,1)}), bf16[16,16,1152]{2,1,0:T(8,128)(2,1)S(1)}, u32[]{:S(2)}, u32[]{:S(2)}) %all-to-all-start.1) | async-done | bytes 589856 | tf_op jit(solution)/shard_map/all_to_all | solution.py:37
  75.0 1.8 multiply_convert_fusion
  77.0 0.7 div.68
  77.7 6.4 %all-to-all-start.2 = ((f32[32,16,1]{1,2,0:T(1,128)}), f32[32,16,1]{1,2,0:T(1,128)S(1)}, u32[]{:S(2)}, u32[]{:S(2)}) async-start(f32[32,16,1]{1,2,0:T(1,128)} %bitcast.2), calls=%async_computation.2 | async-start | bytes 32768 | tf_op jit(solution)/shard_map/all_to_all | solution.py:41
  84.1 1.9 %fusion.19 = f32[32,16,1152]{2,1,0:T(8,128)} fusion(bf16[32,16,256]{2,1,0:T(8,128)(2,1)S(1)} %bitcast.25, bf16[256,1152,1]{1,0,2:T(8,128)(2,1)S(1)} %bitcast.24), kind=kOutput, calls=%fused_computation.45 | convolution fusion | flops 301989888 | bytes 3211264 | tf_op jit(solution)/shard_map/dot_general | solution.py:70
  86.0 3.5 %all-to-all-done.2 = f32[32,16,1]{1,2,0:T(1,128)S(1)} async-done(((f32[32,16,1]{1,2,0:T(1,128)}), f32[32,16,1]{1,2,0:T(1,128)S(1)}, u32[]{:S(2)}, u32[]{:S(2)}) %all-to-all-start.2) | async-done | bytes 2080 | tf_op jit(solution)/shard_map/all_to_all | solution.py:41
  89.5 5.8 %all-to-all-start.3 = ((f32[32,16,1152]{2,1,0:T(8,128)}), f32[32,16,1152]{2,1,0:T(8,128)S(1)}, u32[]{:S(2)}, u32[]{:S(2)}) async-start(f32[32,16,1152]{2,1,0:T(8,128)} %fusion.19), calls=%async_computation.3 | async-start | bytes 4718592 | tf_op jit(solution)/shard_map/all_to_all | solution.py:41
  95.3 1.3 fusion.3
  96.7 1.5 fusion.20
  98.2 26.7 %all-to-all-done.3 = f32[32,16,1152]{2,1,0:T(8,128)S(1)} async-done(((f32[32,16,1152]{2,1,0:T(8,128)}), f32[32,16,1152]{2,1,0:T(8,128)S(1)}, u32[]{:S(2)}, u32[]{:S(2)}) %all-to-all-start.3) | async-done | bytes 2359328 | tf_op jit(solution)/shard_map/all_to_all | solution.py:41
  124.9 6.4 %all-to-all-start.4 = ((f32[16,16,1152]{2,1,0:T(8,128)}), f32[16,16,1152]{2,1,0:T(8,128)S(1)}, u32[]{:S(2)}, u32[]{:S(2)}) async-start(f32[16,16,1152]{2,1,0:T(8,128)} %fusion.20), calls=%async_computation.4 | async-start | bytes 2359296 | tf_op jit(solution)/shard_map/all_to_all | solution.py:41
  131.4 0.6 reduce_sum.75
  131.9 0.8 reduce_sum.76
  132.7 1.1 multiply_reduce_fusion.1
  133.8 1.6 subtract_divide_fusion.1
  135.4 51.4 %all-to-all-done.4 = f32[16,16,1152]{2,1,0:T(8,128)S(1)} async-done(((f32[16,16,1152]{2,1,0:T(8,128)}), f32[16,16,1152]{2,1,0:T(8,128)S(1)}, u32[]{:S(2)}, u32[]{:S(2)}) %all-to-all-start.4) | async-done | bytes 1179680 | tf_op jit(solution)/shard_map/all_to_all | solution.py:41
  187.0 0.7 subtract_divide_fusion
  (32 shorter events, 1.2 us)
Async XLA Ops:
  1.5 2.0 %copy-start.5 = (f32[16]{0:T(128)}, f32[16]{0:T(128)S(1)}, u32[]{:S(2)}) copy-start(f32[16]{0:T(128)S(1)} %add_sqrt_fusion.1) | copy-start | bytes 196
  3.5 9.4 %copy-start = (bf16[16,1152]{1,0:T(8,128)(2,1)S(1)}, bf16[16,1152]{1,0:T(8,128)(2,1)}, u32[]{:S(2)}) copy-start(bf16[16,1152]{1,0:T(8,128)(2,1)} %param.5) | copy-start | bytes 110596
  3.5 26.2 %all-to-all-start = ((bf16[32,16,1152]{2,1,0:T(8,128)(2,1)}), bf16[32,16,1152]{2,1,0:T(8,128)(2,1)S(1)}, u32[]{:S(2)}, u32[]{:S(2)}) async-start(bf16[32,16,1152]{2,1,0:T(8,128)(2,1)} %tile.4), calls=%async_computation | async-start | bytes 2359296 | tf_op jit(solution)/shard_map/all_to_all | solution.py:37
  13.0 0.5 copy-start.3
  30.5 44.5 %all-to-all-start.1 = ((bf16[16,16,1152]{2,1,0:T(8,128)(2,1)}), bf16[16,16,1152]{2,1,0:T(8,128)(2,1)S(1)}, u32[]{:S(2)}, u32[]{:S(2)}) async-start(bf16[16,16,1152]{2,1,0:T(8,128)(2,1)} %tile.5), calls=%async_computation.1 | async-start | bytes 1179648 | tf_op jit(solution)/shard_map/all_to_all | solution.py:37
  45.0 31.8 %copy-start.8 = (pred[512]{0:T(512)(128)(4,1)}, pred[512]{0:T(512)(128)(4,1)S(1)}, u32[]{:S(2)}) copy-start(pred[512]{0:T(512)(128)(4,1)S(1)} %fusion.10) | copy-start | bytes 1540
  45.1 31.7 %copy-start.9 = (pred[256]{0:T(512)(128)(4,1)}, pred[256]{0:T(512)(128)(4,1)S(1)}, u32[]{:S(2)}) copy-start(pred[256]{0:T(512)(128)(4,1)S(1)} %fusion.16) | copy-start | bytes 772
  45.1 31.7 %copy-start.7 = (s32[256]{0:T(256)}, s32[256]{0:T(256)S(1)}, u32[]{:S(2)}) copy-start(s32[256]{0:T(256)S(1)} %and_select_fusion) | copy-start | bytes 3076
  45.1 31.7 %copy-start.2 = (s32[512]{0:T(512)}, s32[512]{0:T(512)S(1)}, u32[]{:S(2)}) copy-start(s32[512]{0:T(512)S(1)} %fusion.6) | copy-start | bytes 6148
  77.7 11.9 %all-to-all-start.2 = ((f32[32,16,1]{1,2,0:T(1,128)}), f32[32,16,1]{1,2,0:T(1,128)S(1)}, u32[]{:S(2)}, u32[]{:S(2)}) async-start(f32[32,16,1]{1,2,0:T(1,128)} %bitcast.2), calls=%async_computation.2 | async-start | bytes 32768 | tf_op jit(solution)/shard_map/all_to_all | solution.py:41
  89.5 35.4 %all-to-all-start.3 = ((f32[32,16,1152]{2,1,0:T(8,128)}), f32[32,16,1152]{2,1,0:T(8,128)S(1)}, u32[]{:S(2)}, u32[]{:S(2)}) async-start(f32[32,16,1152]{2,1,0:T(8,128)} %fusion.19), calls=%async_computation.3 | async-start | bytes 4718592 | tf_op jit(solution)/shard_map/all_to_all | solution.py:41
  124.9 61.8 %all-to-all-start.4 = ((f32[16,16,1152]{2,1,0:T(8,128)}), f32[16,16,1152]{2,1,0:T(8,128)S(1)}, u32[]{:S(2)}, u32[]{:S(2)}) async-start(f32[16,16,1152]{2,1,0:T(8,128)} %fusion.20), calls=%async_computation.4 | async-start | bytes 2359296 | tf_op jit(solution)/shard_map/all_to_all | solution.py:41
  131.9 0.8 copy-start.6
  132.7 54.1 %copy-start.1 = (bf16[16,1152]{1,0:T(8,128)(2,1)S(1)}, bf16[16,1152]{1,0:T(8,128)(2,1)}, u32[]{:S(2)}) copy-start(bf16[16,1152]{1,0:T(8,128)(2,1)} %param.5) | copy-start | bytes 110596
  132.7 54.1 %copy-start.4 = (f32[16]{0:T(128)S(1)}, f32[16]{0:T(128)}, u32[]{:S(2)}) copy-start(f32[16]{0:T(128)} %copy-done.3) | copy-start | bytes 196

commit v4 on v3

--- a/solution.py
+++ b/solution.py
@@ -1,11 +1,17 @@
+import functools
+
 import jax
 import jax.numpy as jnp
 from jax import lax
+from jax.experimental import pallas as pl
+from jax.experimental.pallas import tpu as pltpu
 from jax.sharding import Mesh, PartitionSpec as P
 
 ROWS_AXES = ("x", "zh", "y", "zl", "c")
 IMAGE_AXES = ("x", "y", "c")
 TEXT_AXES = ("zh", "zl")
+MESH_IDS = pl.DeviceIdType.MESH
+LOSS_LANES = 128
 
 
 def unit_rows(values):
@@ -32,18 +38,83 @@
     return size
 
 
-def spread(block, axes, count):
-    copies = jnp.tile(block, (count,) + (1,) * (block.ndim - 1))
-    return lax.all_to_all(copies, axes, 0, 0, tiled=True)
+def member(axes, k):
+    coords = {}
+    for name in reversed(axes):
+        size = lax.axis_size(name)
+        coords[name] = k % size
+        k = k // size
+    return tuple(coords[name] if name in coords else lax.axis_index(name) for name in ROWS_AXES)
 
 
-def gather_sum(parts, axes, count):
-    received = lax.all_to_all(parts, axes, 0, 0, tiled=True)
-    return jnp.sum(received.reshape((count, -1) + parts.shape[1:]), 0)
+def exchange_kernel(scatter, image_src, text_src, image_out, text_out, image_send, image_recv, text_send, text_recv):
+    groups = ((IMAGE_AXES, image_src, image_out, image_send, image_recv),
+              (TEXT_AXES, text_src, text_out, text_send, text_recv))
+    barrier = pltpu.get_barrier_semaphore()
+    peers = 0
+    for axes, src, out, send, recv in groups:
+        count, me = group_size(axes), linear_index(axes)
+        peers += count - 1
+
+        def greet(step, carry, axes=axes, count=count, me=me):
+            pl.semaphore_signal(barrier, 1, device_id=member(axes, (me + step) % count), device_id_type=MESH_IDS)
+            return carry
+
+        lax.fori_loop(1, count, greet, 0)
+    pl.semaphore_wait(barrier, peers)
+
+    for axes, src, out, send, recv in groups:
+        count, me = group_size(axes), linear_index(axes)
+        out[me] = src[me] if scatter else src[...]
+
+        def start(step, carry, axes=axes, count=count, me=me, src=src, out=out, send=send, recv=recv):
+            peer = (me + step) % count
+            pltpu.make_async_remote_copy(
+                src.at[peer] if scatter else src, out.at[me], send.at[peer], recv.at[me],
+                device_id=member(axes, peer), device_id_type=MESH_IDS,
+            ).start()
+            return carry
+
+        lax.fori_loop(1, count, start, 0)
+
+    for axes, src, out, send, recv in groups:
+        count, me = group_size(axes), linear_index(axes)
+
+        def finish(step, carry, axes=axes, count=count, me=me, src=src, out=out, send=send, recv=recv):
+            peer = (me + step) % count
+            copy = pltpu.make_async_remote_copy(
+                src.at[peer] if scatter else src, out.at[peer], send.at[peer], recv.at[peer],
+                device_id=member(axes, peer), device_id_type=MESH_IDS,
+            )
+            copy.wait_send()
+            copy.wait_recv()
+            return carry
+
+        lax.fori_loop(1, count, finish, 0)
+
+
+def exchange(image_src, text_src, scatter, tag):
+    image_count, text_count = group_size(IMAGE_AXES), group_size(TEXT_AXES)
+    image_shape = image_src.shape if scatter else (image_count,) + image_src.shape
+    text_shape = text_src.shape if scatter else (text_count,) + text_src.shape
+    vmem = pl.BlockSpec(memory_space=pltpu.VMEM)
+    return pl.pallas_call(
+        functools.partial(exchange_kernel, scatter),
+        out_shape=(jax.ShapeDtypeStruct(image_shape, image_src.dtype), jax.ShapeDtypeStruct(text_shape, text_src.dtype)),
+        in_specs=[vmem, vmem],
+        out_specs=(vmem, vmem),
+        scratch_shapes=[
+            pltpu.SemaphoreType.DMA((image_count,)),
+            pltpu.SemaphoreType.DMA((image_count,)),
+            pltpu.SemaphoreType.DMA((text_count,)),
+            pltpu.SemaphoreType.DMA((text_count,)),
+        ],
+        compiler_params=pltpu.CompilerParams(collective_id=tag, has_side_effects=True),
+    )(image_src, text_src)
 
 
 def local(images, texts, scale, shift):
-    rows = images.shape[0]
+    rows, width = images.shape
     image_unit, image_norm = unit_rows(images)
     text_unit, text_norm = unit_rows(texts)
     image_emb = image_unit.astype(jnp.bfloat16)
@@ -51,8 +122,9 @@
     image_count = group_size(IMAGE_AXES)
     text_count = group_size(TEXT_AXES)
     total = image_count * text_count * rows
-    gathered = spread(image_emb, IMAGE_AXES, image_count)
-    seen = spread(text_emb, TEXT_AXES, text_count)
+    gathered, seen = exchange(image_emb, text_emb, False, 0)
+    gathered = gathered.reshape(image_count * rows, width)
+    seen = seen.reshape(text_count * rows, width)
     image_ids = jnp.arange(image_count * rows, dtype=jnp.int32)[:, None]
     text_ids = jnp.arange(text_count * rows, dtype=jnp.int32)[None, :]
     mine_i = linear_index(IMAGE_AXES)
@@ -65,16 +137,19 @@
         * lax.dot_general(gathered, seen, (((1,), (1,)), ((), ())), preferred_element_type=jnp.float32)
         + shift
     )
-    loss = jnp.sum(jax.nn.softplus(logit * (1.0 - 2.0 * label)), 1) / total
+    loss = jnp.sum(jax.nn.softplus(logit * (1.0 - 2.0 * label)), 1, keepdims=True) / total
     coef = ((jax.nn.sigmoid(logit) - label) * scale).astype(jnp.bfloat16)
     image_part = jnp.dot(coef, seen, preferred_element_type=jnp.float32)
     text_part = lax.dot_general(coef, gathered, (((0,), (0,)), ((), ())), preferred_element_type=jnp.float32)
-    image_sum = gather_sum(image_part, IMAGE_AXES, image_count)
-    image_loss = gather_sum(loss, IMAGE_AXES, image_count)
-    text_sum = gather_sum(text_part, TEXT_AXES, text_count)
-    image_grad = back_rows(image_sum, image_unit, image_norm)
+    image_part = jnp.concatenate([image_part, jnp.broadcast_to(loss, (image_count * rows, LOSS_LANES))], 1)
+    image_in, text_in = exchange(
+        image_part.reshape(image_count, rows, width + LOSS_LANES), text_part.reshape(text_count, rows, width), True, 1
+    )
+    image_in = jnp.sum(image_in, 0)
+    text_sum = jnp.sum(text_in, 0)
+    image_grad = back_rows(image_in[:, :width], image_unit, image_norm)
     text_grad = back_rows(text_sum, text_unit, text_norm)
-    return (image_loss, image_grad, text_grad)
+    return (image_in[:, width], image_grad, text_grad)
 
 
 def solution(mesh):

time: 190 us -> 134 us (0.71)
  the two profiles are of different devices: /device:TPU:24 before, /device:TPU:14 now
where the time goes in v4:
time: 134 us
  Pallas kernels  116 us (87%)
  other arithmetic  9.14 us (7%)
  matrix products  4.73 us (4%)
  between operations  2.04 us (2%)
  local copies, waits for them, and re-layouts  1.55 us (1%)
    pallas_call x2, Pallas kernels, exchange(): pl.pallas_call(functools.partial(exchange_kernel, scatter), out_shape=(ja...  116 us

profile of v4, /device:TPU:14, one launch (start us, length us, event | category | flops | bytes accessed | tf_op | source)
XLA Modules:
  0.0 133.8 jit_solution(5587278009879634133)
XLA Ops:
  2.0 0.9 fusion.10
  2.9 0.9 fusion.11
  3.8 1.5 %fusion.24 = (bf16[16,1152]{1,0:T(8,128)(2,1)}, bf16[16,1152]{1,0:T(8,128)(2,1)}) fusion(f32[16]{0:T(128)S(1)} %add_sqrt_fusion.1, bf16[16,1152]{1,0:T(8,128)(2,1)} %param.4, f32[16]{0:T(128)S(1)} %add_sqrt_fusion, bf16[16,1152]{1,0:T(8,128)(2,1)} %param.5), kind=kLoop, calls=%fused_computation.52 | loop fusion | flops 110592 | bytes 147584 | tf_op jit(solution)/shard_map/convert_element_type | solution.py:120
  5.3 46.0 %shard_map.67 = (bf16[32,16,1152]{2,1,0:T(8,128)(2,1)}, bf16[16,16,1152]{2,1,0:T(8,128)(2,1)}) custom-call(bf16[16,1152]{1,0:T(8,128)(2,1)} %get-tuple-element.13.image_src, bf16[16,1152]{1,0:T(8,128)(2,1)} %get-tuple-element.14.text_src), custom_call_target="tpu_custom_call" | custom-call | tf_op jit(solution)/shard_map/pallas_call | solution.py:101
  51.3 0.0 copy-start
  51.3 2.4 %fusion.1 = (f32[512]{0:T(512)S(1)}, f32[512,256]{0,1:T(8,128)S(1)}) fusion(s32[512]{0:T(512)S(1)} %fusion.12, s32[256]{0:T(256)S(1)} %and_select_fusion, pred[512]{0:T(512)(128)(4,1)S(1)} %fusion.16, pred[256]{0:T(512)(128)(4,1)S(1)} %fusion.22, f32[]{:T(128)S(6)} %copy.8, bf16[512,1152]{1,0:T(8,128)(2,1)} %bitcast.18, bf16[256,1152]{1,0:T(8,128)(2,1)} %bitcast.21, ...), kind=kOutput, calls=%fused_computation.4 | convolution fusion | flops 303955456 | bytes 2299656 | tf_op jit(solution)/shard_map/dot_general | solution.py:137
  53.7 0.1 broadcast_in_dim.2
  53.9 0.2 fusion.3
  54.1 0.0 copy-done
  54.1 0.0 copy-start.4
  54.1 1.6 %fusion.26.text_src = f32[16,16,1152]{2,1,0:T(8,128)} fusion(bf16[16,16,512]{2,1,0:T(8,128)(2,1)S(1)} %bitcast.20, bf16[512,1152,1]{1,0,2:T(8,128)(2,1)S(1)} %bitcast.19), kind=kOutput, calls=%fused_computation.54 | convolution fusion | flops 301989888 | bytes 2621440 | tf_op jit(solution)/shard_map/dot_general | solution.py:143
  55.7 0.7 fusion.4
  56.4 1.7 %pad_maximum_fusion = f32[512,1280]{1,0:T(8,128)} fusion(f32[512,128]{1,0:T(8,128)S(1)} %broadcast_in_dim.2, f32[512,1152]{1,0:T(8,128)S(1)} %fusion.4), kind=kLoop, calls=%fused_computation | loop fusion | flops 655360 | bytes 5242880 | tf_op jit(solution)/shard_map/concatenate | solution.py:144
  58.1 70.3 %shard_map.68 = (f32[32,16,1280]{2,1,0:T(8,128)}, f32[16,16,1152]{2,1,0:T(8,128)}) custom-call(f32[32,16,1280]{2,1,0:T(8,128)} %bitcast.17, f32[16,16,1152]{2,1,0:T(8,128)} %fusion.26.text_src), custom_call_target="tpu_custom_call" | custom-call | tf_op jit(solution)/shard_map/pallas_call | solution.py:101
  128.5 2.0 %reduce_sum.66 = f32[16,1280]{1,0:T(8,128)S(1)} reduce(f32[32,16,1280]{2,1,0:T(8,128)} %get-tuple-element.9, f32[]{:T(128)} %constant.74.clone.1), dimensions={0}, to_apply=%region_3.4 | reduce | flops 634880 | bytes 2703364 | tf_op jit(solution)/shard_map/reduce_sum | solution.py:148
  130.4 0.1 copy-done.1
  130.5 0.1 reduce_sum.68
  130.6 0.7 copy-done.2
  131.3 0.2 multiply_reduce_fusion
  131.5 0.7 subtract_divide_fusion
  132.2 0.0 copy-done.3
  132.2 0.2 multiply_reduce_fusion.1
  132.4 0.6 slice_reduce_fusion
  133.0 0.7 subtract_divide_fusion.1
  (11 shorter events, 0.1 us)
Async XLA Ops:
  51.3 2.8 %copy-start = (bf16[32,16,1152]{2,1,0:T(8,128)(2,1)S(1)}, bf16[32,16,1152]{2,1,0:T(8,128)(2,1)}, u32[]{:S(2)}) copy-start(bf16[32,16,1152]{2,1,0:T(8,128)(2,1)} %get-tuple-element.7) | copy-start | bytes 3538948
  54.1 1.6 %copy-start.4 = (bf16[16,16,1152]{2,1,0:T(8,128)(2,1)S(1)}, bf16[16,16,1152]{2,1,0:T(8,128)(2,1)}, u32[]{:S(2)}) copy-start(bf16[16,16,1152]{2,1,0:T(8,128)(2,1)} %get-tuple-element.8) | copy-start | bytes 1769476
  128.5 2.1 %copy-start.1 = (f32[16,16,1152]{2,1,0:T(8,128)S(1)}, f32[16,16,1152]{2,1,0:T(8,128)}, u32[]{:S(2)}) copy-start(f32[16,16,1152]{2,1,0:T(8,128)} %get-tuple-element.10) | copy-start | bytes 3538948
  130.5 0.8 copy-start.2
  130.5 1.7 %copy-start.3 = (bf16[16,1152]{1,0:T(8,128)(2,1)S(1)}, bf16[16,1152]{1,0:T(8,128)(2,1)}, u32[]{:S(2)}) copy-start(bf16[16,1152]{1,0:T(8,128)(2,1)} %param.4) | copy-start | bytes 110596

commit v5 on v4

--- a/solution.py
+++ b/solution.py
@@ -8,7 +8,8 @@
 from jax.sharding import Mesh, PartitionSpec as P
 
 ROWS_AXES = ("x", "zh", "y", "zl", "c")
-IMAGE_AXES = ("x", "y", "c")
+CHIP_AXES = ("x", "y")
+CORE_AXES = ("c",)
 TEXT_AXES = ("zh", "zl")
 MESH_IDS = pl.DeviceIdType.MESH
 LOSS_LANES = 128
@@ -47,12 +48,16 @@
     return tuple(coords[name] if name in coords else lax.axis_index(name) for name in ROWS_AXES)
 
 
-def exchange_kernel(scatter, image_src, text_src, image_out, text_out, image_send, image_recv, text_send, text_recv):
-    groups = ((IMAGE_AXES, image_src, image_out, image_send, image_recv),
-              (TEXT_AXES, text_src, text_out, text_send, text_recv))
+def exchange_kernel(plan, *refs):
+    count_groups = len(plan)
+    srcs, outs = refs[:count_groups], refs[count_groups:2 * count_groups]
+    sems = refs[2 * count_groups:]
+    groups = [
+        (axes, scatter, srcs[g], outs[g], sems[2 * g], sems[2 * g + 1]) for g, (axes, scatter) in enumerate(plan)
+    ]
     barrier = pltpu.get_barrier_semaphore()
     peers = 0
-    for axes, src, out, send, recv in groups:
+    for axes, scatter, src, out, send, recv in groups:
         count, me = group_size(axes), linear_index(axes)
         peers += count - 1
 
@@ -63,11 +68,10 @@
         lax.fori_loop(1, count, greet, 0)
     pl.semaphore_wait(barrier, peers)
 
-    for axes, src, out, send, recv in groups:
+    for axes, scatter, src, out, send, recv in groups:
         count, me = group_size(axes), linear_index(axes)
-        out[me] = src[me] if scatter else src[...]
 
-        def start(step, carry, axes=axes, count=count, me=me, src=src, out=out, send=send, recv=recv):
+        def start(step, carry, axes=axes, scatter=scatter, count=count, me=me, src=src, out=out, send=send, recv=recv):
             peer = (me + step) % count
             pltpu.make_async_remote_copy(
                 src.at[peer] if scatter else src, out.at[me], send.at[peer], recv.at[me],
@@ -77,10 +81,14 @@
 
         lax.fori_loop(1, count, start, 0)
 
-    for axes, src, out, send, recv in groups:
+    for axes, scatter, src, out, send, recv in groups:
+        count, me = group_size(axes), linear_index(axes)
+        out[me] = src[me] if scatter else src[...]
+
+    for axes, scatter, src, out, send, recv in groups:
         count, me = group_size(axes), linear_index(axes)
 
-        def finish(step, carry, axes=axes, count=count, me=me, src=src, out=out, send=send, recv=recv):
+        def finish(step, carry, axes=axes, scatter=scatter, count=count, me=me, src=src, out=out, send=send, recv=recv):
             peer = (me + step) % count
             copy = pltpu.make_async_remote_copy(
                 src.at[peer] if scatter else src, out.at[peer], send.at[peer], recv.at[peer],
@@ -93,24 +101,25 @@
         lax.fori_loop(1, count, finish, 0)
 
 
-def exchange(image_src, text_src, scatter, tag):
-    image_count, text_count = group_size(IMAGE_AXES), group_size(TEXT_AXES)
-    image_shape = image_src.shape if scatter else (image_count,) + image_src.shape
-    text_shape = text_src.shape if scatter else (text_count,) + text_src.shape
+def exchange(routes, tag):
+    plan = tuple((axes, scatter) for axes, src, scatter in routes)
+    srcs = [src for axes, src, scatter in routes]
+    shapes = [
+        jax.ShapeDtypeStruct(src.shape if scatter else (group_size(axes),) + src.shape, src.dtype)
+        for axes, src, scatter in routes
+    ]
+    sems = []
+    for axes, src, scatter in routes:
+        sems += [pltpu.SemaphoreType.DMA((group_size(axes),))] * 2
     vmem = pl.BlockSpec(memory_space=pltpu.VMEM)
     return pl.pallas_call(
-        functools.partial(exchange_kernel, scatter),
-        out_shape=(jax.ShapeDtypeStruct(image_shape, image_src.dtype), jax.ShapeDtypeStruct(text_shape, text_src.dtype)),
-        in_specs=[vmem, vmem],
-        out_specs=(vmem, vmem),
-        scratch_shapes=[
-            pltpu.SemaphoreType.DMA((image_count,)),
-            pltpu.SemaphoreType.DMA((image_count,)),
-            pltpu.SemaphoreType.DMA((text_count,)),
-            pltpu.SemaphoreType.DMA((text_count,)),
-        ],
+        functools.partial(exchange_kernel, plan),
+        out_shape=tuple(shapes),
+        in_specs=[vmem] * len(routes),
+        out_specs=tuple([vmem] * len(routes)),
+        scratch_shapes=sems,
         compiler_params=pltpu.CompilerParams(collective_id=tag, has_side_effects=True),
-    )(image_src, text_src)
+    )(*srcs)
 
 
 def local(images, texts, scale, shift):
@@ -119,15 +128,18 @@
     text_unit, text_norm = unit_rows(texts)
     image_emb = image_unit.astype(jnp.bfloat16)
     text_emb = text_unit.astype(jnp.bfloat16)
-    image_count = group_size(IMAGE_AXES)
+    chips = group_size(CHIP_AXES)
+    cores = group_size(CORE_AXES)
+    image_count = chips * cores
     text_count = group_size(TEXT_AXES)
     total = image_count * text_count * rows
-    gathered, seen = exchange(image_emb, text_emb, False, 0)
+    same_core, seen = exchange([(CHIP_AXES, image_emb, False), (TEXT_AXES, text_emb, False)], 0)
+    (gathered,) = exchange([(CORE_AXES, same_core, False)], 1)
     gathered = gathered.reshape(image_count * rows, width)
     seen = seen.reshape(text_count * rows, width)
     image_ids = jnp.arange(image_count * rows, dtype=jnp.int32)[:, None]
     text_ids = jnp.arange(text_count * rows, dtype=jnp.int32)[None, :]
-    mine_i = linear_index(IMAGE_AXES)
+    mine_i = linear_index(CORE_AXES + CHIP_AXES)
     mine_t = linear_index(TEXT_AXES)
     label = (
         (image_ids // rows == mine_i) & (text_ids // rows == mine_t) & (image_ids % rows == text_ids % rows)
@@ -142,8 +154,10 @@
     image_part = jnp.dot(coef, seen, preferred_element_type=jnp.float32)
     text_part = lax.dot_general(coef, gathered, (((0,), (0,)), ((), ())), preferred_element_type=jnp.float32)
     image_part = jnp.concatenate([image_part, jnp.broadcast_to(loss, (image_count * rows, LOSS_LANES))], 1)
+    (halves,) = exchange([(CORE_AXES, image_part.reshape(cores, chips, rows, width + LOSS_LANES), True)], 2)
+    chip_sum = jnp.sum(halves, 0)
     image_in, text_in = exchange(
-        image_part.reshape(image_count, rows, width + LOSS_LANES), text_part.reshape(text_count, rows, width), True, 1
+        [(CHIP_AXES, chip_sum, True), (TEXT_AXES, text_part.reshape(text_count, rows, width), True)], 3
     )
     image_in = jnp.sum(image_in, 0)
     text_sum = jnp.sum(text_in, 0)

time: 134 us -> 148 us (1.10)
  the two profiles are of different devices: /device:TPU:14 before, /device:TPU:1 now
where the time goes in v5:
time: 148 us; the launch traced here: 147 us
  Pallas kernels  128 us (86%)
  other arithmetic  11.8 us (8%)
  matrix products  4.59 us (3%)
  between operations  2.09 us (1%)
    pallas_call x4, Pallas kernels, exchange(): pl.pallas_call(functools.partial(exchange_kernel, plan), out_shape=tuple(...  128 us
    reduce_sum x1, other arithmetic, local(): chip_sum = jnp.sum(halves, 0)  3.13 us

profile of v5, /device:TPU:1, one launch (start us, length us, event | category | flops | bytes accessed | tf_op | source)
XLA Modules:
  0.0 146.9 jit_solution(18024386445352555251)
XLA Ops:
  2.0 0.9 fusion.10
  2.9 0.9 fusion.11
  3.8 1.5 %fusion.24 = (bf16[16,1152]{1,0:T(8,128)(2,1)}, bf16[16,1152]{1,0:T(8,128)(2,1)}) fusion(f32[16]{0:T(128)S(1)} %add_sqrt_fusion.1, bf16[16,1152]{1,0:T(8,128)(2,1)} %param.4, f32[16]{0:T(128)S(1)} %add_sqrt_fusion, bf16[16,1152]{1,0:T(8,128)(2,1)} %param.5), kind=kLoop, calls=%fused_computation.52 | loop fusion | flops 110592 | bytes 147584 | tf_op jit(solution)/shard_map/convert_element_type | solution.py:129
  5.3 44.9 %shard_map.67 = (bf16[16,16,1152]{2,1,0:T(8,128)(2,1)}, bf16[16,16,1152]{2,1,0:T(8,128)(2,1)}) custom-call(bf16[16,1152]{1,0:T(8,128)(2,1)} %get-tuple-element.13.refs_0_, bf16[16,1152]{1,0:T(8,128)(2,1)} %get-tuple-element.14.refs_1_), custom_call_target="tpu_custom_call" | custom-call | tf_op jit(solution)/shard_map/pallas_call | solution.py:115
  50.2 8.7 %shard_map.68 = bf16[2,16,16,1152]{3,2,1,0:T(8,128)(2,1)} custom-call(bf16[16,16,1152]{2,1,0:T(8,128)(2,1)} %get-tuple-element.7.refs_0_), custom_call_target="tpu_custom_call" | custom-call | tf_op jit(solution)/shard_map/pallas_call | solution.py:115
  58.9 2.3 %fusion.1 = (f32[512]{0:T(512)S(1)}, f32[512,256]{0,1:T(8,128)S(1)}) fusion(s32[512]{0:T(512)S(1)} %fusion.12, s32[256]{0:T(256)S(1)} %and_select_fusion, pred[512]{0:T(512)(128)(4,1)S(1)} %fusion.16, pred[256]{0:T(512)(128)(4,1)S(1)} %fusion.22, f32[]{:T(128)S(6)} %copy.8, bf16[512,1152]{1,0:T(8,128)(2,1)} %bitcast.18, bf16[256,1152]{1,0:T(8,128)(2,1)S(1)} %bitcast.21, ...), kind=kOutput, calls=%fused_computation.4 | convolution fusion | flops 303955456 | bytes 2299656 | tf_op jit(solution)/shard_map/dot_general | solution.py:149
  61.2 0.1 broadcast_in_dim.2
  61.4 0.2 fusion.3
  61.6 1.6 %fusion.26.refs_1_ = f32[16,16,1152]{2,1,0:T(8,128)} fusion(bf16[16,16,512]{2,1,0:T(8,128)(2,1)S(1)} %bitcast.20, bf16[512,1152,1]{1,0,2:T(8,128)(2,1)S(1)} %bitcast.19), kind=kOutput, calls=%fused_computation.54 | convolution fusion | flops 301989888 | bytes 2621440 | tf_op jit(solution)/shard_map/dot_general | solution.py:155
  63.2 0.7 fusion.4
  63.9 1.7 %pad_maximum_fusion = f32[512,1280]{1,0:T(8,128)} fusion(f32[512,128]{1,0:T(8,128)S(1)} %broadcast_in_dim.2, f32[512,1152]{1,0:T(8,128)S(1)} %fusion.4), kind=kLoop, calls=%fused_computation | loop fusion | flops 655360 | bytes 5242880 | tf_op jit(solution)/shard_map/concatenate | solution.py:156
  65.7 7.0 %shard_map.69 = f32[2,16,16,1280]{3,2,1,0:T(8,128)} custom-call(f32[2,16,16,1280]{3,2,1,0:T(8,128)} %bitcast.17), custom_call_target="tpu_custom_call" | custom-call | tf_op jit(solution)/shard_map/pallas_call | solution.py:115
  72.7 3.1 %reduce_sum.75.refs_0_ = f32[16,16,1280]{2,1,0:T(8,128)} reduce(f32[2,16,16,1280]{3,2,1,0:T(8,128)} %shard_map.69, f32[]{:T(128)} %constant.73.clone.1), dimensions={0}, to_apply=%region_3.4 | reduce | flops 327680 | bytes 3932164 | tf_op jit(solution)/shard_map/reduce_sum | solution.py:158
  75.8 66.9 %shard_map.70 = (f32[16,16,1280]{2,1,0:T(8,128)}, f32[16,16,1152]{2,1,0:T(8,128)}) custom-call(f32[16,16,1280]{2,1,0:T(8,128)} %reduce_sum.75.refs_0_, f32[16,16,1152]{2,1,0:T(8,128)} %fusion.26.refs_1_), custom_call_target="tpu_custom_call" | custom-call | tf_op jit(solution)/shard_map/pallas_call | solution.py:115
  142.7 0.0 copy-start.2
  142.8 0.0 copy-start.3
  142.8 1.5 %reduce_sum.76 = f32[16,1280]{1,0:T(8,128)S(1)} reduce(f32[16,16,1280]{2,1,0:T(8,128)} %get-tuple-element.9, f32[]{:T(128)} %constant.73.clone.1), dimensions={0}, to_apply=%region_4.5 | reduce | flops 307200 | bytes 1392644 | tf_op jit(solution)/shard_map/reduce_sum | solution.py:162
  144.2 0.1 copy-done.1
  144.4 0.1 reduce_sum.78
  144.5 0.2 multiply_reduce_fusion
  144.7 0.7 subtract_divide_fusion
  145.4 0.2 multiply_reduce_fusion.1
  145.6 0.6 slice_reduce_fusion
  146.2 0.7 subtract_divide_fusion.1
  (14 shorter events, 0.1 us)
Async XLA Ops:
  50.2 8.8 %copy-start.4 = (bf16[16,16,1152]{2,1,0:T(8,128)(2,1)S(1)}, bf16[16,16,1152]{2,1,0:T(8,128)(2,1)}, u32[]{:S(2)}) copy-start(bf16[16,16,1152]{2,1,0:T(8,128)(2,1)} %get-tuple-element.8) | copy-start | bytes 1769476
  58.9 2.7 %copy-start = (bf16[2,16,16,1152]{3,2,1,0:T(8,128)(2,1)S(1)}, bf16[2,16,16,1152]{3,2,1,0:T(8,128)(2,1)}, u32[]{:S(2)}) copy-start(bf16[2,16,16,1152]{3,2,1,0:T(8,128)(2,1)} %shard_map.68) | copy-start | bytes 3538948
  142.7 1.7 %copy-start.1 = (f32[16,16,1152]{2,1,0:T(8,128)S(1)}, f32[16,16,1152]{2,1,0:T(8,128)}, u32[]{:S(2)}) copy-start(f32[16,16,1152]{2,1,0:T(8,128)} %get-tuple-element.10) | copy-start | bytes 3538948
  142.7 1.7 %copy-start.2 = (bf16[16,1152]{1,0:T(8,128)(2,1)S(1)}, bf16[16,1152]{1,0:T(8,128)(2,1)}, u32[]{:S(2)}) copy-start(bf16[16,1152]{1,0:T(8,128)(2,1)} %param.5) | copy-start | bytes 110596
  142.8 2.6 %copy-start.3 = (bf16[16,1152]{1,0:T(8,128)(2,1)S(1)}, bf16[16,1152]{1,0:T(8,128)(2,1)}, u32[]{:S(2)}) copy-start(bf16[16,1152]{1,0:T(8,128)(2,1)} %param.4) | copy-start | bytes 110596

commit v6 on v4

--- a/solution.py
+++ b/solution.py
@@ -47,68 +47,124 @@
     return tuple(coords[name] if name in coords else lax.axis_index(name) for name in ROWS_AXES)
 
 
-def exchange_kernel(scatter, image_src, text_src, image_out, text_out, image_send, image_recv, text_send, text_recv):
-    groups = ((IMAGE_AXES, image_src, image_out, image_send, image_recv),
-              (TEXT_AXES, text_src, text_out, text_send, text_recv))
-    barrier = pltpu.get_barrier_semaphore()
-    peers = 0
-    for axes, src, out, send, recv in groups:
-        count, me = group_size(axes), linear_index(axes)
-        peers += count - 1
-
-        def greet(step, carry, axes=axes, count=count, me=me):
-            pl.semaphore_signal(barrier, 1, device_id=member(axes, (me + step) % count), device_id_type=MESH_IDS)
-            return carry
-
-        lax.fori_loop(1, count, greet, 0)
-    pl.semaphore_wait(barrier, peers)
-
-    for axes, src, out, send, recv in groups:
-        count, me = group_size(axes), linear_index(axes)
-        out[me] = src[me] if scatter else src[...]
-
-        def start(step, carry, axes=axes, count=count, me=me, src=src, out=out, send=send, recv=recv):
-            peer = (me + step) % count
-            pltpu.make_async_remote_copy(
-                src.at[peer] if scatter else src, out.at[me], send.at[peer], recv.at[me],
-                device_id=member(axes, peer), device_id_type=MESH_IDS,
-            ).start()
-            return carry
-
-        lax.fori_loop(1, count, start, 0)
-
-    for axes, src, out, send, recv in groups:
-        count, me = group_size(axes), linear_index(axes)
-
-        def finish(step, carry, axes=axes, count=count, me=me, src=src, out=out, send=send, recv=recv):
-            peer = (me + step) % count
-            copy = pltpu.make_async_remote_copy(
-                src.at[peer] if scatter else src, out.at[peer], send.at[peer], recv.at[peer],
-                device_id=member(axes, peer), device_id_type=MESH_IDS,
-            )
-            copy.wait_send()
-            copy.wait_recv()
-            return carry
-
-        lax.fori_loop(1, count, finish, 0)
+def ring_peers():
+    count, me = group_size(TEXT_AXES), linear_index(TEXT_AXES)
+    return count, me, member(TEXT_AXES, (me + 1) % count), member(TEXT_AXES, (me + count - 1) % count)
+
+
+def remote(src, dst, send, recv, device):
+    return pltpu.make_async_remote_copy(src, dst, send, recv, device_id=device, device_id_type=MESH_IDS)
+
+
+def greet_all(barrier, image_count, image_me, right, left):
+    def greet(step, carry):
+        pl.semaphore_signal(barrier, 1, device_id=member(IMAGE_AXES, (image_me + step) % image_count),
+                            device_id_type=MESH_IDS)
+        return carry
+
+    lax.fori_loop(1, image_count, greet, 0)
+    for device in (right, left):
+        pl.semaphore_signal(barrier, 1, device_id=device, device_id_type=MESH_IDS)
+    pl.semaphore_wait(barrier, image_count + 1)
+
+
+def image_direct(scatter, src, out, send, recv, count, me):
+    def start(step, carry):
+        peer = (me + step) % count
+        remote(src.at[peer] if scatter else src, out.at[me], send.at[peer], recv.at[me],
+               member(IMAGE_AXES, peer)).start()
+        return carry
+
+    lax.fori_loop(1, count, start, 0)
+    out[me] = src[me] if scatter else src[...]
+
+    def finish(step, carry):
+        peer = (me + step) % count
+        copy = remote(src.at[peer] if scatter else src, out.at[peer], send.at[peer], recv.at[peer],
+                      member(IMAGE_AXES, peer))
+        copy.wait_send()
+        copy.wait_recv()
+        return carry
+
+    return finish
+
+
+def gather_kernel(image_src, text_src, image_out, text_out, image_send, image_recv, text_send, text_recv):
+    image_count, image_me = group_size(IMAGE_AXES), linear_index(IMAGE_AXES)
+    count, me, right, left = ring_peers()
+    half = count // 2
+    greet_all(pltpu.get_barrier_semaphore(), image_count, image_me, right, left)
+    finish = image_direct(False, image_src, image_out, image_send, image_recv, image_count, image_me)
+    sends = [remote(text_src, text_out.at[me], text_send.at[0], text_recv.at[me], right),
+             remote(text_src, text_out.at[me], text_send.at[half], text_recv.at[me], left)]
+    for copy in sends:
+        copy.start()
+    text_out[me] = text_src[...]
+    for step in range(1, half):
+        for origin, device, slot in (((me + count - step) % count, right, step), ((me + step) % count, left, half + step)):
+            if slot >= count - 1:
+                continue
+            arrived = remote(text_out.at[origin], text_out.at[origin], text_send.at[slot], text_recv.at[origin], device)
+            arrived.wait_recv()
+            arrived.start()
+            sends.append(arrived)
+    for origin in ((me + count - half) % count, (me + half - 1) % count):
+        remote(text_out.at[origin], text_out.at[origin], text_send.at[0], text_recv.at[origin], right).wait_recv()
+    for copy in sends:
+        copy.wait_send()
+    lax.fori_loop(1, image_count, finish, 0)
+
+
+def reduce_kernel(image_src, text_src, image_out, text_out, image_send, image_recv, text_send, text_recv,
+                  inbox, outbox):
+    image_count, image_me = group_size(IMAGE_AXES), linear_index(IMAGE_AXES)
+    count, me, right, left = ring_peers()
+    half = count // 2
+    greet_all(pltpu.get_barrier_semaphore(), image_count, image_me, right, left)
+    finish = image_direct(True, image_src, image_out, image_send, image_recv, image_count, image_me)
+    sends = [remote(text_src.at[(me + half) % count], inbox.at[0], text_send.at[0], text_recv.at[0], right),
+             remote(text_src.at[(me + half + 1) % count], inbox.at[half], text_send.at[half], text_recv.at[half], left)]
+    for copy in sends:
+        copy.start()
+    for step in range(1, half):
+        chains = ((step, (me + half - step) % count, right), (half + step, (me + half + 1 + step) % count, left))
+        for slot, target, device in chains:
+            if slot >= count - 1:
+                continue
+            remote(inbox.at[slot - 1], inbox.at[slot - 1], text_send.at[slot], text_recv.at[slot - 1], device).wait_recv()
+            outbox[slot] = inbox[slot - 1] + text_src[target]
+            copy = remote(outbox.at[slot], inbox.at[slot], text_send.at[slot], text_recv.at[slot], device)
+            copy.start()
+            sends.append(copy)
+    last_right, last_left = half - 1, count - 2
+    for slot in (last_right, last_left):
+        remote(inbox.at[slot], inbox.at[slot], text_send.at[0], text_recv.at[slot], right).wait_recv()
+    text_out[...] = text_src[me] + inbox[last_right] + inbox[last_left]
+    for copy in sends:
+        copy.wait_send()
+    lax.fori_loop(1, image_count, finish, 0)
 
 
 def exchange(image_src, text_src, scatter, tag):
     image_count, text_count = group_size(IMAGE_AXES), group_size(TEXT_AXES)
     image_shape = image_src.shape if scatter else (image_count,) + image_src.shape
-    text_shape = text_src.shape if scatter else (text_count,) + text_src.shape
+    text_shape = text_src.shape[1:] if scatter else (text_count,) + text_src.shape
+    block = text_src.shape[1:] if scatter else text_src.shape
     vmem = pl.BlockSpec(memory_space=pltpu.VMEM)
+    scratch = [
+        pltpu.SemaphoreType.DMA((image_count,)),
+        pltpu.SemaphoreType.DMA((image_count,)),
+        pltpu.SemaphoreType.DMA((text_count,)),
+        pltpu.SemaphoreType.DMA((text_count,)),
+    ]
+    if scatter:
+        scratch += [pltpu.VMEM((text_count,) + block, text_src.dtype)] * 2
     return pl.pallas_call(
-        functools.partial(exchange_kernel, scatter),
+        reduce_kernel if scatter else gather_kernel,
         out_shape=(jax.ShapeDtypeStruct(image_shape, image_src.dtype), jax.ShapeDtypeStruct(text_shape, text_src.dtype)),
         in_specs=[vmem, vmem],
         out_specs=(vmem, vmem),
-        scratch_shapes=[
-            pltpu.SemaphoreType.DMA((image_count,)),
-            pltpu.SemaphoreType.DMA((image_count,)),
-            pltpu.SemaphoreType.DMA((text_count,)),
-            pltpu.SemaphoreType.DMA((text_count,)),
-        ],
+        scratch_shapes=scratch,
         compiler_params=pltpu.CompilerParams(collective_id=tag, has_side_effects=True),
     )(image_src, text_src)
 
@@ -146,7 +202,7 @@
         image_part.reshape(image_count, rows, width + LOSS_LANES), text_part.reshape(text_count, rows, width), True, 1
     )
     image_in = jnp.sum(image_in, 0)
-    text_sum = jnp.sum(text_in, 0)
+    text_sum = text_in
     image_grad = back_rows(image_in[:, :width], image_unit, image_norm)
     text_grad = back_rows(text_sum, text_unit, text_norm)
     return (image_in[:, width], image_grad, text_grad)

time: 134 us -> 130 us (0.970)
  the two profiles are of different devices: /device:TPU:14 before, /device:TPU:24 now
where the time goes in v6:
time: 130 us; the launch traced here: 128 us
  Pallas kernels  112 us (86%)
  other arithmetic  9.02 us (7%)
  matrix products  4.73 us (4%)
  between operations  2.06 us (2%)
    pallas_call x2, Pallas kernels, exchange(): pl.pallas_call(reduce_kernel if scatter else gather_kernel, out_shape=(ja...  112 us

profile of v6, /device:TPU:24, one launch (start us, length us, event | category | flops | bytes accessed | tf_op | source)
XLA Modules:
  0.0 128.3 jit_solution(14684280442943641806)
XLA Ops:
  2.0 0.9 fusion.10
  2.9 0.9 fusion.11
  3.8 1.5 %fusion.24 = (bf16[16,1152]{1,0:T(8,128)(2,1)}, bf16[16,1152]{1,0:T(8,128)(2,1)}) fusion(f32[16]{0:T(128)S(1)} %add_sqrt_fusion.1, bf16[16,1152]{1,0:T(8,128)(2,1)} %param.4, f32[16]{0:T(128)S(1)} %add_sqrt_fusion, bf16[16,1152]{1,0:T(8,128)(2,1)} %param.5), kind=kLoop, calls=%fused_computation.52 | loop fusion | flops 110592 | bytes 147584 | tf_op jit(solution)/shard_map/convert_element_type | solution.py:176
  5.3 42.1 %shard_map.67 = (bf16[32,16,1152]{2,1,0:T(8,128)(2,1)}, bf16[16,16,1152]{2,1,0:T(8,128)(2,1)}) custom-call(bf16[16,1152]{1,0:T(8,128)(2,1)} %get-tuple-element.13.image_src, bf16[16,1152]{1,0:T(8,128)(2,1)} %get-tuple-element.14.text_src), custom_call_target="tpu_custom_call" | custom-call | tf_op jit(solution)/shard_map/pallas_call | solution.py:162
  47.4 0.0 copy-start
  47.4 2.4 %fusion.1 = (f32[512]{0:T(512)S(1)}, f32[512,256]{0,1:T(8,128)S(1)}) fusion(s32[512]{0:T(512)S(1)} %fusion.12, s32[256]{0:T(256)S(1)} %and_select_fusion, pred[512]{0:T(512)(128)(4,1)S(1)} %fusion.16, pred[256]{0:T(512)(128)(4,1)S(1)} %fusion.22, f32[]{:T(128)S(6)} %copy.8, bf16[512,1152]{1,0:T(8,128)(2,1)} %bitcast.18, bf16[256,1152]{1,0:T(8,128)(2,1)} %bitcast.21, ...), kind=kOutput, calls=%fused_computation.4 | convolution fusion | flops 303955456 | bytes 2299656 | tf_op jit(solution)/shard_map/dot_general | solution.py:193
  49.9 0.1 broadcast_in_dim.2
  50.0 0.2 fusion.3
  50.2 0.0 copy-done
  50.3 0.0 copy-start.4
  50.3 1.6 %fusion.26.text_src = f32[16,16,1152]{2,1,0:T(8,128)} fusion(bf16[16,16,512]{2,1,0:T(8,128)(2,1)S(1)} %bitcast.20, bf16[512,1152,1]{1,0,2:T(8,128)(2,1)S(1)} %bitcast.19), kind=kOutput, calls=%fused_computation.54 | convolution fusion | flops 301989888 | bytes 2621440 | tf_op jit(solution)/shard_map/dot_general | solution.py:199
  51.8 0.0 copy-done.4
  51.8 0.7 fusion.4
  52.6 1.7 %pad_maximum_fusion = f32[512,1280]{1,0:T(8,128)} fusion(f32[512,128]{1,0:T(8,128)S(1)} %broadcast_in_dim.2, f32[512,1152]{1,0:T(8,128)S(1)} %fusion.4), kind=kLoop, calls=%fused_computation | loop fusion | flops 655360 | bytes 5242880 | tf_op jit(solution)/shard_map/concatenate | solution.py:200
  54.3 69.6 %shard_map.68 = (f32[32,16,1280]{2,1,0:T(8,128)}, f32[16,1152]{1,0:T(8,128)}) custom-call(f32[32,16,1280]{2,1,0:T(8,128)} %bitcast.17, f32[16,16,1152]{2,1,0:T(8,128)} %fusion.26.text_src), custom_call_target="tpu_custom_call" | custom-call | tf_op jit(solution)/shard_map/pallas_call | solution.py:162
  123.9 0.0 copy-start.1
  123.9 0.0 copy-start.2
  123.9 1.9 %reduce_sum.57 = f32[16,1280]{1,0:T(8,128)S(1)} reduce(f32[32,16,1280]{2,1,0:T(8,128)} %get-tuple-element.9, f32[]{:T(128)} %constant.74.clone.1), dimensions={0}, to_apply=%region_3.4 | reduce | flops 634880 | bytes 2703364 | tf_op jit(solution)/shard_map/reduce_sum | solution.py:204
  125.8 0.2 multiply_reduce_fusion.1
  126.0 0.6 slice_reduce_fusion
  126.7 0.7 subtract_divide_fusion.1
  127.4 0.0 copy-done.3
  127.4 0.2 multiply_reduce_fusion
  127.6 0.7 subtract_divide_fusion
  (10 shorter events, 0.1 us)
Async XLA Ops:
  47.4 2.8 %copy-start = (bf16[32,16,1152]{2,1,0:T(8,128)(2,1)S(1)}, bf16[32,16,1152]{2,1,0:T(8,128)(2,1)}, u32[]{:S(2)}) copy-start(bf16[32,16,1152]{2,1,0:T(8,128)(2,1)} %get-tuple-element.7) | copy-start | bytes 3538948
  50.3 1.6 %copy-start.4 = (bf16[16,16,1152]{2,1,0:T(8,128)(2,1)S(1)}, bf16[16,16,1152]{2,1,0:T(8,128)(2,1)}, u32[]{:S(2)}) copy-start(bf16[16,16,1152]{2,1,0:T(8,128)(2,1)} %get-tuple-element.8) | copy-start | bytes 1769476
  123.9 1.9 %copy-start.1 = (bf16[16,1152]{1,0:T(8,128)(2,1)S(1)}, bf16[16,1152]{1,0:T(8,128)(2,1)}, u32[]{:S(2)}) copy-start(bf16[16,1152]{1,0:T(8,128)(2,1)} %param.4) | copy-start | bytes 110596
  123.9 3.5 %copy-start.2 = (bf16[16,1152]{1,0:T(8,128)(2,1)S(1)}, bf16[16,1152]{1,0:T(8,128)(2,1)}, u32[]{:S(2)}) copy-start(bf16[16,1152]{1,0:T(8,128)(2,1)} %param.5) | copy-start | bytes 110596
  123.9 3.5 %copy-start.3 = (f32[16,1152]{1,0:T(8,128)S(1)}, f32[16,1152]{1,0:T(8,128)}, u32[]{:S(2)}) copy-start(f32[16,1152]{1,0:T(8,128)} %get-tuple-element.10) | copy-start | bytes 221188

commit v7 on v6

--- a/solution.py
+++ b/solution.py
@@ -8,7 +8,8 @@
 from jax.sharding import Mesh, PartitionSpec as P
 
 ROWS_AXES = ("x", "zh", "y", "zl", "c")
-IMAGE_AXES = ("x", "y", "c")
+CHIP_AXES = ("x", "y")
+CORE_AXES = ("c",)
 TEXT_AXES = ("zh", "zl")
 MESH_IDS = pl.DeviceIdType.MESH
 LOSS_LANES = 128
@@ -56,9 +57,9 @@
     return pltpu.make_async_remote_copy(src, dst, send, recv, device_id=device, device_id_type=MESH_IDS)
 
 
-def greet_all(barrier, image_count, image_me, right, left):
+def greet_all(image_axes, barrier, image_count, image_me, right, left):
     def greet(step, carry):
-        pl.semaphore_signal(barrier, 1, device_id=member(IMAGE_AXES, (image_me + step) % image_count),
+        pl.semaphore_signal(barrier, 1, device_id=member(image_axes, (image_me + step) % image_count),
                             device_id_type=MESH_IDS)
         return carry
 
@@ -68,11 +69,11 @@
     pl.semaphore_wait(barrier, image_count + 1)
 
 
-def image_direct(scatter, src, out, send, recv, count, me):
+def image_direct(image_axes, scatter, src, out, send, recv, count, me):
     def start(step, carry):
         peer = (me + step) % count
         remote(src.at[peer] if scatter else src, out.at[me], send.at[peer], recv.at[me],
-               member(IMAGE_AXES, peer)).start()
+               member(image_axes, peer)).start()
         return carry
 
     lax.fori_loop(1, count, start, 0)
@@ -81,7 +82,7 @@
     def finish(step, carry):
         peer = (me + step) % count
         copy = remote(src.at[peer] if scatter else src, out.at[peer], send.at[peer], recv.at[peer],
-                      member(IMAGE_AXES, peer))
+                      member(image_axes, peer))
         copy.wait_send()
         copy.wait_recv()
         return carry
@@ -89,12 +90,12 @@
     return finish
 
 
-def gather_kernel(image_src, text_src, image_out, text_out, image_send, image_recv, text_send, text_recv):
-    image_count, image_me = group_size(IMAGE_AXES), linear_index(IMAGE_AXES)
+def gather_kernel(image_axes, image_src, text_src, image_out, text_out, image_send, image_recv, text_send, text_recv):
+    image_count, image_me = group_size(image_axes), linear_index(image_axes)
     count, me, right, left = ring_peers()
     half = count // 2
-    greet_all(pltpu.get_barrier_semaphore(), image_count, image_me, right, left)
-    finish = image_direct(False, image_src, image_out, image_send, image_recv, image_count, image_me)
+    greet_all(image_axes, pltpu.get_barrier_semaphore(), image_count, image_me, right, left)
+    finish = image_direct(image_axes, False, image_src, image_out, image_send, image_recv, image_count, image_me)
     sends = [remote(text_src, text_out.at[me], text_send.at[0], text_recv.at[me], right),
              remote(text_src, text_out.at[me], text_send.at[half], text_recv.at[me], left)]
     for copy in sends:
@@ -115,13 +116,13 @@
     lax.fori_loop(1, image_count, finish, 0)
 
 
-def reduce_kernel(image_src, text_src, image_out, text_out, image_send, image_recv, text_send, text_recv,
+def reduce_kernel(image_axes, image_src, text_src, image_out, text_out, image_send, image_recv, text_send, text_recv,
                   inbox, outbox):
-    image_count, image_me = group_size(IMAGE_AXES), linear_index(IMAGE_AXES)
+    image_count, image_me = group_size(image_axes), linear_index(image_axes)
     count, me, right, left = ring_peers()
     half = count // 2
-    greet_all(pltpu.get_barrier_semaphore(), image_count, image_me, right, left)
-    finish = image_direct(True, image_src, image_out, image_send, image_recv, image_count, image_me)
+    greet_all(image_axes, pltpu.get_barrier_semaphore(), image_count, image_me, right, left)
+    finish = image_direct(image_axes, True, image_src, image_out, image_send, image_recv, image_count, image_me)
     sends = [remote(text_src.at[(me + half) % count], inbox.at[0], text_send.at[0], text_recv.at[0], right),
              remote(text_src.at[(me + half + 1) % count], inbox.at[half], text_send.at[half], text_recv.at[half], left)]
     for copy in sends:
@@ -146,7 +147,7 @@
 
 
 def exchange(image_src, text_src, scatter, tag):
-    image_count, text_count = group_size(IMAGE_AXES), group_size(TEXT_AXES)
+    image_count, text_count = group_size(CHIP_AXES), group_size(TEXT_AXES)
     image_shape = image_src.shape if scatter else (image_count,) + image_src.shape
     text_shape = text_src.shape[1:] if scatter else (text_count,) + text_src.shape
     block = text_src.shape[1:] if scatter else text_src.shape
@@ -160,7 +161,7 @@
     if scatter:
         scratch += [pltpu.VMEM((text_count,) + block, text_src.dtype)] * 2
     return pl.pallas_call(
-        reduce_kernel if scatter else gather_kernel,
+        functools.partial(reduce_kernel if scatter else gather_kernel, CHIP_AXES),
         out_shape=(jax.ShapeDtypeStruct(image_shape, image_src.dtype), jax.ShapeDtypeStruct(text_shape, text_src.dtype)),
         in_specs=[vmem, vmem],
         out_specs=(vmem, vmem),
@@ -169,21 +170,98 @@
     )(image_src, text_src)
 
 
+def pair_kernel(plan, *refs):
+    count_groups = len(plan)
+    srcs, outs = refs[:count_groups], refs[count_groups:2 * count_groups]
+    sems = refs[2 * count_groups:]
+    groups = [
+        (axes, scatter, srcs[g], outs[g], sems[2 * g], sems[2 * g + 1]) for g, (axes, scatter) in enumerate(plan)
+    ]
+    barrier = pltpu.get_barrier_semaphore()
+    peers = 0
+    for axes, scatter, src, out, send, recv in groups:
+        count, me = group_size(axes), linear_index(axes)
+        peers += count - 1
+
+        def greet(step, carry, axes=axes, count=count, me=me):
+            pl.semaphore_signal(barrier, 1, device_id=member(axes, (me + step) % count), device_id_type=MESH_IDS)
+            return carry
+
+        lax.fori_loop(1, count, greet, 0)
+    pl.semaphore_wait(barrier, peers)
+
+    for axes, scatter, src, out, send, recv in groups:
+        count, me = group_size(axes), linear_index(axes)
+
+        def start(step, carry, axes=axes, scatter=scatter, count=count, me=me, src=src, out=out, send=send, recv=recv):
+            peer = (me + step) % count
+            pltpu.make_async_remote_copy(
+                src.at[peer] if scatter else src, out.at[me], send.at[peer], recv.at[me],
+                device_id=member(axes, peer), device_id_type=MESH_IDS,
+            ).start()
+            return carry
+
+        lax.fori_loop(1, count, start, 0)
+
+    for axes, scatter, src, out, send, recv in groups:
+        count, me = group_size(axes), linear_index(axes)
+        out[me] = src[me] if scatter else src[...]
+
+    for axes, scatter, src, out, send, recv in groups:
+        count, me = group_size(axes), linear_index(axes)
+
+        def finish(step, carry, axes=axes, scatter=scatter, count=count, me=me, src=src, out=out, send=send, recv=recv):
+            peer = (me + step) % count
+            copy = pltpu.make_async_remote_copy(
+                src.at[peer] if scatter else src, out.at[peer], send.at[peer], recv.at[peer],
+                device_id=member(axes, peer), device_id_type=MESH_IDS,
+            )
+            copy.wait_send()
+            copy.wait_recv()
+            return carry
+
+        lax.fori_loop(1, count, finish, 0)
+
+
+def pair_exchange(routes, tag):
+    plan = tuple((axes, scatter) for axes, src, scatter in routes)
+    srcs = [src for axes, src, scatter in routes]
+    shapes = [
+        jax.ShapeDtypeStruct(src.shape if scatter else (group_size(axes),) + src.shape, src.dtype)
+        for axes, src, scatter in routes
+    ]
+    sems = []
+    for axes, src, scatter in routes:
+        sems += [pltpu.SemaphoreType.DMA((group_size(axes),))] * 2
+    vmem = pl.BlockSpec(memory_space=pltpu.VMEM)
+    return pl.pallas_call(
+        functools.partial(pair_kernel, plan),
+        out_shape=tuple(shapes),
+        in_specs=[vmem] * len(routes),
+        out_specs=tuple([vmem] * len(routes)),
+        scratch_shapes=sems,
+        compiler_params=pltpu.CompilerParams(collective_id=tag, has_side_effects=True),
+    )(*srcs)
+
+
 def local(images, texts, scale, shift):
     rows, width = images.shape
     image_unit, image_norm = unit_rows(images)
     text_unit, text_norm = unit_rows(texts)
     image_emb = image_unit.astype(jnp.bfloat16)
     text_emb = text_unit.astype(jnp.bfloat16)
-    image_count = group_size(IMAGE_AXES)
+    chips = group_size(CHIP_AXES)
+    cores = group_size(CORE_AXES)
+    image_count = chips * cores
     text_count = group_size(TEXT_AXES)
     total = image_count * text_count * rows
-    gathered, seen = exchange(image_emb, text_emb, False, 0)
+    same_core, seen = exchange(image_emb, text_emb, False, 0)
+    (gathered,) = pair_exchange([(CORE_AXES, same_core, False)], 1)
     gathered = gathered.reshape(image_count * rows, width)
     seen = seen.reshape(text_count * rows, width)
     image_ids = jnp.arange(image_count * rows, dtype=jnp.int32)[:, None]
     text_ids = jnp.arange(text_count * rows, dtype=jnp.int32)[None, :]
-    mine_i = linear_index(IMAGE_AXES)
+    mine_i = linear_index(CORE_AXES + CHIP_AXES)
     mine_t = linear_index(TEXT_AXES)
     label = (
         (image_ids // rows == mine_i) & (text_ids // rows == mine_t) & (image_ids % rows == text_ids % rows)
@@ -198,9 +276,9 @@
     image_part = jnp.dot(coef, seen, preferred_element_type=jnp.float32)
     text_part = lax.dot_general(coef, gathered, (((0,), (0,)), ((), ())), preferred_element_type=jnp.float32)
     image_part = jnp.concatenate([image_part, jnp.broadcast_to(loss, (image_count * rows, LOSS_LANES))], 1)
-    image_in, text_in = exchange(
-        image_part.reshape(image_count, rows, width + LOSS_LANES), text_part.reshape(text_count, rows, width), True, 1
-    )
+    (halves,) = pair_exchange([(CORE_AXES, image_part.reshape(cores, chips, rows, width + LOSS_LANES), True)], 2)
+    chip_sum = jnp.sum(halves, 0)
+    image_in, text_in = exchange(chip_sum, text_part.reshape(text_count, rows, width), True, 3)
     image_in = jnp.sum(image_in, 0)
     text_sum = text_in
     image_grad = back_rows(image_in[:, :width], image_unit, image_norm)

time: 130 us -> 108 us (0.83)
  Pallas kernels: 112 us -> 87.2 us
  other arithmetic: 9.02 us -> 11.7 us
    pallas_call x2 -> x4, Pallas kernels: 112 us -> 87.2 us  [the longest x2 75.2 us: exchange(): pl.pallas_call(functools.partial(reduce_kernel if scatter else gather_ker...]
    reduce_sum x0 -> x1, other arithmetic: none -> 3.13 us  [local(): chip_sum = jnp.sum(halves, 0)]
where the time goes in v7:
time: 108 us; the launch traced here: 106 us
  Pallas kernels  87.2 us (81%)
  other arithmetic  11.7 us (11%)
  matrix products  4.6 us (4%)
  between operations  2.08 us (2%)
    pallas_call x2, Pallas kernels, exchange(): pl.pallas_call(functools.partial(reduce_kernel if scatter else gather_ker...  75.2 us
    pallas_call x2, Pallas kernels, pair_exchange(): pl.pallas_call(functools.partial(pair_kernel, plan), out_shape=tuple(shap...  11.9 us
    reduce_sum x1, other arithmetic, local(): chip_sum = jnp.sum(halves, 0)  3.13 us
    dot_general x1, matrix products, local(): lax.dot_general(gathered, seen, (((1,), (1,)), ((), ())), preferred_eleme...  2.3 us

profile of v7, /device:TPU:24, one launch (start us, length us, event | category | flops | bytes accessed | tf_op | source)
XLA Modules:
  0.0 106.3 jit_solution(17421493102533495888)
XLA Ops:
  2.0 0.9 fusion.10
  2.9 0.9 fusion.11
  3.8 1.5 %fusion.24 = (bf16[16,1152]{1,0:T(8,128)(2,1)}, bf16[16,1152]{1,0:T(8,128)(2,1)}) fusion(f32[16]{0:T(128)S(1)} %add_sqrt_fusion.1, bf16[16,1152]{1,0:T(8,128)(2,1)} %param.4, f32[16]{0:T(128)S(1)} %add_sqrt_fusion, bf16[16,1152]{1,0:T(8,128)(2,1)} %param.5), kind=kLoop, calls=%fused_computation.52 | loop fusion | flops 110592 | bytes 147584 | tf_op jit(solution)/shard_map/convert_element_type | solution.py:251
  5.3 40.8 %shard_map.67 = (bf16[16,16,1152]{2,1,0:T(8,128)(2,1)}, bf16[16,16,1152]{2,1,0:T(8,128)(2,1)}) custom-call(bf16[16,1152]{1,0:T(8,128)(2,1)} %get-tuple-element.13.image_src, bf16[16,1152]{1,0:T(8,128)(2,1)} %get-tuple-element.14.text_src), custom_call_target="tpu_custom_call" | custom-call | tf_op jit(solution)/shard_map/pallas_call | solution.py:163
  46.1 4.9 %shard_map.68 = bf16[2,16,16,1152]{3,2,1,0:T(8,128)(2,1)} custom-call(bf16[16,16,1152]{2,1,0:T(8,128)(2,1)} %get-tuple-element.7.refs_0_), custom_call_target="tpu_custom_call" | custom-call | tf_op jit(solution)/shard_map/pallas_call | solution.py:237
  51.1 0.0 copy-done.4
  51.1 0.0 copy-start
  51.1 2.3 %fusion.1 = (f32[512]{0:T(512)S(1)}, f32[512,256]{0,1:T(8,128)S(1)}) fusion(s32[512]{0:T(512)S(1)} %fusion.12, s32[256]{0:T(256)S(1)} %and_select_fusion, pred[512]{0:T(512)(128)(4,1)S(1)} %fusion.16, pred[256]{0:T(512)(128)(4,1)S(1)} %fusion.22, f32[]{:T(128)S(6)} %copy.8, bf16[512,1152]{1,0:T(8,128)(2,1)} %bitcast.18, bf16[256,1152]{1,0:T(8,128)(2,1)S(1)} %bitcast.21, ...), kind=kOutput, calls=%fused_computation.4 | convolution fusion | flops 303955456 | bytes 2299656 | tf_op jit(solution)/shard_map/dot_general | solution.py:271
  53.4 0.1 broadcast_in_dim.2
  53.5 0.2 fusion.3
  53.8 1.6 %fusion.26.text_src = f32[16,16,1152]{2,1,0:T(8,128)} fusion(bf16[16,16,512]{2,1,0:T(8,128)(2,1)S(1)} %bitcast.20, bf16[512,1152,1]{1,0,2:T(8,128)(2,1)S(1)} %bitcast.19), kind=kOutput, calls=%fused_computation.54 | convolution fusion | flops 301989888 | bytes 2621440 | tf_op jit(solution)/shard_map/dot_general | solution.py:277
  55.4 0.7 fusion.4
  56.1 1.7 %pad_maximum_fusion = f32[512,1280]{1,0:T(8,128)} fusion(f32[512,128]{1,0:T(8,128)S(1)} %broadcast_in_dim.2, f32[512,1152]{1,0:T(8,128)S(1)} %fusion.4), kind=kLoop, calls=%fused_computation | loop fusion | flops 655360 | bytes 5242880 | tf_op jit(solution)/shard_map/concatenate | solution.py:278
  57.8 7.0 %shard_map.69 = f32[2,16,16,1280]{3,2,1,0:T(8,128)} custom-call(f32[2,16,16,1280]{3,2,1,0:T(8,128)} %bitcast.17), custom_call_target="tpu_custom_call" | custom-call | tf_op jit(solution)/shard_map/pallas_call | solution.py:237
  64.8 3.1 %reduce_sum.66.image_src = f32[16,16,1280]{2,1,0:T(8,128)} reduce(f32[2,16,16,1280]{3,2,1,0:T(8,128)} %shard_map.69, f32[]{:T(128)} %constant.73.clone.1), dimensions={0}, to_apply=%region_3.4 | reduce | flops 327680 | bytes 3932164 | tf_op jit(solution)/shard_map/reduce_sum | solution.py:280
  68.0 34.4 %shard_map.70 = (f32[16,16,1280]{2,1,0:T(8,128)}, f32[16,1152]{1,0:T(8,128)}) custom-call(f32[16,16,1280]{2,1,0:T(8,128)} %reduce_sum.66.image_src, f32[16,16,1152]{2,1,0:T(8,128)} %fusion.26.text_src), custom_call_target="tpu_custom_call" | custom-call | tf_op jit(solution)/shard_map/pallas_call | solution.py:163
  102.4 0.0 copy-start.1
  102.4 0.0 copy-start.2
  102.4 1.4 %reduce_sum.67 = f32[16,1280]{1,0:T(8,128)S(1)} reduce(f32[16,16,1280]{2,1,0:T(8,128)} %get-tuple-element.9, f32[]{:T(128)} %constant.73.clone.1), dimensions={0}, to_apply=%region_4.5 | reduce | flops 307200 | bytes 1392644 | tf_op jit(solution)/shard_map/reduce_sum | solution.py:282
  103.8 0.2 multiply_reduce_fusion.1
  104.0 0.6 slice_reduce_fusion
  104.7 0.7 subtract_divide_fusion.1
  105.4 0.2 multiply_reduce_fusion
  105.6 0.7 subtract_divide_fusion
  (13 shorter events, 0.1 us)
Async XLA Ops:
  46.1 5.0 %copy-start.4 = (bf16[16,16,1152]{2,1,0:T(8,128)(2,1)S(1)}, bf16[16,16,1152]{2,1,0:T(8,128)(2,1)}, u32[]{:S(2)}) copy-start(bf16[16,16,1152]{2,1,0:T(8,128)(2,1)} %get-tuple-element.8) | copy-start | bytes 1769476
  51.1 2.7 %copy-start = (bf16[2,16,16,1152]{3,2,1,0:T(8,128)(2,1)S(1)}, bf16[2,16,16,1152]{3,2,1,0:T(8,128)(2,1)}, u32[]{:S(2)}) copy-start(bf16[2,16,16,1152]{3,2,1,0:T(8,128)(2,1)} %shard_map.68) | copy-start | bytes 3538948
  102.4 1.5 %copy-start.1 = (bf16[16,1152]{1,0:T(8,128)(2,1)S(1)}, bf16[16,1152]{1,0:T(8,128)(2,1)}, u32[]{:S(2)}) copy-start(bf16[16,1152]{1,0:T(8,128)(2,1)} %param.4) | copy-start | bytes 110596
  102.4 3.0 %copy-start.2 = (bf16[16,1152]{1,0:T(8,128)(2,1)S(1)}, bf16[16,1152]{1,0:T(8,128)(2,1)}, u32[]{:S(2)}) copy-start(bf16[16,1152]{1,0:T(8,128)(2,1)} %param.5) | copy-start | bytes 110596
  102.4 3.0 %copy-start.3 = (f32[16,1152]{1,0:T(8,128)S(1)}, f32[16,1152]{1,0:T(8,128)}, u32[]{:S(2)}) copy-start(f32[16,1152]{1,0:T(8,128)} %get-tuple-element.10) | copy-start | bytes 221188

commit v8 on v7

--- a/solution.py
+++ b/solution.py
@@ -146,8 +146,8 @@
     lax.fori_loop(1, image_count, finish, 0)
 
 
-def exchange(image_src, text_src, scatter, tag):
-    image_count, text_count = group_size(CHIP_AXES), group_size(TEXT_AXES)
+def exchange(image_axes, image_src, text_src, scatter, tag):
+    image_count, text_count = group_size(image_axes), group_size(TEXT_AXES)
     image_shape = image_src.shape if scatter else (image_count,) + image_src.shape
     text_shape = text_src.shape[1:] if scatter else (text_count,) + text_src.shape
     block = text_src.shape[1:] if scatter else text_src.shape
@@ -161,7 +161,7 @@
     if scatter:
         scratch += [pltpu.VMEM((text_count,) + block, text_src.dtype)] * 2
     return pl.pallas_call(
-        functools.partial(reduce_kernel if scatter else gather_kernel, CHIP_AXES),
+        functools.partial(reduce_kernel if scatter else gather_kernel, image_axes),
         out_shape=(jax.ShapeDtypeStruct(image_shape, image_src.dtype), jax.ShapeDtypeStruct(text_shape, text_src.dtype)),
         in_specs=[vmem, vmem],
         out_specs=(vmem, vmem),
@@ -255,8 +255,7 @@
     image_count = chips * cores
     text_count = group_size(TEXT_AXES)
     total = image_count * text_count * rows
-    same_core, seen = exchange(image_emb, text_emb, False, 0)
-    (gathered,) = pair_exchange([(CORE_AXES, same_core, False)], 1)
+    gathered, seen = exchange(CORE_AXES + CHIP_AXES, image_emb, text_emb, False, 0)
     gathered = gathered.reshape(image_count * rows, width)
     seen = seen.reshape(text_count * rows, width)
     image_ids = jnp.arange(image_count * rows, dtype=jnp.int32)[:, None]
@@ -278,7 +277,7 @@
     image_part = jnp.concatenate([image_part, jnp.broadcast_to(loss, (image_count * rows, LOSS_LANES))], 1)
     (halves,) = pair_exchange([(CORE_AXES, image_part.reshape(cores, chips, rows, width + LOSS_LANES), True)], 2)
     chip_sum = jnp.sum(halves, 0)
-    image_in, text_in = exchange(chip_sum, text_part.reshape(text_count, rows, width), True, 3)
+    image_in, text_in = exchange(CHIP_AXES, chip_sum, text_part.reshape(text_count, rows, width), True, 3)
     image_in = jnp.sum(image_in, 0)
     text_sum = text_in
     image_grad = back_rows(image_in[:, :width], image_unit, image_norm)

time: 108 us -> 104 us (0.963)
  Pallas kernels: 87.2 us -> 83.2 us
    pallas_call x2 -> x1, Pallas kernels: 11.9 us -> 7 us  [pair_exchange(): pl.pallas_call(functools.partial(pair_kernel, plan), out_shape=tuple(shap...]
where the time goes in v8:
time: 104 us; the launch traced here: 102 us
  Pallas kernels  83.2 us (80%)
  other arithmetic  11.7 us (11%)
  matrix products  4.73 us (5%)
  between operations  2.07 us (2%)
    pallas_call x2, Pallas kernels, exchange(): pl.pallas_call(functools.partial(reduce_kernel if scatter else gather_ker...  76.2 us
    pallas_call x1, Pallas kernels, pair_exchange(): pl.pallas_call(functools.partial(pair_kernel, plan), out_shape=tuple(shap...  7 us
    reduce_sum x1, other arithmetic, local(): chip_sum = jnp.sum(halves, 0)  3.13 us
    dot_general x1, matrix products, local(): lax.dot_general(gathered, seen, (((1,), (1,)), ((), ())), preferred_eleme...  2.44 us

profile of v8, /device:TPU:24, one launch (start us, length us, event | category | flops | bytes accessed | tf_op | source)
XLA Modules:
  0.0 102.5 jit_solution(168200405160550902)
XLA Ops:
  2.0 0.9 fusion.10
  2.9 0.9 fusion.11
  3.8 1.5 %fusion.24 = (bf16[16,1152]{1,0:T(8,128)(2,1)}, bf16[16,1152]{1,0:T(8,128)(2,1)}) fusion(f32[16]{0:T(128)S(1)} %add_sqrt_fusion.1, bf16[16,1152]{1,0:T(8,128)(2,1)} %param.4, f32[16]{0:T(128)S(1)} %add_sqrt_fusion, bf16[16,1152]{1,0:T(8,128)(2,1)} %param.5), kind=kLoop, calls=%fused_computation.52 | loop fusion | flops 110592 | bytes 147584 | tf_op jit(solution)/shard_map/convert_element_type | solution.py:251
  5.3 42.2 %shard_map.67 = (bf16[32,16,1152]{2,1,0:T(8,128)(2,1)}, bf16[16,16,1152]{2,1,0:T(8,128)(2,1)}) custom-call(bf16[16,1152]{1,0:T(8,128)(2,1)} %get-tuple-element.13.image_src, bf16[16,1152]{1,0:T(8,128)(2,1)} %get-tuple-element.14.text_src), custom_call_target="tpu_custom_call" | custom-call | tf_op jit(solution)/shard_map/pallas_call | solution.py:163
  47.5 0.0 copy-start
  47.5 2.4 %fusion.1 = (f32[512]{0:T(512)S(1)}, f32[512,256]{0,1:T(8,128)S(1)}) fusion(s32[512]{0:T(512)S(1)} %fusion.12, s32[256]{0:T(256)S(1)} %and_select_fusion, pred[512]{0:T(512)(128)(4,1)S(1)} %fusion.16, pred[256]{0:T(512)(128)(4,1)S(1)} %fusion.22, f32[]{:T(128)S(6)} %copy.8, bf16[512,1152]{1,0:T(8,128)(2,1)} %bitcast.18, bf16[256,1152]{1,0:T(8,128)(2,1)} %bitcast.21, ...), kind=kOutput, calls=%fused_computation.4 | convolution fusion | flops 303955456 | bytes 2299656 | tf_op jit(solution)/shard_map/dot_general | solution.py:270
  49.9 0.1 broadcast_in_dim.2
  50.1 0.2 fusion.3
  50.3 0.0 copy-done
  50.3 1.6 %fusion.26.text_src = f32[16,16,1152]{2,1,0:T(8,128)} fusion(bf16[16,16,512]{2,1,0:T(8,128)(2,1)S(1)} %bitcast.20, bf16[512,1152,1]{1,0,2:T(8,128)(2,1)S(1)} %bitcast.19), kind=kOutput, calls=%fused_computation.54 | convolution fusion | flops 301989888 | bytes 2621440 | tf_op jit(solution)/shard_map/dot_general | solution.py:276
  51.9 0.0 copy-done.4
  51.9 0.7 fusion.4
  52.6 1.7 %pad_maximum_fusion = f32[512,1280]{1,0:T(8,128)} fusion(f32[512,128]{1,0:T(8,128)S(1)} %broadcast_in_dim.2, f32[512,1152]{1,0:T(8,128)S(1)} %fusion.4), kind=kLoop, calls=%fused_computation | loop fusion | flops 655360 | bytes 5242880 | tf_op jit(solution)/shard_map/concatenate | solution.py:277
  54.4 7.0 %shard_map.68 = f32[2,16,16,1280]{3,2,1,0:T(8,128)} custom-call(f32[2,16,16,1280]{3,2,1,0:T(8,128)} %bitcast.17), custom_call_target="tpu_custom_call" | custom-call | tf_op jit(solution)/shard_map/pallas_call | solution.py:237
  61.4 3.1 %reduce_sum.66.image_src = f32[16,16,1280]{2,1,0:T(8,128)} reduce(f32[2,16,16,1280]{3,2,1,0:T(8,128)} %shard_map.68, f32[]{:T(128)} %constant.73.clone.1), dimensions={0}, to_apply=%region_3.4 | reduce | flops 327680 | bytes 3932164 | tf_op jit(solution)/shard_map/reduce_sum | solution.py:279
  64.5 34.0 %shard_map.69 = (f32[16,16,1280]{2,1,0:T(8,128)}, f32[16,1152]{1,0:T(8,128)}) custom-call(f32[16,16,1280]{2,1,0:T(8,128)} %reduce_sum.66.image_src, f32[16,16,1152]{2,1,0:T(8,128)} %fusion.26.text_src), custom_call_target="tpu_custom_call" | custom-call | tf_op jit(solution)/shard_map/pallas_call | solution.py:163
  98.5 0.0 copy-start.1
  98.6 0.0 copy-start.2
  98.6 1.4 %reduce_sum.67 = f32[16,1280]{1,0:T(8,128)S(1)} reduce(f32[16,16,1280]{2,1,0:T(8,128)} %get-tuple-element.9, f32[]{:T(128)} %constant.73.clone.1), dimensions={0}, to_apply=%region_4.5 | reduce | flops 307200 | bytes 1392644 | tf_op jit(solution)/shard_map/reduce_sum | solution.py:281
  100.0 0.2 multiply_reduce_fusion.1
  100.2 0.6 slice_reduce_fusion
  100.8 0.7 subtract_divide_fusion.1
  101.6 0.2 multiply_reduce_fusion
  101.8 0.7 subtract_divide_fusion
  (12 shorter events, 0.1 us)
Async XLA Ops:
  47.5 2.8 %copy-start = (bf16[32,16,1152]{2,1,0:T(8,128)(2,1)S(1)}, bf16[32,16,1152]{2,1,0:T(8,128)(2,1)}, u32[]{:S(2)}) copy-start(bf16[32,16,1152]{2,1,0:T(8,128)(2,1)} %get-tuple-element.7) | copy-start | bytes 3538948
  50.3 1.6 %copy-start.4 = (bf16[16,16,1152]{2,1,0:T(8,128)(2,1)S(1)}, bf16[16,16,1152]{2,1,0:T(8,128)(2,1)}, u32[]{:S(2)}) copy-start(bf16[16,16,1152]{2,1,0:T(8,128)(2,1)} %get-tuple-element.8) | copy-start | bytes 1769476
  98.5 1.5 %copy-start.1 = (bf16[16,1152]{1,0:T(8,128)(2,1)S(1)}, bf16[16,1152]{1,0:T(8,128)(2,1)}, u32[]{:S(2)}) copy-start(bf16[16,1152]{1,0:T(8,128)(2,1)} %param.4) | copy-start | bytes 110596
  98.6 3.0 %copy-start.2 = (bf16[16,1152]{1,0:T(8,128)(2,1)S(1)}, bf16[16,1152]{1,0:T(8,128)(2,1)}, u32[]{:S(2)}) copy-start(bf16[16,1152]{1,0:T(8,128)(2,1)} %param.5) | copy-start | bytes 110596
  98.6 3.0 %copy-start.3 = (f32[16,1152]{1,0:T(8,128)S(1)}, f32[16,1152]{1,0:T(8,128)}, u32[]{:S(2)}) copy-start(f32[16,1152]{1,0:T(8,128)} %get-tuple-element.10) | copy-start | bytes 221188

commit v9 on v8

--- a/solution.py
+++ b/solution.py
@@ -57,16 +57,16 @@
     return pltpu.make_async_remote_copy(src, dst, send, recv, device_id=device, device_id_type=MESH_IDS)
 
 
-def greet_all(image_axes, barrier, image_count, image_me, right, left):
+def greet_all(image_axes, barrier, image_count, image_me, right, left, extra=()):
     def greet(step, carry):
         pl.semaphore_signal(barrier, 1, device_id=member(image_axes, (image_me + step) % image_count),
                             device_id_type=MESH_IDS)
         return carry
 
     lax.fori_loop(1, image_count, greet, 0)
-    for device in (right, left):
+    for device in (right, left) + tuple(extra):
         pl.semaphore_signal(barrier, 1, device_id=device, device_id_type=MESH_IDS)
-    pl.semaphore_wait(barrier, image_count + 1)
+    pl.semaphore_wait(barrier, image_count + 1 + len(extra))
 
 
 def image_direct(image_axes, scatter, src, out, send, recv, count, me):
@@ -144,6 +144,69 @@
     for copy in sends:
         copy.wait_send()
     lax.fori_loop(1, image_count, finish, 0)
+
+
+def merged_reduce_kernel(image_axes, image_src, text_src, image_out, text_out, image_send, image_recv, text_send,
+                         text_recv, inbox, outbox, halfbox, summed, half_sems):
+    image_count, image_me = group_size(image_axes), linear_index(image_axes)
+    count, me, right, left = ring_peers()
+    half = count // 2
+    core = linear_index(CORE_AXES)
+    partner = member(CORE_AXES, 1 - core)
+    greet_all(image_axes, pltpu.get_barrier_semaphore(), image_count, image_me, right, left, (partner,))
+    sends = [remote(text_src.at[(me + half) % count], inbox.at[0], text_send.at[0], text_recv.at[0], right),
+             remote(text_src.at[(me + half + 1) % count], inbox.at[half], text_send.at[half], text_recv.at[half], left)]
+    for copy in sends:
+        copy.start()
+    swap = remote(image_src.at[1 - core], halfbox, half_sems.at[0], half_sems.at[1], partner)
+    swap.start()
+    swap.wait_recv()
+    summed[...] = image_src[core] + halfbox[...]
+    finish = image_direct(image_axes, True, summed, image_out, image_send, image_recv, image_count, image_me)
+    for step in range(1, half):
+        chains = ((step, (me + half - step) % count, right), (half + step, (me + half + 1 + step) % count, left))
+        for slot, target, device in chains:
+            if slot >= count - 1:
+                continue
+            remote(inbox.at[slot - 1], inbox.at[slot - 1], text_send.at[slot], text_recv.at[slot - 1], device).wait_recv()
+            outbox[slot] = inbox[slot - 1] + text_src[target]
+            copy = remote(outbox.at[slot], inbox.at[slot], text_send.at[slot], text_recv.at[slot], device)
+            copy.start()
+            sends.append(copy)
+    last_right, last_left = half - 1, count - 2
+    for slot in (last_right, last_left):
+        remote(inbox.at[slot], inbox.at[slot], text_send.at[0], text_recv.at[slot], right).wait_recv()
+    text_out[...] = text_src[me] + inbox[last_right] + inbox[last_left]
+    for copy in sends:
+        copy.wait_send()
+    swap.wait_send()
+    lax.fori_loop(1, image_count, finish, 0)
+
+
+def merged_reduce(image_axes, image_src, text_src, tag):
+    image_count, text_count = group_size(image_axes), group_size(TEXT_AXES)
+    image_shape = image_src.shape[1:]
+    block = text_src.shape[1:]
+    vmem = pl.BlockSpec(memory_space=pltpu.VMEM)
+    scratch = [
+        pltpu.SemaphoreType.DMA((image_count,)),
+        pltpu.SemaphoreType.DMA((image_count,)),
+        pltpu.SemaphoreType.DMA((text_count,)),
+        pltpu.SemaphoreType.DMA((text_count,)),
+        pltpu.VMEM((text_count,) + block, text_src.dtype),
+        pltpu.VMEM((text_count,) + block, text_src.dtype),
+        pltpu.VMEM(image_shape, image_src.dtype),
+        pltpu.VMEM(image_shape, image_src.dtype),
+        pltpu.SemaphoreType.DMA((2,)),
+    ]
+    return pl.pallas_call(
+        functools.partial(merged_reduce_kernel, image_axes),
+        out_shape=(jax.ShapeDtypeStruct(image_shape, image_src.dtype), jax.ShapeDtypeStruct(block, text_src.dtype)),
+        in_specs=[vmem, vmem],
+        out_specs=(vmem, vmem),
+        scratch_shapes=scratch,
+        compiler_params=pltpu.CompilerParams(collective_id=tag, has_side_effects=True),
+    )(image_src, text_src)
 
 
 def exchange(image_axes, image_src, text_src, scatter, tag):
@@ -275,9 +338,9 @@
     image_part = jnp.dot(coef, seen, preferred_element_type=jnp.float32)
     text_part = lax.dot_general(coef, gathered, (((0,), (0,)), ((), ())), preferred_element_type=jnp.float32)
     image_part = jnp.concatenate([image_part, jnp.broadcast_to(loss, (image_count * rows, LOSS_LANES))], 1)
-    (halves,) = pair_exchange([(CORE_AXES, image_part.reshape(cores, chips, rows, width + LOSS_LANES), True)], 2)
-    chip_sum = jnp.sum(halves, 0)
-    image_in, text_in = exchange(CHIP_AXES, chip_sum, text_part.reshape(text_count, rows, width), True, 3)
+    image_in, text_in = merged_reduce(
+        CHIP_AXES, image_part.reshape(cores, chips, rows, width + LOSS_LANES), text_part.reshape(text_count, rows, width), 3
+    )
     image_in = jnp.sum(image_in, 0)
     text_sum = text_in
     image_grad = back_rows(image_in[:, :width], image_unit, image_norm)

time: 104 us -> 94.5 us (0.909)
  Pallas kernels: 83.2 us -> 77.1 us
  other arithmetic: 11.7 us -> 8.53 us
    pallas_call x2 -> x1, Pallas kernels: 76.2 us -> 42.2 us  [exchange(): pl.pallas_call(functools.partial(reduce_kernel if scatter else gather_ker...]
    pallas_call x1, Pallas kernels: 7 us -> 34.9 us  [merged_reduce(): pl.pallas_call(functools.partial(merged_reduce_kernel, image_axes), out_s...]
    reduce_sum x1 -> x0, other arithmetic: 3.13 us -> none  [local(): chip_sum = jnp.sum(halves, 0)]
where the time goes in v9:
time: 94.5 us; the launch traced here: 93.2 us
  Pallas kernels  77.1 us (82%)
  other arithmetic  8.53 us (9%)
  matrix products  4.72 us (5%)
  between operations  2.06 us (2%)
    pallas_call x1, Pallas kernels, exchange(): pl.pallas_call(functools.partial(reduce_kernel if scatter else gather_ker...  42.2 us
    pallas_call x1, Pallas kernels, merged_reduce(): pl.pallas_call(functools.partial(merged_reduce_kernel, image_axes), out_s...  34.9 us
    dot_general x1, matrix products, local(): lax.dot_general(gathered, seen, (((1,), (1,)), ((), ())), preferred_eleme...  2.44 us

profile of v9, /device:TPU:24, one launch (start us, length us, event | category | flops | bytes accessed | tf_op | source)
XLA Modules:
  0.0 93.2 jit_solution(4883171112443079987)
XLA Ops:
  2.0 0.9 fusion.10
  2.9 0.9 fusion.11
  3.8 1.5 %fusion.24 = (bf16[16,1152]{1,0:T(8,128)(2,1)}, bf16[16,1152]{1,0:T(8,128)(2,1)}) fusion(f32[16]{0:T(128)S(1)} %add_sqrt_fusion.1, bf16[16,1152]{1,0:T(8,128)(2,1)} %param.4, f32[16]{0:T(128)S(1)} %add_sqrt_fusion, bf16[16,1152]{1,0:T(8,128)(2,1)} %param.5), kind=kLoop, calls=%fused_computation.52 | loop fusion | flops 110592 | bytes 147584 | tf_op jit(solution)/shard_map/convert_element_type | solution.py:314
  5.3 42.2 %shard_map.67 = (bf16[32,16,1152]{2,1,0:T(8,128)(2,1)}, bf16[16,16,1152]{2,1,0:T(8,128)(2,1)}) custom-call(bf16[16,1152]{1,0:T(8,128)(2,1)} %get-tuple-element.13.image_src, bf16[16,1152]{1,0:T(8,128)(2,1)} %get-tuple-element.14.text_src), custom_call_target="tpu_custom_call" | custom-call | tf_op jit(solution)/shard_map/pallas_call | solution.py:226
  47.5 0.0 copy-start
  47.5 2.4 %fusion.1 = (f32[512]{0:T(512)S(1)}, f32[512,256]{0,1:T(8,128)S(1)}) fusion(s32[512]{0:T(512)S(1)} %fusion.12, s32[256]{0:T(256)S(1)} %and_select_fusion, pred[512]{0:T(512)(128)(4,1)S(1)} %fusion.16, pred[256]{0:T(512)(128)(4,1)S(1)} %fusion.22, f32[]{:T(128)S(6)} %copy.8, bf16[512,1152]{1,0:T(8,128)(2,1)} %bitcast.18, bf16[256,1152]{1,0:T(8,128)(2,1)} %bitcast.21, ...), kind=kOutput, calls=%fused_computation.4 | convolution fusion | flops 303955456 | bytes 2299656 | tf_op jit(solution)/shard_map/dot_general | solution.py:333
  49.9 0.1 broadcast_in_dim.2
  50.1 0.2 fusion.3
  50.3 0.0 copy-done
  50.3 0.0 copy-start.4
  50.3 1.6 %fusion.26.text_src = f32[16,16,1152]{2,1,0:T(8,128)} fusion(bf16[16,16,512]{2,1,0:T(8,128)(2,1)S(1)} %bitcast.20, bf16[512,1152,1]{1,0,2:T(8,128)(2,1)S(1)} %bitcast.19), kind=kOutput, calls=%fused_computation.54 | convolution fusion | flops 301989888 | bytes 2621440 | tf_op jit(solution)/shard_map/dot_general | solution.py:339
  51.9 0.7 fusion.4
  52.6 1.7 %pad_maximum_fusion = f32[512,1280]{1,0:T(8,128)} fusion(f32[512,128]{1,0:T(8,128)S(1)} %broadcast_in_dim.2, f32[512,1152]{1,0:T(8,128)S(1)} %fusion.4), kind=kLoop, calls=%fused_computation | loop fusion | flops 655360 | bytes 5242880 | tf_op jit(solution)/shard_map/concatenate | solution.py:340
  54.3 34.9 %shard_map.68 = (f32[16,16,1280]{2,1,0:T(8,128)}, f32[16,1152]{1,0:T(8,128)}) custom-call(f32[2,16,16,1280]{3,2,1,0:T(8,128)} %bitcast.17, f32[16,16,1152]{2,1,0:T(8,128)} %fusion.26.text_src), custom_call_target="tpu_custom_call" | custom-call | tf_op jit(solution)/shard_map/pallas_call | solution.py:202
  89.3 0.0 copy-start.1
  89.3 0.0 copy-start.2
  89.3 1.4 %reduce_sum.57 = f32[16,1280]{1,0:T(8,128)S(1)} reduce(f32[16,16,1280]{2,1,0:T(8,128)} %get-tuple-element.9, f32[]{:T(128)} %constant.73.clone.1), dimensions={0}, to_apply=%region_3.4 | reduce | flops 307200 | bytes 1392644 | tf_op jit(solution)/shard_map/reduce_sum | solution.py:344
  90.7 0.0 copy-done.1
  90.7 0.2 multiply_reduce_fusion.1
  90.9 0.6 slice_reduce_fusion
  91.5 0.7 subtract_divide_fusion.1
  92.3 0.0 copy-done.3
  92.3 0.2 multiply_reduce_fusion
  92.5 0.7 subtract_divide_fusion
  (10 shorter events, 0.1 us)
Async XLA Ops:
  47.5 2.8 %copy-start = (bf16[32,16,1152]{2,1,0:T(8,128)(2,1)S(1)}, bf16[32,16,1152]{2,1,0:T(8,128)(2,1)}, u32[]{:S(2)}) copy-start(bf16[32,16,1152]{2,1,0:T(8,128)(2,1)} %get-tuple-element.7) | copy-start | bytes 3538948
  50.3 1.6 %copy-start.4 = (bf16[16,16,1152]{2,1,0:T(8,128)(2,1)S(1)}, bf16[16,16,1152]{2,1,0:T(8,128)(2,1)}, u32[]{:S(2)}) copy-start(bf16[16,16,1152]{2,1,0:T(8,128)(2,1)} %get-tuple-element.8) | copy-start | bytes 1769476
  89.3 1.5 %copy-start.1 = (bf16[16,1152]{1,0:T(8,128)(2,1)S(1)}, bf16[16,1152]{1,0:T(8,128)(2,1)}, u32[]{:S(2)}) copy-start(bf16[16,1152]{1,0:T(8,128)(2,1)} %param.4) | copy-start | bytes 110596
  89.3 3.0 %copy-start.2 = (bf16[16,1152]{1,0:T(8,128)(2,1)S(1)}, bf16[16,1152]{1,0:T(8,128)(2,1)}, u32[]{:S(2)}) copy-start(bf16[16,1152]{1,0:T(8,128)(2,1)} %param.5) | copy-start | bytes 110596
  89.3 3.0 %copy-start.3 = (f32[16,1152]{1,0:T(8,128)S(1)}, f32[16,1152]{1,0:T(8,128)}, u32[]{:S(2)}) copy-start(f32[16,1152]{1,0:T(8,128)} %get-tuple-element.10) | copy-start | bytes 221188

commit v10 on v9

--- a/solution.py
+++ b/solution.py
@@ -70,13 +70,16 @@
 
 
 def image_direct(image_axes, scatter, src, out, send, recv, count, me):
-    def start(step, carry):
-        peer = (me + step) % count
-        remote(src.at[peer] if scatter else src, out.at[me], send.at[peer], recv.at[me],
-               member(image_axes, peer)).start()
-        return carry
-
-    lax.fori_loop(1, count, start, 0)
+    def start(lo, hi):
+        def one(step, carry):
+            peer = (me + step) % count
+            remote(src.at[peer] if scatter else src, out.at[me], send.at[peer], recv.at[me],
+                   member(image_axes, peer)).start()
+            return carry
+
+        if hi > lo:
+            lax.fori_loop(lo, hi, one, 0)
+
     out[me] = src[me] if scatter else src[...]
 
     def finish(step, carry):
@@ -87,7 +90,12 @@
         copy.wait_recv()
         return carry
 
-    return finish
+    return start, finish
+
+
+def share(count, steps, step):
+    per = -(-(count - 1) // steps)
+    return min(count, 1 + per * step), min(count, 1 + per * (step + 1))
 
 
 def gather_kernel(image_axes, image_src, text_src, image_out, text_out, image_send, image_recv, text_send, text_recv):
@@ -95,13 +103,15 @@
     count, me, right, left = ring_peers()
     half = count // 2
     greet_all(image_axes, pltpu.get_barrier_semaphore(), image_count, image_me, right, left)
-    finish = image_direct(image_axes, False, image_src, image_out, image_send, image_recv, image_count, image_me)
+    start, finish = image_direct(image_axes, False, image_src, image_out, image_send, image_recv, image_count, image_me)
     sends = [remote(text_src, text_out.at[me], text_send.at[0], text_recv.at[me], right),
              remote(text_src, text_out.at[me], text_send.at[half], text_recv.at[me], left)]
     for copy in sends:
         copy.start()
     text_out[me] = text_src[...]
+    start(*share(image_count, half, 0))
     for step in range(1, half):
+        start(*share(image_count, half, step))
         for origin, device, slot in (((me + count - step) % count, right, step), ((me + step) % count, left, half + step)):
             if slot >= count - 1:
                 continue
@@ -122,7 +132,8 @@
     count, me, right, left = ring_peers()
     half = count // 2
     greet_all(image_axes, pltpu.get_barrier_semaphore(), image_count, image_me, right, left)
-    finish = image_direct(image_axes, True, image_src, image_out, image_send, image_recv, image_count, image_me)
+    start, finish = image_direct(image_axes, True, image_src, image_out, image_send, image_recv, image_count, image_me)
+    start(1, image_count)
     sends = [remote(text_src.at[(me + half) % count], inbox.at[0], text_send.at[0], text_recv.at[0], right),
              remote(text_src.at[(me + half + 1) % count], inbox.at[half], text_send.at[half], text_recv.at[half], left)]
     for copy in sends:
@@ -162,8 +173,10 @@
     swap.start()
     swap.wait_recv()
     summed[...] = image_src[core] + halfbox[...]
-    finish = image_direct(image_axes, True, summed, image_out, image_send, image_recv, image_count, image_me)
+    start, finish = image_direct(image_axes, True, summed, image_out, image_send, image_recv, image_count, image_me)
+    start(*share(image_count, half, 0))
     for step in range(1, half):
+        start(*share(image_count, half, step))
         chains = ((step, (me + half - step) % count, right), (half + step, (me + half + 1 + step) % count, left))
         for slot, target, device in chains:
             if slot >= count - 1:

time: 94.5 us -> 94.3 us (level)
  no operation moved by 1% of the time
where the time goes in v10:
time: 94.3 us; the launch traced here: 92.6 us
  Pallas kernels  76.5 us (81%)
  other arithmetic  8.53 us (9%)
  matrix products  4.71 us (5%)
  between operations  2.06 us (2%)
    pallas_call x1, Pallas kernels, exchange(): pl.pallas_call(functools.partial(reduce_kernel if scatter else gather_ker...  41.8 us
    pallas_call x1, Pallas kernels, merged_reduce(): pl.pallas_call(functools.partial(merged_reduce_kernel, image_axes), out_s...  34.8 us
    dot_general x1, matrix products, local(): lax.dot_general(gathered, seen, (((1,), (1,)), ((), ())), preferred_eleme...  2.44 us

profile of v10, /device:TPU:24, one launch (start us, length us, event | category | flops | bytes accessed | tf_op | source)
XLA Modules:
  0.0 92.6 jit_solution(16025812050521760122)
XLA Ops:
  2.0 0.9 fusion.10
  2.9 0.9 fusion.11
  3.8 1.5 %fusion.24 = (bf16[16,1152]{1,0:T(8,128)(2,1)}, bf16[16,1152]{1,0:T(8,128)(2,1)}) fusion(f32[16]{0:T(128)S(1)} %add_sqrt_fusion.1, bf16[16,1152]{1,0:T(8,128)(2,1)} %param.4, f32[16]{0:T(128)S(1)} %add_sqrt_fusion, bf16[16,1152]{1,0:T(8,128)(2,1)} %param.5), kind=kLoop, calls=%fused_computation.52 | loop fusion | flops 110592 | bytes 147584 | tf_op jit(solution)/shard_map/convert_element_type | solution.py:327
  5.3 41.8 %shard_map.67 = (bf16[32,16,1152]{2,1,0:T(8,128)(2,1)}, bf16[16,16,1152]{2,1,0:T(8,128)(2,1)}) custom-call(bf16[16,1152]{1,0:T(8,128)(2,1)} %get-tuple-element.13.image_src, bf16[16,1152]{1,0:T(8,128)(2,1)} %get-tuple-element.14.text_src), custom_call_target="tpu_custom_call" | custom-call | tf_op jit(solution)/shard_map/pallas_call | solution.py:239
  47.1 0.0 copy-start
  47.1 2.4 %fusion.1 = (f32[512]{0:T(512)S(1)}, f32[512,256]{0,1:T(8,128)S(1)}) fusion(s32[512]{0:T(512)S(1)} %fusion.12, s32[256]{0:T(256)S(1)} %and_select_fusion, pred[512]{0:T(512)(128)(4,1)S(1)} %fusion.16, pred[256]{0:T(512)(128)(4,1)S(1)} %fusion.22, f32[]{:T(128)S(6)} %copy.8, bf16[512,1152]{1,0:T(8,128)(2,1)} %bitcast.18, bf16[256,1152]{1,0:T(8,128)(2,1)} %bitcast.21, ...), kind=kOutput, calls=%fused_computation.4 | convolution fusion | flops 303955456 | bytes 2299656 | tf_op jit(solution)/shard_map/dot_general | solution.py:346
  49.5 0.1 broadcast_in_dim.2
  49.6 0.2 fusion.3
  49.9 0.0 copy-done
  49.9 0.0 copy-start.4
  49.9 1.6 %fusion.26.text_src = f32[16,16,1152]{2,1,0:T(8,128)} fusion(bf16[16,16,512]{2,1,0:T(8,128)(2,1)S(1)} %bitcast.20, bf16[512,1152,1]{1,0,2:T(8,128)(2,1)S(1)} %bitcast.19), kind=kOutput, calls=%fused_computation.54 | convolution fusion | flops 301989888 | bytes 2621440 | tf_op jit(solution)/shard_map/dot_general | solution.py:352
  51.5 0.0 copy-done.4
  51.5 0.7 fusion.4
  52.2 1.7 %pad_maximum_fusion = f32[512,1280]{1,0:T(8,128)} fusion(f32[512,128]{1,0:T(8,128)S(1)} %broadcast_in_dim.2, f32[512,1152]{1,0:T(8,128)S(1)} %fusion.4), kind=kLoop, calls=%fused_computation | loop fusion | flops 655360 | bytes 5242880 | tf_op jit(solution)/shard_map/concatenate | solution.py:353
  53.9 34.8 %shard_map.68 = (f32[16,16,1280]{2,1,0:T(8,128)}, f32[16,1152]{1,0:T(8,128)}) custom-call(f32[2,16,16,1280]{3,2,1,0:T(8,128)} %bitcast.17, f32[16,16,1152]{2,1,0:T(8,128)} %fusion.26.text_src), custom_call_target="tpu_custom_call" | custom-call | tf_op jit(solution)/shard_map/pallas_call | solution.py:215
  88.7 0.0 copy-start.1
  88.7 0.0 copy-start.2
  88.7 0.0 copy-start.3
  88.7 1.4 %reduce_sum.57 = f32[16,1280]{1,0:T(8,128)S(1)} reduce(f32[16,16,1280]{2,1,0:T(8,128)} %get-tuple-element.9, f32[]{:T(128)} %constant.73.clone.1), dimensions={0}, to_apply=%region_3.4 | reduce | flops 307200 | bytes 1392644 | tf_op jit(solution)/shard_map/reduce_sum | solution.py:357
  90.2 0.2 multiply_reduce_fusion.1
  90.3 0.6 slice_reduce_fusion
  91.0 0.7 subtract_divide_fusion.1
  91.7 0.2 multiply_reduce_fusion
  91.9 0.7 subtract_divide_fusion
  (10 shorter events, 0.1 us)
Async XLA Ops:
  47.1 2.8 %copy-start = (bf16[32,16,1152]{2,1,0:T(8,128)(2,1)S(1)}, bf16[32,16,1152]{2,1,0:T(8,128)(2,1)}, u32[]{:S(2)}) copy-start(bf16[32,16,1152]{2,1,0:T(8,128)(2,1)} %get-tuple-element.7) | copy-start | bytes 3538948
  49.9 1.6 %copy-start.4 = (bf16[16,16,1152]{2,1,0:T(8,128)(2,1)S(1)}, bf16[16,16,1152]{2,1,0:T(8,128)(2,1)}, u32[]{:S(2)}) copy-start(bf16[16,16,1152]{2,1,0:T(8,128)(2,1)} %get-tuple-element.8) | copy-start | bytes 1769476
  88.7 1.5 %copy-start.1 = (bf16[16,1152]{1,0:T(8,128)(2,1)S(1)}, bf16[16,1152]{1,0:T(8,128)(2,1)}, u32[]{:S(2)}) copy-start(bf16[16,1152]{1,0:T(8,128)(2,1)} %param.4) | copy-start | bytes 110596
  88.7 3.0 %copy-start.2 = (bf16[16,1152]{1,0:T(8,128)(2,1)S(1)}, bf16[16,1152]{1,0:T(8,128)(2,1)}, u32[]{:S(2)}) copy-start(bf16[16,1152]{1,0:T(8,128)(2,1)} %param.5) | copy-start | bytes 110596
  88.7 3.0 %copy-start.3 = (f32[16,1152]{1,0:T(8,128)S(1)}, f32[16,1152]{1,0:T(8,128)}, u32[]{:S(2)}) copy-start(f32[16,1152]{1,0:T(8,128)} %get-tuple-element.10) | copy-start | bytes 221188

commit v11 on v9

--- a/solution.py
+++ b/solution.py
@@ -93,24 +93,42 @@
 def gather_kernel(image_axes, image_src, text_src, image_out, text_out, image_send, image_recv, text_send, text_recv):
     image_count, image_me = group_size(image_axes), linear_index(image_axes)
     count, me, right, left = ring_peers()
+    right2 = member(TEXT_AXES, (me + 2) % count)
+    left2 = member(TEXT_AXES, (me + count - 2) % count)
+    greet_all(image_axes, pltpu.get_barrier_semaphore(), image_count, image_me, right, left, (right2, left2))
+    finish = image_direct(image_axes, False, image_src, image_out, image_send, image_recv, image_count, image_me)
+    sends = []
+
+    def send(src, origin, device, slot):
+        copy = remote(src, text_out.at[origin], text_send.at[slot], text_recv.at[origin], device)
+        copy.start()
+        sends.append(copy)
+
+    def arrive(origin):
+        remote(text_out.at[origin], text_out.at[origin], text_send.at[0], text_recv.at[origin], right).wait_recv()
+
     half = count // 2
-    greet_all(image_axes, pltpu.get_barrier_semaphore(), image_count, image_me, right, left)
-    finish = image_direct(image_axes, False, image_src, image_out, image_send, image_recv, image_count, image_me)
-    sends = [remote(text_src, text_out.at[me], text_send.at[0], text_recv.at[me], right),
-             remote(text_src, text_out.at[me], text_send.at[half], text_recv.at[me], left)]
-    for copy in sends:
-        copy.start()
+    for slot, device in ((0, right), (1, right2), (half, left), (half + 1, left2)):
+        send(text_src, me, device, slot)
     text_out[me] = text_src[...]
-    for step in range(1, half):
-        for origin, device, slot in (((me + count - step) % count, right, step), ((me + step) % count, left, half + step)):
-            if slot >= count - 1:
+    slot_right, slot_left = 2, half + 2
+    for step in range(2, half // 2 + 1):
+        for distance in (2 * step - 3, 2 * step - 2):
+            origin = (me + count - distance) % count
+            arrive(origin)
+            send(text_out.at[origin], origin, right2, slot_right)
+            slot_right += 1
+        for distance in (2 * step - 3, 2 * step - 2):
+            if distance > half - 3:
                 continue
-            arrived = remote(text_out.at[origin], text_out.at[origin], text_send.at[slot], text_recv.at[origin], device)
-            arrived.wait_recv()
-            arrived.start()
-            sends.append(arrived)
-    for origin in ((me + count - half) % count, (me + half - 1) % count):
-        remote(text_out.at[origin], text_out.at[origin], text_send.at[0], text_recv.at[origin], right).wait_recv()
+            origin = (me + distance) % count
+            arrive(origin)
+            send(text_out.at[origin], origin, left2, slot_left)
+            slot_left += 1
+    for distance in (half - 1, half):
+        arrive((me + count - distance) % count)
+    for distance in (half - 2, half - 1):
+        arrive((me + distance) % count)
     for copy in sends:
         copy.wait_send()
     lax.fori_loop(1, image_count, finish, 0)

time: 94.5 us -> 90.5 us (0.958)
  Pallas kernels: 77.1 us -> 72.6 us
    pallas_call x1, Pallas kernels: 42.2 us -> 36.5 us  [exchange(): pl.pallas_call(functools.partial(reduce_kernel if scatter else gather_ker...]
    pallas_call x1, Pallas kernels: 34.9 us -> 36 us  [merged_reduce(): pl.pallas_call(functools.partial(merged_reduce_kernel, image_axes), out_s...]
where the time goes in v11:
time: 90.5 us; the launch traced here: 88.7 us
  Pallas kernels  72.6 us (80%)
  other arithmetic  8.53 us (9%)
  matrix products  4.72 us (5%)
  between operations  2.06 us (2%)
    pallas_call x1, Pallas kernels, exchange(): pl.pallas_call(functools.partial(reduce_kernel if scatter else gather_ker...  36.5 us
    pallas_call x1, Pallas kernels, merged_reduce(): pl.pallas_call(functools.partial(merged_reduce_kernel, image_axes), out_s...  36 us
    dot_general x1, matrix products, local(): lax.dot_general(gathered, seen, (((1,), (1,)), ((), ())), preferred_eleme...  2.44 us

profile of v11, /device:TPU:24, one launch (start us, length us, event | category | flops | bytes accessed | tf_op | source)
XLA Modules:
  0.0 88.7 jit_solution(4824464752944500605)
XLA Ops:
  2.0 0.9 %fusion.10 = f32[16]{0:T(128)S(1)} fusion(bf16[16,1152]{1,0:T(8,128)(2,1)} %param.4), kind=kLoop, calls=%fused_computation.21 | loop fusion | flops 55280 | bytes 36928 | tf_op jit(solution)/shard_map/reduce_sum | solution.py:20
  2.9 0.9 %fusion.11 = f32[16]{0:T(128)S(1)} fusion(bf16[16,1152]{1,0:T(8,128)(2,1)} %param.5), kind=kLoop, calls=%fused_computation.22 | loop fusion | flops 55280 | bytes 36928 | tf_op jit(solution)/shard_map/reduce_sum | solution.py:20
  3.8 1.5 %fusion.24 = (bf16[16,1152]{1,0:T(8,128)(2,1)}, bf16[16,1152]{1,0:T(8,128)(2,1)}) fusion(f32[16]{0:T(128)S(1)} %add_sqrt_fusion.1, bf16[16,1152]{1,0:T(8,128)(2,1)} %param.4, f32[16]{0:T(128)S(1)} %add_sqrt_fusion, bf16[16,1152]{1,0:T(8,128)(2,1)} %param.5), kind=kLoop, calls=%fused_computation.52 | loop fusion | flops 110592 | bytes 147584 | tf_op jit(solution)/shard_map/convert_element_type | solution.py:332
  5.3 36.5 %shard_map.67 = (bf16[32,16,1152]{2,1,0:T(8,128)(2,1)}, bf16[16,16,1152]{2,1,0:T(8,128)(2,1)}) custom-call(bf16[16,1152]{1,0:T(8,128)(2,1)} %get-tuple-element.13.image_src, bf16[16,1152]{1,0:T(8,128)(2,1)} %get-tuple-element.14.text_src), custom_call_target="tpu_custom_call" | custom-call | tf_op jit(solution)/shard_map/pallas_call | solution.py:244
  41.8 0.0 copy-start
  41.9 2.4 %fusion.1 = (f32[512]{0:T(512)S(1)}, f32[512,256]{0,1:T(8,128)S(1)}) fusion(s32[512]{0:T(512)S(1)} %fusion.12, s32[256]{0:T(256)S(1)} %and_select_fusion, pred[512]{0:T(512)(128)(4,1)S(1)} %fusion.16, pred[256]{0:T(512)(128)(4,1)S(1)} %fusion.22, f32[]{:T(128)S(6)} %copy.8, bf16[512,1152]{1,0:T(8,128)(2,1)} %bitcast.18, bf16[256,1152]{1,0:T(8,128)(2,1)} %bitcast.21, ...), kind=kOutput, calls=%fused_computation.4 | convolution fusion | flops 303955456 | bytes 2299656 | tf_op jit(solution)/shard_map/dot_general | solution.py:351
  44.3 0.1 broadcast_in_dim.2
  44.4 0.2 fusion.3
  44.7 0.0 copy-done
  44.7 0.0 copy-start.4
  44.7 1.6 %fusion.26.text_src = f32[16,16,1152]{2,1,0:T(8,128)} fusion(bf16[16,16,512]{2,1,0:T(8,128)(2,1)S(1)} %bitcast.20, bf16[512,1152,1]{1,0,2:T(8,128)(2,1)S(1)} %bitcast.19), kind=kOutput, calls=%fused_computation.54 | convolution fusion | flops 301989888 | bytes 2621440 | tf_op jit(solution)/shard_map/dot_general | solution.py:357
  46.3 0.0 copy-done.4
  46.3 0.7 fusion.4
  47.0 1.7 %pad_maximum_fusion = f32[512,1280]{1,0:T(8,128)} fusion(f32[512,128]{1,0:T(8,128)S(1)} %broadcast_in_dim.2, f32[512,1152]{1,0:T(8,128)S(1)} %fusion.4), kind=kLoop, calls=%fused_computation | loop fusion | flops 655360 | bytes 5242880 | tf_op jit(solution)/shard_map/concatenate | solution.py:358
  48.7 36.0 %shard_map.68 = (f32[16,16,1280]{2,1,0:T(8,128)}, f32[16,1152]{1,0:T(8,128)}) custom-call(f32[2,16,16,1280]{3,2,1,0:T(8,128)} %bitcast.17, f32[16,16,1152]{2,1,0:T(8,128)} %fusion.26.text_src), custom_call_target="tpu_custom_call" | custom-call | tf_op jit(solution)/shard_map/pallas_call | solution.py:220
  84.7 0.0 copy-start.1
  84.8 0.0 copy-start.2
  84.8 0.0 copy-start.3
  84.8 1.4 %reduce_sum.57 = f32[16,1280]{1,0:T(8,128)S(1)} reduce(f32[16,16,1280]{2,1,0:T(8,128)} %get-tuple-element.9, f32[]{:T(128)} %constant.73.clone.1), dimensions={0}, to_apply=%region_3.4 | reduce | flops 307200 | bytes 1392644 | tf_op jit(solution)/shard_map/reduce_sum | solution.py:362
  86.2 0.2 multiply_reduce_fusion.1
  86.4 0.6 slice_reduce_fusion
  87.0 0.7 subtract_divide_fusion.1
  87.8 0.2 multiply_reduce_fusion
  88.0 0.7 subtract_divide_fusion
  (10 shorter events, 0.1 us)
Async XLA Ops:
  41.8 2.8 %copy-start = (bf16[32,16,1152]{2,1,0:T(8,128)(2,1)S(1)}, bf16[32,16,1152]{2,1,0:T(8,128)(2,1)}, u32[]{:S(2)}) copy-start(bf16[32,16,1152]{2,1,0:T(8,128)(2,1)} %get-tuple-element.7) | copy-start | bytes 3538948
  44.7 1.6 %copy-start.4 = (bf16[16,16,1152]{2,1,0:T(8,128)(2,1)S(1)}, bf16[16,16,1152]{2,1,0:T(8,128)(2,1)}, u32[]{:S(2)}) copy-start(bf16[16,16,1152]{2,1,0:T(8,128)(2,1)} %get-tuple-element.8) | copy-start | bytes 1769476
  84.7 1.5 %copy-start.1 = (bf16[16,1152]{1,0:T(8,128)(2,1)S(1)}, bf16[16,1152]{1,0:T(8,128)(2,1)}, u32[]{:S(2)}) copy-start(bf16[16,1152]{1,0:T(8,128)(2,1)} %param.4) | copy-start | bytes 110596
  84.8 3.0 %copy-start.2 = (bf16[16,1152]{1,0:T(8,128)(2,1)S(1)}, bf16[16,1152]{1,0:T(8,128)(2,1)}, u32[]{:S(2)}) copy-start(bf16[16,1152]{1,0:T(8,128)(2,1)} %param.5) | copy-start | bytes 110596
  84.8 3.0 %copy-start.3 = (f32[16,1152]{1,0:T(8,128)S(1)}, f32[16,1152]{1,0:T(8,128)}, u32[]{:S(2)}) copy-start(f32[16,1152]{1,0:T(8,128)} %get-tuple-element.10) | copy-start | bytes 221188

commit v12 on v11

--- a/solution.py
+++ b/solution.py
@@ -168,33 +168,48 @@
                          text_recv, inbox, outbox, halfbox, summed, half_sems):
     image_count, image_me = group_size(image_axes), linear_index(image_axes)
     count, me, right, left = ring_peers()
-    half = count // 2
+    right2 = member(TEXT_AXES, (me + 2) % count)
+    left2 = member(TEXT_AXES, (me + count - 2) % count)
     core = linear_index(CORE_AXES)
     partner = member(CORE_AXES, 1 - core)
-    greet_all(image_axes, pltpu.get_barrier_semaphore(), image_count, image_me, right, left, (partner,))
-    sends = [remote(text_src.at[(me + half) % count], inbox.at[0], text_send.at[0], text_recv.at[0], right),
-             remote(text_src.at[(me + half + 1) % count], inbox.at[half], text_send.at[half], text_recv.at[half], left)]
-    for copy in sends:
-        copy.start()
+    greet_all(image_axes, pltpu.get_barrier_semaphore(), image_count, image_me, right, left, (right2, left2, partner))
+    chains = (
+        (0, 4, lambda step: right2, lambda step: 10 - 2 * step),
+        (4, 4, lambda step: right2 if step < 4 else right, lambda step: 9 - 2 * step),
+        (8, 3, lambda step: left2, lambda step: 2 * step - 8),
+        (11, 4, lambda step: left2 if step < 4 else left, lambda step: 2 * step - 9),
+    )
+    sends = []
+
+    def step_sends(step):
+        for base, steps, device, offset in chains:
+            if step > steps:
+                continue
+            slot = base + step - 1
+            target = (me + count + offset(step)) % count
+            if step == 1:
+                source = text_src.at[target]
+            else:
+                remote(inbox.at[slot - 1], inbox.at[slot - 1], text_send.at[slot], text_recv.at[slot - 1],
+                       right).wait_recv()
+                outbox[slot] = inbox[slot - 1] + text_src[target]
+                source = outbox.at[slot]
+            copy = remote(source, inbox.at[slot], text_send.at[slot], text_recv.at[slot], device(step))
+            copy.start()
+            sends.append(copy)
+
+    step_sends(1)
     swap = remote(image_src.at[1 - core], halfbox, half_sems.at[0], half_sems.at[1], partner)
     swap.start()
     swap.wait_recv()
     summed[...] = image_src[core] + halfbox[...]
     finish = image_direct(image_axes, True, summed, image_out, image_send, image_recv, image_count, image_me)
-    for step in range(1, half):
-        chains = ((step, (me + half - step) % count, right), (half + step, (me + half + 1 + step) % count, left))
-        for slot, target, device in chains:
-            if slot >= count - 1:
-                continue
-            remote(inbox.at[slot - 1], inbox.at[slot - 1], text_send.at[slot], text_recv.at[slot - 1], device).wait_recv()
-            outbox[slot] = inbox[slot - 1] + text_src[target]
-            copy = remote(outbox.at[slot], inbox.at[slot], text_send.at[slot], text_recv.at[slot], device)
-            copy.start()
-            sends.append(copy)
-    last_right, last_left = half - 1, count - 2
-    for slot in (last_right, last_left):
+    for step in range(2, 5):
+        step_sends(step)
+    finals = (3, 7, 10, 14)
+    for slot in finals:
         remote(inbox.at[slot], inbox.at[slot], text_send.at[0], text_recv.at[slot], right).wait_recv()
-    text_out[...] = text_src[me] + inbox[last_right] + inbox[last_left]
+    text_out[...] = text_src[me] + inbox[finals[0]] + inbox[finals[1]] + inbox[finals[2]] + inbox[finals[3]]
     for copy in sends:
         copy.wait_send()
     swap.wait_send()

time: 90.5 us -> 88.2 us (0.975)
  the two profiles are of different devices: /device:TPU:24 before, /device:TPU:8 now
where the time goes in v12:
time: 88.2 us; the launch traced here: 87.8 us
  Pallas kernels  71.7 us (81%)
  other arithmetic  8.53 us (10%)
  matrix products  4.71 us (5%)
  between operations  2.06 us (2%)
    pallas_call x1, Pallas kernels, exchange(): pl.pallas_call(functools.partial(reduce_kernel if scatter else gather_ker...  36.1 us
    pallas_call x1, Pallas kernels, merged_reduce(): pl.pallas_call(functools.partial(merged_reduce_kernel, image_axes), out_s...  35.6 us
    dot_general x1, matrix products, local(): lax.dot_general(gathered, seen, (((1,), (1,)), ((), ())), preferred_eleme...  2.44 us
    reduce_sum x2, other arithmetic, unit_rows(): norms = jnp.sqrt(jnp.sum(floats * floats, 1, keepdims=True) + 1e-06)  1.79 us

profile of v12, /device:TPU:8, one launch (start us, length us, event | category | flops | bytes accessed | tf_op | source)
XLA Modules:
  0.0 87.8 jit_solution(8035485072030104843)
XLA Ops:
  2.0 0.9 %fusion.10 = f32[16]{0:T(128)S(1)} fusion(bf16[16,1152]{1,0:T(8,128)(2,1)} %param.4), kind=kLoop, calls=%fused_computation.21 | loop fusion | flops 55280 | bytes 36928 | tf_op jit(solution)/shard_map/reduce_sum | solution.py:20
  2.9 0.9 %fusion.11 = f32[16]{0:T(128)S(1)} fusion(bf16[16,1152]{1,0:T(8,128)(2,1)} %param.5), kind=kLoop, calls=%fused_computation.22 | loop fusion | flops 55280 | bytes 36928 | tf_op jit(solution)/shard_map/reduce_sum | solution.py:20
  3.8 1.5 %fusion.24 = (bf16[16,1152]{1,0:T(8,128)(2,1)}, bf16[16,1152]{1,0:T(8,128)(2,1)}) fusion(f32[16]{0:T(128)S(1)} %add_sqrt_fusion.1, bf16[16,1152]{1,0:T(8,128)(2,1)} %param.4, f32[16]{0:T(128)S(1)} %add_sqrt_fusion, bf16[16,1152]{1,0:T(8,128)(2,1)} %param.5), kind=kLoop, calls=%fused_computation.52 | loop fusion | flops 110592 | bytes 147584 | tf_op jit(solution)/shard_map/convert_element_type | solution.py:347
  5.3 36.1 %shard_map.67 = (bf16[32,16,1152]{2,1,0:T(8,128)(2,1)}, bf16[16,16,1152]{2,1,0:T(8,128)(2,1)}) custom-call(bf16[16,1152]{1,0:T(8,128)(2,1)} %get-tuple-element.13.image_src, bf16[16,1152]{1,0:T(8,128)(2,1)} %get-tuple-element.14.text_src), custom_call_target="tpu_custom_call" | custom-call | tf_op jit(solution)/shard_map/pallas_call | solution.py:259
  41.3 0.0 copy-start
  41.4 2.4 %fusion.1 = (f32[512]{0:T(512)S(1)}, f32[512,256]{0,1:T(8,128)S(1)}) fusion(s32[512]{0:T(512)S(1)} %fusion.12, s32[256]{0:T(256)S(1)} %and_select_fusion, pred[512]{0:T(512)(128)(4,1)S(1)} %fusion.16, pred[256]{0:T(512)(128)(4,1)S(1)} %fusion.22, f32[]{:T(128)S(6)} %copy.8, bf16[512,1152]{1,0:T(8,128)(2,1)} %bitcast.18, bf16[256,1152]{1,0:T(8,128)(2,1)} %bitcast.21, ...), kind=kOutput, calls=%fused_computation.4 | convolution fusion | flops 303955456 | bytes 2299656 | tf_op jit(solution)/shard_map/dot_general | solution.py:366
  43.8 0.1 broadcast_in_dim.2
  43.9 0.2 fusion.3
  44.2 0.0 copy-done
  44.2 0.0 copy-start.4
  44.2 1.6 %fusion.26.text_src = f32[16,16,1152]{2,1,0:T(8,128)} fusion(bf16[16,16,512]{2,1,0:T(8,128)(2,1)S(1)} %bitcast.20, bf16[512,1152,1]{1,0,2:T(8,128)(2,1)S(1)} %bitcast.19), kind=kOutput, calls=%fused_computation.54 | convolution fusion | flops 301989888 | bytes 2621440 | tf_op jit(solution)/shard_map/dot_general | solution.py:372
  45.8 0.0 copy-done.4
  45.8 0.7 fusion.4
  46.5 1.7 %pad_maximum_fusion = f32[512,1280]{1,0:T(8,128)} fusion(f32[512,128]{1,0:T(8,128)S(1)} %broadcast_in_dim.2, f32[512,1152]{1,0:T(8,128)S(1)} %fusion.4), kind=kLoop, calls=%fused_computation | loop fusion | flops 655360 | bytes 5242880 | tf_op jit(solution)/shard_map/concatenate | solution.py:373
  48.2 35.6 %shard_map.68 = (f32[16,16,1280]{2,1,0:T(8,128)}, f32[16,1152]{1,0:T(8,128)}) custom-call(f32[2,16,16,1280]{3,2,1,0:T(8,128)} %bitcast.17, f32[16,16,1152]{2,1,0:T(8,128)} %fusion.26.text_src), custom_call_target="tpu_custom_call" | custom-call | tf_op jit(solution)/shard_map/pallas_call | solution.py:235
  83.8 0.0 copy-start.1
  83.8 0.0 copy-start.2
  83.8 0.0 copy-start.3
  83.9 1.4 %reduce_sum.57 = f32[16,1280]{1,0:T(8,128)S(1)} reduce(f32[16,16,1280]{2,1,0:T(8,128)} %get-tuple-element.9, f32[]{:T(128)} %constant.73.clone.1), dimensions={0}, to_apply=%region_3.4 | reduce | flops 307200 | bytes 1392644 | tf_op jit(solution)/shard_map/reduce_sum | solution.py:377
  85.3 0.2 multiply_reduce_fusion.1
  85.5 0.6 slice_reduce_fusion
  86.1 0.7 subtract_divide_fusion.1
  86.8 0.2 multiply_reduce_fusion
  87.0 0.7 subtract_divide_fusion
  (10 shorter events, 0.1 us)
Async XLA Ops:
  41.3 2.8 %copy-start = (bf16[32,16,1152]{2,1,0:T(8,128)(2,1)S(1)}, bf16[32,16,1152]{2,1,0:T(8,128)(2,1)}, u32[]{:S(2)}) copy-start(bf16[32,16,1152]{2,1,0:T(8,128)(2,1)} %get-tuple-element.7) | copy-start | bytes 3538948
  44.2 1.6 %copy-start.4 = (bf16[16,16,1152]{2,1,0:T(8,128)(2,1)S(1)}, bf16[16,16,1152]{2,1,0:T(8,128)(2,1)}, u32[]{:S(2)}) copy-start(bf16[16,16,1152]{2,1,0:T(8,128)(2,1)} %get-tuple-element.8) | copy-start | bytes 1769476
  83.8 1.5 %copy-start.1 = (bf16[16,1152]{1,0:T(8,128)(2,1)S(1)}, bf16[16,1152]{1,0:T(8,128)(2,1)}, u32[]{:S(2)}) copy-start(bf16[16,1152]{1,0:T(8,128)(2,1)} %param.4) | copy-start | bytes 110596
  83.8 3.0 %copy-start.2 = (bf16[16,1152]{1,0:T(8,128)(2,1)S(1)}, bf16[16,1152]{1,0:T(8,128)(2,1)}, u32[]{:S(2)}) copy-start(bf16[16,1152]{1,0:T(8,128)(2,1)} %param.5) | copy-start | bytes 110596
  83.8 3.0 %copy-start.3 = (f32[16,1152]{1,0:T(8,128)S(1)}, f32[16,1152]{1,0:T(8,128)}, u32[]{:S(2)}) copy-start(f32[16,1152]{1,0:T(8,128)} %get-tuple-element.10) | copy-start | bytes 221188

commit v13 on v12

--- a/solution.py
+++ b/solution.py
@@ -198,13 +198,14 @@
             copy.start()
             sends.append(copy)
 
-    step_sends(1)
     swap = remote(image_src.at[1 - core], halfbox, half_sems.at[0], half_sems.at[1], partner)
     swap.start()
+    step_sends(1)
+    step_sends(2)
     swap.wait_recv()
     summed[...] = image_src[core] + halfbox[...]
     finish = image_direct(image_axes, True, summed, image_out, image_send, image_recv, image_count, image_me)
-    for step in range(2, 5):
+    for step in range(3, 5):
         step_sends(step)
     finals = (3, 7, 10, 14)
     for slot in finals:

time: 88.2 us -> 87.4 us (level)
  the two profiles are of different devices: /device:TPU:8 before, /device:TPU:24 now
where the time goes in v13:
time: 87.4 us; the launch traced here: 86.8 us
  Pallas kernels  70.7 us (81%)
  other arithmetic  8.53 us (10%)
  matrix products  4.72 us (5%)
  between operations  2.06 us (2%)
    pallas_call x1, Pallas kernels, exchange(): pl.pallas_call(functools.partial(reduce_kernel if scatter else gather_ker...  36.5 us
    pallas_call x1, Pallas kernels, merged_reduce(): pl.pallas_call(functools.partial(merged_reduce_kernel, image_axes), out_s...  34.1 us
    dot_general x1, matrix products, local(): lax.dot_general(gathered, seen, (((1,), (1,)), ((), ())), preferred_eleme...  2.44 us
    reduce_sum x2, other arithmetic, unit_rows(): norms = jnp.sqrt(jnp.sum(floats * floats, 1, keepdims=True) + 1e-06)  1.79 us

profile of v13, /device:TPU:24, one launch (start us, length us, event | category | flops | bytes accessed | tf_op | source)
XLA Modules:
  0.0 86.8 jit_solution(7431369373719239255)
XLA Ops:
  2.0 0.9 %fusion.10 = f32[16]{0:T(128)S(1)} fusion(bf16[16,1152]{1,0:T(8,128)(2,1)} %param.4), kind=kLoop, calls=%fused_computation.21 | loop fusion | flops 55280 | bytes 36928 | tf_op jit(solution)/shard_map/reduce_sum | solution.py:20
  2.9 0.9 %fusion.11 = f32[16]{0:T(128)S(1)} fusion(bf16[16,1152]{1,0:T(8,128)(2,1)} %param.5), kind=kLoop, calls=%fused_computation.22 | loop fusion | flops 55280 | bytes 36928 | tf_op jit(solution)/shard_map/reduce_sum | solution.py:20
  3.8 1.5 %fusion.24 = (bf16[16,1152]{1,0:T(8,128)(2,1)}, bf16[16,1152]{1,0:T(8,128)(2,1)}) fusion(f32[16]{0:T(128)S(1)} %add_sqrt_fusion.1, bf16[16,1152]{1,0:T(8,128)(2,1)} %param.4, f32[16]{0:T(128)S(1)} %add_sqrt_fusion, bf16[16,1152]{1,0:T(8,128)(2,1)} %param.5), kind=kLoop, calls=%fused_computation.52 | loop fusion | flops 110592 | bytes 147584 | tf_op jit(solution)/shard_map/convert_element_type | solution.py:348
  5.3 36.5 %shard_map.67 = (bf16[32,16,1152]{2,1,0:T(8,128)(2,1)}, bf16[16,16,1152]{2,1,0:T(8,128)(2,1)}) custom-call(bf16[16,1152]{1,0:T(8,128)(2,1)} %get-tuple-element.13.image_src, bf16[16,1152]{1,0:T(8,128)(2,1)} %get-tuple-element.14.text_src), custom_call_target="tpu_custom_call" | custom-call | tf_op jit(solution)/shard_map/pallas_call | solution.py:260
  41.8 0.0 copy-start
  41.9 2.4 %fusion.1 = (f32[512]{0:T(512)S(1)}, f32[512,256]{0,1:T(8,128)S(1)}) fusion(s32[512]{0:T(512)S(1)} %fusion.12, s32[256]{0:T(256)S(1)} %and_select_fusion, pred[512]{0:T(512)(128)(4,1)S(1)} %fusion.16, pred[256]{0:T(512)(128)(4,1)S(1)} %fusion.22, f32[]{:T(128)S(6)} %copy.8, bf16[512,1152]{1,0:T(8,128)(2,1)} %bitcast.18, bf16[256,1152]{1,0:T(8,128)(2,1)} %bitcast.21, ...), kind=kOutput, calls=%fused_computation.4 | convolution fusion | flops 303955456 | bytes 2299656 | tf_op jit(solution)/shard_map/dot_general | solution.py:367
  44.3 0.1 broadcast_in_dim.2
  44.4 0.2 fusion.3
  44.7 0.0 copy-done
  44.7 0.0 copy-start.4
  44.7 1.6 %fusion.26.text_src = f32[16,16,1152]{2,1,0:T(8,128)} fusion(bf16[16,16,512]{2,1,0:T(8,128)(2,1)S(1)} %bitcast.20, bf16[512,1152,1]{1,0,2:T(8,128)(2,1)S(1)} %bitcast.19), kind=kOutput, calls=%fused_computation.54 | convolution fusion | flops 301989888 | bytes 2621440 | tf_op jit(solution)/shard_map/dot_general | solution.py:373
  46.3 0.0 copy-done.4
  46.3 0.7 fusion.4
  47.0 1.7 %pad_maximum_fusion = f32[512,1280]{1,0:T(8,128)} fusion(f32[512,128]{1,0:T(8,128)S(1)} %broadcast_in_dim.2, f32[512,1152]{1,0:T(8,128)S(1)} %fusion.4), kind=kLoop, calls=%fused_computation | loop fusion | flops 655360 | bytes 5242880 | tf_op jit(solution)/shard_map/concatenate | solution.py:374
  48.7 34.1 %shard_map.68 = (f32[16,16,1280]{2,1,0:T(8,128)}, f32[16,1152]{1,0:T(8,128)}) custom-call(f32[2,16,16,1280]{3,2,1,0:T(8,128)} %bitcast.17, f32[16,16,1152]{2,1,0:T(8,128)} %fusion.26.text_src), custom_call_target="tpu_custom_call" | custom-call | tf_op jit(solution)/shard_map/pallas_call | solution.py:236
  82.8 0.0 copy-start.1
  82.9 0.0 copy-start.2
  82.9 1.4 %reduce_sum.57 = f32[16,1280]{1,0:T(8,128)S(1)} reduce(f32[16,16,1280]{2,1,0:T(8,128)} %get-tuple-element.9, f32[]{:T(128)} %constant.73.clone.1), dimensions={0}, to_apply=%region_3.4 | reduce | flops 307200 | bytes 1392644 | tf_op jit(solution)/shard_map/reduce_sum | solution.py:378
  84.3 0.0 copy-done.1
  84.3 0.2 multiply_reduce_fusion.1
  84.5 0.6 slice_reduce_fusion
  85.1 0.7 subtract_divide_fusion.1
  85.9 0.2 multiply_reduce_fusion
  86.1 0.7 subtract_divide_fusion
  (10 shorter events, 0.1 us)
Async XLA Ops:
  41.8 2.8 %copy-start = (bf16[32,16,1152]{2,1,0:T(8,128)(2,1)S(1)}, bf16[32,16,1152]{2,1,0:T(8,128)(2,1)}, u32[]{:S(2)}) copy-start(bf16[32,16,1152]{2,1,0:T(8,128)(2,1)} %get-tuple-element.7) | copy-start | bytes 3538948
  44.7 1.6 %copy-start.4 = (bf16[16,16,1152]{2,1,0:T(8,128)(2,1)S(1)}, bf16[16,16,1152]{2,1,0:T(8,128)(2,1)}, u32[]{:S(2)}) copy-start(bf16[16,16,1152]{2,1,0:T(8,128)(2,1)} %get-tuple-element.8) | copy-start | bytes 1769476
  82.8 1.5 %copy-start.1 = (bf16[16,1152]{1,0:T(8,128)(2,1)S(1)}, bf16[16,1152]{1,0:T(8,128)(2,1)}, u32[]{:S(2)}) copy-start(bf16[16,1152]{1,0:T(8,128)(2,1)} %param.4) | copy-start | bytes 110596
  82.9 3.0 %copy-start.2 = (bf16[16,1152]{1,0:T(8,128)(2,1)S(1)}, bf16[16,1152]{1,0:T(8,128)(2,1)}, u32[]{:S(2)}) copy-start(bf16[16,1152]{1,0:T(8,128)(2,1)} %param.5) | copy-start | bytes 110596
  82.9 3.0 %copy-start.3 = (f32[16,1152]{1,0:T(8,128)S(1)}, f32[16,1152]{1,0:T(8,128)}, u32[]{:S(2)}) copy-start(f32[16,1152]{1,0:T(8,128)} %get-tuple-element.10) | copy-start | bytes 221188

commit v14 on v13

--- a/solution.py
+++ b/solution.py
@@ -93,9 +93,11 @@
 def gather_kernel(image_axes, image_src, text_src, image_out, text_out, image_send, image_recv, text_send, text_recv):
     image_count, image_me = group_size(image_axes), linear_index(image_axes)
     count, me, right, left = ring_peers()
-    right2 = member(TEXT_AXES, (me + 2) % count)
-    left2 = member(TEXT_AXES, (me + count - 2) % count)
-    greet_all(image_axes, pltpu.get_barrier_semaphore(), image_count, image_me, right, left, (right2, left2))
+    half = count // 2
+    reach = half // 2
+    near = [(member(TEXT_AXES, (me + d) % count), member(TEXT_AXES, (me + count - d) % count)) for d in range(1, reach + 1)]
+    extra = tuple(device for pair in near[1:] for device in pair)
+    greet_all(image_axes, pltpu.get_barrier_semaphore(), image_count, image_me, right, left, extra)
     finish = image_direct(image_axes, False, image_src, image_out, image_send, image_recv, image_count, image_me)
     sends = []
 
@@ -107,28 +109,24 @@
     def arrive(origin):
         remote(text_out.at[origin], text_out.at[origin], text_send.at[0], text_recv.at[origin], right).wait_recv()
 
-    half = count // 2
-    for slot, device in ((0, right), (1, right2), (half, left), (half + 1, left2)):
-        send(text_src, me, device, slot)
+    for d in range(1, reach + 1):
+        send(text_src, me, near[d - 1][0], d - 1)
+        send(text_src, me, near[d - 1][1], half + d - 1)
     text_out[me] = text_src[...]
-    slot_right, slot_left = 2, half + 2
-    for step in range(2, half // 2 + 1):
-        for distance in (2 * step - 3, 2 * step - 2):
-            origin = (me + count - distance) % count
-            arrive(origin)
-            send(text_out.at[origin], origin, right2, slot_right)
-            slot_right += 1
-        for distance in (2 * step - 3, 2 * step - 2):
-            if distance > half - 3:
-                continue
-            origin = (me + distance) % count
-            arrive(origin)
-            send(text_out.at[origin], origin, left2, slot_left)
-            slot_left += 1
-    for distance in (half - 1, half):
-        arrive((me + count - distance) % count)
-    for distance in (half - 2, half - 1):
-        arrive((me + distance) % count)
+    far_right, far_left = near[reach - 1]
+    for d in range(1, reach + 1):
+        origin = (me + count - d) % count
+        arrive(origin)
+        send(text_out.at[origin], origin, far_right, reach + d - 1)
+    for d in range(1, reach):
+        origin = (me + d) % count
+        arrive(origin)
+        send(text_out.at[origin], origin, far_left, half + reach + d - 1)
+    arrive((me + reach) % count)
+    for d in range(reach + 1, half + 1):
+        arrive((me + count - d) % count)
+    for d in range(reach + 1, half):
+        arrive((me + d) % count)
     for copy in sends:
         copy.wait_send()
     lax.fori_loop(1, image_count, finish, 0)

time: 87.4 us -> 95 us (1.087)
  Pallas kernels: 70.7 us -> 78.4 us
    pallas_call x1, Pallas kernels: 36.5 us -> 40.7 us  [exchange(): pl.pallas_call(functools.partial(reduce_kernel if scatter else gather_ker...]
    pallas_call x1, Pallas kernels: 34.1 us -> 37.7 us  [merged_reduce(): pl.pallas_call(functools.partial(merged_reduce_kernel, image_axes), out_s...]
where the time goes in v14:
time: 95 us; the launch traced here: 94.5 us
  Pallas kernels  78.4 us (83%)
  other arithmetic  8.53 us (9%)
  matrix products  4.72 us (5%)
  between operations  2.06 us (2%)
    pallas_call x1, Pallas kernels, exchange(): pl.pallas_call(functools.partial(reduce_kernel if scatter else gather_ker...  40.7 us
    pallas_call x1, Pallas kernels, merged_reduce(): pl.pallas_call(functools.partial(merged_reduce_kernel, image_axes), out_s...  37.7 us
    dot_general x1, matrix products, local(): lax.dot_general(gathered, seen, (((1,), (1,)), ((), ())), preferred_eleme...  2.44 us

profile of v14, /device:TPU:24, one launch (start us, length us, event | category | flops | bytes accessed | tf_op | source)
XLA Modules:
  0.0 94.5 jit_solution(11804685259644280814)
XLA Ops:
  2.0 0.9 fusion.10
  2.9 0.9 fusion.11
  3.8 1.5 %fusion.24 = (bf16[16,1152]{1,0:T(8,128)(2,1)}, bf16[16,1152]{1,0:T(8,128)(2,1)}) fusion(f32[16]{0:T(128)S(1)} %add_sqrt_fusion.1, bf16[16,1152]{1,0:T(8,128)(2,1)} %param.4, f32[16]{0:T(128)S(1)} %add_sqrt_fusion, bf16[16,1152]{1,0:T(8,128)(2,1)} %param.5), kind=kLoop, calls=%fused_computation.52 | loop fusion | flops 110592 | bytes 147584 | tf_op jit(solution)/shard_map/convert_element_type | solution.py:346
  5.3 40.7 %shard_map.67 = (bf16[32,16,1152]{2,1,0:T(8,128)(2,1)}, bf16[16,16,1152]{2,1,0:T(8,128)(2,1)}) custom-call(bf16[16,1152]{1,0:T(8,128)(2,1)} %get-tuple-element.13.image_src, bf16[16,1152]{1,0:T(8,128)(2,1)} %get-tuple-element.14.text_src), custom_call_target="tpu_custom_call" | custom-call | tf_op jit(solution)/shard_map/pallas_call | solution.py:258
  46.0 0.0 copy-start
  46.0 2.4 %fusion.1 = (f32[512]{0:T(512)S(1)}, f32[512,256]{0,1:T(8,128)S(1)}) fusion(s32[512]{0:T(512)S(1)} %fusion.12, s32[256]{0:T(256)S(1)} %and_select_fusion, pred[512]{0:T(512)(128)(4,1)S(1)} %fusion.16, pred[256]{0:T(512)(128)(4,1)S(1)} %fusion.22, f32[]{:T(128)S(6)} %copy.8, bf16[512,1152]{1,0:T(8,128)(2,1)} %bitcast.18, bf16[256,1152]{1,0:T(8,128)(2,1)} %bitcast.21, ...), kind=kOutput, calls=%fused_computation.4 | convolution fusion | flops 303955456 | bytes 2299656 | tf_op jit(solution)/shard_map/dot_general | solution.py:365
  48.5 0.1 broadcast_in_dim.2
  48.6 0.2 fusion.3
  48.8 0.0 copy-done
  48.9 0.0 copy-start.4
  48.9 1.6 %fusion.26.text_src = f32[16,16,1152]{2,1,0:T(8,128)} fusion(bf16[16,16,512]{2,1,0:T(8,128)(2,1)S(1)} %bitcast.20, bf16[512,1152,1]{1,0,2:T(8,128)(2,1)S(1)} %bitcast.19), kind=kOutput, calls=%fused_computation.54 | convolution fusion | flops 301989888 | bytes 2621440 | tf_op jit(solution)/shard_map/dot_general | solution.py:371
  50.4 0.0 copy-done.4
  50.4 0.7 fusion.4
  51.2 1.7 %pad_maximum_fusion = f32[512,1280]{1,0:T(8,128)} fusion(f32[512,128]{1,0:T(8,128)S(1)} %broadcast_in_dim.2, f32[512,1152]{1,0:T(8,128)S(1)} %fusion.4), kind=kLoop, calls=%fused_computation | loop fusion | flops 655360 | bytes 5242880 | tf_op jit(solution)/shard_map/concatenate | solution.py:372
  52.9 37.7 %shard_map.68 = (f32[16,16,1280]{2,1,0:T(8,128)}, f32[16,1152]{1,0:T(8,128)}) custom-call(f32[2,16,16,1280]{3,2,1,0:T(8,128)} %bitcast.17, f32[16,16,1152]{2,1,0:T(8,128)} %fusion.26.text_src), custom_call_target="tpu_custom_call" | custom-call | tf_op jit(solution)/shard_map/pallas_call | solution.py:234
  90.6 0.0 copy-start.1
  90.6 0.0 copy-start.2
  90.6 0.0 copy-start.3
  90.6 1.4 %reduce_sum.57 = f32[16,1280]{1,0:T(8,128)S(1)} reduce(f32[16,16,1280]{2,1,0:T(8,128)} %get-tuple-element.9, f32[]{:T(128)} %constant.73.clone.1), dimensions={0}, to_apply=%region_3.4 | reduce | flops 307200 | bytes 1392644 | tf_op jit(solution)/shard_map/reduce_sum | solution.py:376
  92.1 0.2 multiply_reduce_fusion.1
  92.3 0.6 slice_reduce_fusion
  92.9 0.7 subtract_divide_fusion.1
  93.6 0.2 multiply_reduce_fusion
  93.8 0.7 subtract_divide_fusion
  (10 shorter events, 0.1 us)
Async XLA Ops:
  46.0 2.9 %copy-start = (bf16[32,16,1152]{2,1,0:T(8,128)(2,1)S(1)}, bf16[32,16,1152]{2,1,0:T(8,128)(2,1)}, u32[]{:S(2)}) copy-start(bf16[32,16,1152]{2,1,0:T(8,128)(2,1)} %get-tuple-element.7) | copy-start | bytes 3538948
  48.9 1.6 %copy-start.4 = (bf16[16,16,1152]{2,1,0:T(8,128)(2,1)S(1)}, bf16[16,16,1152]{2,1,0:T(8,128)(2,1)}, u32[]{:S(2)}) copy-start(bf16[16,16,1152]{2,1,0:T(8,128)(2,1)} %get-tuple-element.8) | copy-start | bytes 1769476
  90.6 1.5 %copy-start.1 = (bf16[16,1152]{1,0:T(8,128)(2,1)S(1)}, bf16[16,1152]{1,0:T(8,128)(2,1)}, u32[]{:S(2)}) copy-start(bf16[16,1152]{1,0:T(8,128)(2,1)} %param.4) | copy-start | bytes 110596
  90.6 3.0 %copy-start.2 = (bf16[16,1152]{1,0:T(8,128)(2,1)S(1)}, bf16[16,1152]{1,0:T(8,128)(2,1)}, u32[]{:S(2)}) copy-start(bf16[16,1152]{1,0:T(8,128)(2,1)} %param.5) | copy-start | bytes 110596
  90.6 3.0 %copy-start.3 = (f32[16,1152]{1,0:T(8,128)S(1)}, f32[16,1152]{1,0:T(8,128)}, u32[]{:S(2)}) copy-start(f32[16,1152]{1,0:T(8,128)} %get-tuple-element.10) | copy-start | bytes 221188

commit v15 on v13

--- a/solution.py
+++ b/solution.py
@@ -164,8 +164,9 @@
     lax.fori_loop(1, image_count, finish, 0)
 
 
-def merged_reduce_kernel(image_axes, image_src, text_src, image_out, text_out, image_send, image_recv, text_send,
-                         text_recv, inbox, outbox, halfbox, summed, half_sems):
+def merged_reduce_kernel(image_axes, image_src, text_src, image_unit, image_norm, text_unit, text_norm, loss_out,
+                         image_grad, text_grad, image_send, image_recv, text_send, text_recv, inbox, outbox, halfbox,
+                         summed, half_sems, image_out):
     image_count, image_me = group_size(image_axes), linear_index(image_axes)
     count, me, right, left = ring_peers()
     right2 = member(TEXT_AXES, (me + 2) % count)
@@ -210,17 +211,23 @@
     finals = (3, 7, 10, 14)
     for slot in finals:
         remote(inbox.at[slot], inbox.at[slot], text_send.at[0], text_recv.at[slot], right).wait_recv()
-    text_out[...] = text_src[me] + inbox[finals[0]] + inbox[finals[1]] + inbox[finals[2]] + inbox[finals[3]]
+    text_sum = text_src[me] + inbox[finals[0]] + inbox[finals[1]] + inbox[finals[2]] + inbox[finals[3]]
+    text_grad[...] = back_rows(text_sum, text_unit[...], text_norm[...])
     for copy in sends:
         copy.wait_send()
     swap.wait_send()
     lax.fori_loop(1, image_count, finish, 0)
-
-
-def merged_reduce(image_axes, image_src, text_src, tag):
+    width = image_grad.shape[1]
+    image_sum = jnp.sum(image_out[...], 0)
+    image_grad[...] = back_rows(image_sum[:, :width], image_unit[...], image_norm[...])
+    loss_out[...] = image_sum[:, width:]
+
+
+def merged_reduce(image_axes, image_src, text_src, units, tag):
     image_count, text_count = group_size(image_axes), group_size(TEXT_AXES)
     image_shape = image_src.shape[1:]
     block = text_src.shape[1:]
+    rows, lanes = image_shape[1:]
     vmem = pl.BlockSpec(memory_space=pltpu.VMEM)
     scratch = [
         pltpu.SemaphoreType.DMA((image_count,)),
@@ -232,15 +239,20 @@
         pltpu.VMEM(image_shape, image_src.dtype),
         pltpu.VMEM(image_shape, image_src.dtype),
         pltpu.SemaphoreType.DMA((2,)),
+        pltpu.VMEM(image_shape, image_src.dtype),
     ]
     return pl.pallas_call(
         functools.partial(merged_reduce_kernel, image_axes),
-        out_shape=(jax.ShapeDtypeStruct(image_shape, image_src.dtype), jax.ShapeDtypeStruct(block, text_src.dtype)),
-        in_specs=[vmem, vmem],
-        out_specs=(vmem, vmem),
+        out_shape=(
+            jax.ShapeDtypeStruct((rows, lanes - block[1]), jnp.float32),
+            jax.ShapeDtypeStruct(block, jnp.float32),
+            jax.ShapeDtypeStruct(block, jnp.float32),
+        ),
+        in_specs=[vmem] * 6,
+        out_specs=(vmem, vmem, vmem),
         scratch_shapes=scratch,
         compiler_params=pltpu.CompilerParams(collective_id=tag, has_side_effects=True),
-    )(image_src, text_src)
+    )(image_src, text_src, *units)
 
 
 def exchange(image_axes, image_src, text_src, scatter, tag):
@@ -372,14 +384,11 @@
     image_part = jnp.dot(coef, seen, preferred_element_type=jnp.float32)
     text_part = lax.dot_general(coef, gathered, (((0,), (0,)), ((), ())), preferred_element_type=jnp.float32)
     image_part = jnp.concatenate([image_part, jnp.broadcast_to(loss, (image_count * rows, LOSS_LANES))], 1)
-    image_in, text_in = merged_reduce(
-        CHIP_AXES, image_part.reshape(cores, chips, rows, width + LOSS_LANES), text_part.reshape(text_count, rows, width), 3
+    loss_lanes, image_grad, text_grad = merged_reduce(
+        CHIP_AXES, image_part.reshape(cores, chips, rows, width + LOSS_LANES), text_part.reshape(text_count, rows, width),
+        (image_unit, image_norm, text_unit, text_norm), 3
     )
-    image_in = jnp.sum(image_in, 0)
-    text_sum = text_in
-    image_grad = back_rows(image_in[:, :width], image_unit, image_norm)
-    text_grad = back_rows(text_sum, text_unit, text_norm)
-    return (image_in[:, width], image_grad, text_grad)
+    return (loss_lanes[:, 0], image_grad, text_grad)
 
 
 def solution(mesh):

time: 87.4 us -> 89.4 us (1.023)
  local copies, waits for them, and re-layouts: 0.78 us -> 5.85 us
  other arithmetic: 8.53 us -> 5.31 us
    unnamed x10 -> x6, local copies, waits for them, and re-layouts: 0.03 us -> 3.05 us
    reduce_sum x3 -> x0, other arithmetic: 1.81 us -> none  [the longest x1 1.42 us: local(): image_in = jnp.sum(image_in, 0)]
    convert_element_type x1 -> x0, other arithmetic: 1.5 us -> none  [local(): image_emb = image_unit.astype(jnp.bfloat16)]
    sqrt x0 -> x2, local copies, waits for them, and re-layouts: none -> 1.35 us  [unit_rows(): norms = jnp.sqrt(jnp.sum(floats * floats, 1, keepdims=True) + 1e-06)]
where the time goes in v15:
time: 89.4 us; the launch traced here: 88.6 us
  Pallas kernels  70.7 us (79%)
  local copies, waits for them, and re-layouts  5.85 us (7%)
  other arithmetic  5.31 us (6%)
  matrix products  4.71 us (5%)
  between operations  2.04 us (2%)
    pallas_call x1, Pallas kernels, exchange(): pl.pallas_call(functools.partial(reduce_kernel if scatter else gather_ker...  36.5 us
    pallas_call x1, Pallas kernels, merged_reduce(): pl.pallas_call(functools.partial(merged_reduce_kernel, image_axes), out_s...  34.2 us
    unnamed x6, local copies, waits for them, and re-layouts  3.05 us
    dot_general x1, matrix products, local(): lax.dot_general(gathered, seen, (((1,), (1,)), ((), ())), preferred_eleme...  2.44 us

profile of v15, /device:TPU:24, one launch (start us, length us, event | category | flops | bytes accessed | tf_op | source)
XLA Modules:
  0.0 88.6 jit_solution(3910880788411532424)
XLA Ops:
  2.0 0.9 %fusion.10 = f32[16]{0:T(128)S(1)} fusion(bf16[16,1152]{1,0:T(8,128)(2,1)} %param.4), kind=kLoop, calls=%fused_computation.21 | loop fusion | flops 55280 | bytes 36928 | tf_op jit(solution)/shard_map/reduce_sum | solution.py:20
  2.8 0.9 %fusion.11 = f32[16]{0:T(128)S(1)} fusion(bf16[16,1152]{1,0:T(8,128)(2,1)} %param.5), kind=kLoop, calls=%fused_computation.22 | loop fusion | flops 55280 | bytes 36928 | tf_op jit(solution)/shard_map/reduce_sum | solution.py:20
  3.8 0.7 copy.9.image_norm
  4.5 0.7 copy.10.text_norm
  5.1 1.5 %convert_divide_fusion = (f32[16,1152]{1,0:T(8,128)}, bf16[16,1152]{1,0:T(8,128)(2,1)}, bf16[16,1152]{1,0:T(8,128)(2,1)}, f32[16,1152]{1,0:T(8,128)}) fusion(bf16[16,1152]{1,0:T(8,128)(2,1)} %param.5, f32[16]{0:T(128)S(1)} %get-tuple-element.18, f32[16]{0:T(128)S(1)} %get-tuple-element.20, bf16[16,1152]{1,0:T(8,128)(2,1)} %param.4), kind=kLoop, calls=%fused_computation.17 | loop fusion | flops 110592 | bytes 295040 | tf_op jit(solution)/shard_map/div | solution.py:21
  6.7 36.5 %shard_map.67 = (bf16[32,16,1152]{2,1,0:T(8,128)(2,1)}, bf16[16,16,1152]{2,1,0:T(8,128)(2,1)}) custom-call(bf16[16,1152]{1,0:T(8,128)(2,1)} %get-tuple-element.23.image_src, bf16[16,1152]{1,0:T(8,128)(2,1)} %get-tuple-element.14.text_src), custom_call_target="tpu_custom_call" | custom-call | tf_op jit(solution)/shard_map/pallas_call | solution.py:272
  43.2 0.0 copy-start
  43.2 2.4 %fusion.1 = (f32[512]{0:T(512)S(1)}, f32[512,256]{0,1:T(8,128)S(1)}) fusion(s32[512]{0:T(512)S(1)} %fusion.12, s32[256]{0:T(256)S(1)} %and_select_fusion, pred[512]{0:T(512)(128)(4,1)S(1)} %fusion.16, pred[256]{0:T(512)(128)(4,1)S(1)} %fusion.22, f32[]{:T(128)S(6)} %copy.14, bf16[512,1152]{1,0:T(8,128)(2,1)} %bitcast.22, bf16[256,1152]{1,0:T(8,128)(2,1)} %bitcast.25, ...), kind=kOutput, calls=%fused_computation.4 | convolution fusion | flops 303955456 | bytes 2299656 | tf_op jit(solution)/shard_map/dot_general | solution.py:379
  45.7 0.1 broadcast_in_dim.2
  45.8 0.2 fusion.3
  46.1 0.0 copy-done
  46.1 0.0 copy-start.1
  46.1 1.5 %fusion.28.text_src = f32[16,16,1152]{2,1,0:T(8,128)} fusion(bf16[16,16,512]{2,1,0:T(8,128)(2,1)S(1)} %bitcast.24, bf16[512,1152,1]{1,0,2:T(8,128)(2,1)S(1)} %bitcast.23), kind=kOutput, calls=%fused_computation.52 | convolution fusion | flops 301989888 | bytes 2621440 | tf_op jit(solution)/shard_map/dot_general | solution.py:385
  47.6 0.0 copy-done.1
  47.6 0.7 fusion.4
  48.4 1.7 %pad_maximum_fusion = f32[512,1280]{1,0:T(8,128)} fusion(f32[512,128]{1,0:T(8,128)S(1)} %broadcast_in_dim.2, f32[512,1152]{1,0:T(8,128)S(1)} %fusion.4), kind=kLoop, calls=%fused_computation | loop fusion | flops 655360 | bytes 5242880 | tf_op jit(solution)/shard_map/concatenate | solution.py:386
  50.1 34.2 %shard_map.68 = (f32[16,128]{1,0:T(8,128)}, f32[16,1152]{1,0:T(8,128)}, f32[16,1152]{1,0:T(8,128)}) custom-call(f32[2,16,16,1280]{3,2,1,0:T(8,128)} %bitcast.21, f32[16,16,1152]{2,1,0:T(8,128)} %fusion.28.text_src, f32[16,1152]{1,0:T(8,128)} %get-tuple-element.24.image_unit, f32[16,1]{1,0:T(8,128)} %copy.9.image_norm, ...), custom_call_target="tpu_custom_call" | custom-call | tf_op jit(solution)/shard_map/pallas_call | solution.py:244
  84.3 1.3 %slice_reduce_fusion = f32[16]{0:T(128)} fusion(f32[16,128]{1,0:T(8,128)} %get-tuple-element.10), kind=kLoop, calls=%fused_computation.23 | loop fusion | bytes 128 | tf_op jit(solution)/shard_map/slice | solution.py:391
  85.6 1.5 %copy.15 = f32[16,1152]{1,0:T(8,128)} copy(f32[16,1152]{1,0:T(8,128)} %get-tuple-element.29) | data formatting | bytes 147456
  87.1 1.5 %copy.16 = f32[16,1152]{1,0:T(8,128)} copy(f32[16,1152]{1,0:T(8,128)} %get-tuple-element.30) | data formatting | bytes 147456
  (7 shorter events, 0.0 us)
Async XLA Ops:
  43.2 2.8 %copy-start = (bf16[32,16,1152]{2,1,0:T(8,128)(2,1)S(1)}, bf16[32,16,1152]{2,1,0:T(8,128)(2,1)}, u32[]{:S(2)}) copy-start(bf16[32,16,1152]{2,1,0:T(8,128)(2,1)} %get-tuple-element.8) | copy-start | bytes 3538948
  46.1 1.6 %copy-start.1 = (bf16[16,16,1152]{2,1,0:T(8,128)(2,1)S(1)}, bf16[16,16,1152]{2,1,0:T(8,128)(2,1)}, u32[]{:S(2)}) copy-start(bf16[16,16,1152]{2,1,0:T(8,128)(2,1)} %get-tuple-element.9) | copy-start | bytes 1769476

commit v16 on v15

--- a/solution.py
+++ b/solution.py
@@ -164,7 +164,7 @@
     lax.fori_loop(1, image_count, finish, 0)
 
 
-def merged_reduce_kernel(image_axes, image_src, text_src, image_unit, image_norm, text_unit, text_norm, loss_out,
+def merged_reduce_kernel(image_axes, image_src, text_src, image_unit, text_unit, loss_out,
                          image_grad, text_grad, image_send, image_recv, text_send, text_recv, inbox, outbox, halfbox,
                          summed, half_sems, image_out):
     image_count, image_me = group_size(image_axes), linear_index(image_axes)
@@ -212,14 +212,15 @@
     for slot in finals:
         remote(inbox.at[slot], inbox.at[slot], text_send.at[0], text_recv.at[slot], right).wait_recv()
     text_sum = text_src[me] + inbox[finals[0]] + inbox[finals[1]] + inbox[finals[2]] + inbox[finals[3]]
-    text_grad[...] = back_rows(text_sum, text_unit[...], text_norm[...])
+    text_grad[...] = text_sum - text_unit[...] * jnp.sum(text_unit[...] * text_sum, 1, keepdims=True)
     for copy in sends:
         copy.wait_send()
     swap.wait_send()
     lax.fori_loop(1, image_count, finish, 0)
     width = image_grad.shape[1]
     image_sum = jnp.sum(image_out[...], 0)
-    image_grad[...] = back_rows(image_sum[:, :width], image_unit[...], image_norm[...])
+    image_part = image_sum[:, :width]
+    image_grad[...] = image_part - image_unit[...] * jnp.sum(image_unit[...] * image_part, 1, keepdims=True)
     loss_out[...] = image_sum[:, width:]
 
 
@@ -248,7 +249,7 @@
             jax.ShapeDtypeStruct(block, jnp.float32),
             jax.ShapeDtypeStruct(block, jnp.float32),
         ),
-        in_specs=[vmem] * 6,
+        in_specs=[vmem] * 4,
         out_specs=(vmem, vmem, vmem),
         scratch_shapes=scratch,
         compiler_params=pltpu.CompilerParams(collective_id=tag, has_side_effects=True),
@@ -386,9 +387,9 @@
     image_part = jnp.concatenate([image_part, jnp.broadcast_to(loss, (image_count * rows, LOSS_LANES))], 1)
     loss_lanes, image_grad, text_grad = merged_reduce(
         CHIP_AXES, image_part.reshape(cores, chips, rows, width + LOSS_LANES), text_part.reshape(text_count, rows, width),
-        (image_unit, image_norm, text_unit, text_norm), 3
+        (image_unit, text_unit), 3
     )
-    return (loss_lanes[:, 0], image_grad, text_grad)
+    return (loss_lanes[:, 0], image_grad / image_norm, text_grad / text_norm)
 
 
 def solution(mesh):

time: 89.4 us -> 87.9 us (0.983)
  local copies, waits for them, and re-layouts: 5.85 us -> 1.46 us
  other arithmetic: 5.31 us -> 8.51 us
    div x0 -> x2, other arithmetic: none -> 3.19 us  [local(): return (loss_lanes[:, 0], image_grad / image_norm, text_grad / text_norm)]
    unnamed x6 -> x4, local copies, waits for them, and re-layouts: 3.05 us -> 0.01 us
    sqrt x2 -> x0, local copies, waits for them, and re-layouts: 1.35 us -> none  [unit_rows(): norms = jnp.sqrt(jnp.sum(floats * floats, 1, keepdims=True) + 1e-06)]
where the time goes in v16:
time: 87.9 us; the launch traced here: 87.3 us
  Pallas kernels  70.6 us (80%)
  other arithmetic  8.51 us (10%)
  matrix products  4.71 us (5%)
  between operations  2.03 us (2%)
  local copies, waits for them, and re-layouts  1.46 us (2%)
    pallas_call x1, Pallas kernels, exchange(): pl.pallas_call(functools.partial(reduce_kernel if scatter else gather_ker...  36.5 us
    pallas_call x1, Pallas kernels, merged_reduce(): pl.pallas_call(functools.partial(merged_reduce_kernel, image_axes), out_s...  34 us
    div x2, other arithmetic, local(): return (loss_lanes[:, 0], image_grad / image_norm, text_grad / text_norm)  3.19 us
    dot_general x1, matrix products, local(): lax.dot_general(gathered, seen, (((1,), (1,)), ((), ())), preferred_eleme...  2.44 us
    reduce_sum x2, other arithmetic, unit_rows(): norms = jnp.sqrt(jnp.sum(floats * floats, 1, keepdims=True) + 1e-06)  1.79 us

profile of v16, /device:TPU:24, one launch (start us, length us, event | category | flops | bytes accessed | tf_op | source)
XLA Modules:
  0.0 87.3 jit_solution(13324958388825519996)
XLA Ops:
  2.0 0.9 %fusion.10 = f32[16]{0:T(128)S(1)} fusion(bf16[16,1152]{1,0:T(8,128)(2,1)} %param.4), kind=kLoop, calls=%fused_computation.21 | loop fusion | flops 55280 | bytes 36928 | tf_op jit(solution)/shard_map/reduce_sum | solution.py:20
  2.9 0.9 %fusion.11 = f32[16]{0:T(128)S(1)} fusion(bf16[16,1152]{1,0:T(8,128)(2,1)} %param.5), kind=kLoop, calls=%fused_computation.22 | loop fusion | flops 55280 | bytes 36928 | tf_op jit(solution)/shard_map/reduce_sum | solution.py:20
  3.8 1.5 %convert_divide_fusion = (f32[16,1152]{1,0:T(8,128)}, bf16[16,1152]{1,0:T(8,128)(2,1)}, bf16[16,1152]{1,0:T(8,128)(2,1)}, f32[16,1152]{1,0:T(8,128)}) fusion(bf16[16,1152]{1,0:T(8,128)(2,1)} %param.5, f32[16]{0:T(128)S(1)} %add_sqrt_fusion, f32[16]{0:T(128)S(1)} %add_sqrt_fusion.1, bf16[16,1152]{1,0:T(8,128)(2,1)} %param.4), kind=kLoop, calls=%fused_computation.17 | loop fusion | flops 110592 | bytes 295040 | tf_op jit(solution)/shard_map/div | solution.py:21
  5.3 36.5 %shard_map.67 = (bf16[32,16,1152]{2,1,0:T(8,128)(2,1)}, bf16[16,16,1152]{2,1,0:T(8,128)(2,1)}) custom-call(bf16[16,1152]{1,0:T(8,128)(2,1)} %get-tuple-element.19.image_src, bf16[16,1152]{1,0:T(8,128)(2,1)} %get-tuple-element.14.text_src), custom_call_target="tpu_custom_call" | custom-call | tf_op jit(solution)/shard_map/pallas_call | solution.py:273
  41.9 0.0 copy-start
  41.9 2.4 %fusion.1 = (f32[512]{0:T(512)S(1)}, f32[512,256]{0,1:T(8,128)S(1)}) fusion(s32[512]{0:T(512)S(1)} %fusion.12, s32[256]{0:T(256)S(1)} %and_select_fusion, pred[512]{0:T(512)(128)(4,1)S(1)} %fusion.16, pred[256]{0:T(512)(128)(4,1)S(1)} %fusion.22, f32[]{:T(128)S(6)} %copy.8, bf16[512,1152]{1,0:T(8,128)(2,1)} %bitcast.18, bf16[256,1152]{1,0:T(8,128)(2,1)} %bitcast.21, ...), kind=kOutput, calls=%fused_computation.4 | convolution fusion | flops 303955456 | bytes 2299656 | tf_op jit(solution)/shard_map/dot_general | solution.py:380
  44.3 0.1 broadcast_in_dim.2
  44.5 0.2 fusion.3
  44.7 0.0 copy-done
  44.7 0.0 copy-start.1
  44.8 1.5 %fusion.26.text_src = f32[16,16,1152]{2,1,0:T(8,128)} fusion(bf16[16,16,512]{2,1,0:T(8,128)(2,1)S(1)} %bitcast.20, bf16[512,1152,1]{1,0,2:T(8,128)(2,1)S(1)} %bitcast.19), kind=kOutput, calls=%fused_computation.52 | convolution fusion | flops 301989888 | bytes 2621440 | tf_op jit(solution)/shard_map/dot_general | solution.py:386
  46.3 0.0 copy-done.1
  46.3 0.7 fusion.4
  47.0 1.7 %pad_maximum_fusion = f32[512,1280]{1,0:T(8,128)} fusion(f32[512,128]{1,0:T(8,128)S(1)} %broadcast_in_dim.2, f32[512,1152]{1,0:T(8,128)S(1)} %fusion.4), kind=kLoop, calls=%fused_computation | loop fusion | flops 655360 | bytes 5242880 | tf_op jit(solution)/shard_map/concatenate | solution.py:387
  48.7 34.0 %shard_map.68 = (f32[16,128]{1,0:T(8,128)}, f32[16,1152]{1,0:T(8,128)}, f32[16,1152]{1,0:T(8,128)}) custom-call(f32[2,16,16,1280]{3,2,1,0:T(8,128)} %bitcast.17, f32[16,16,1152]{2,1,0:T(8,128)} %fusion.26.text_src, f32[16,1152]{1,0:T(8,128)} %get-tuple-element.20.image_unit, f32[16,1152]{1,0:T(8,128)} %get-tuple-element.13.text_unit), custom_call_target="tpu_custom_call" | custom-call | tf_op jit(solution)/shard_map/pallas_call | solution.py:245
  82.8 1.3 %slice_reduce_fusion = f32[16]{0:T(128)} fusion(f32[16,128]{1,0:T(8,128)} %get-tuple-element.10), kind=kLoop, calls=%fused_computation.25 | loop fusion | bytes 128 | tf_op jit(solution)/shard_map/slice | solution.py:392
  84.1 1.6 %broadcast_divide_fusion.1 = f32[16,1152]{1,0:T(8,128)} fusion(f32[16,1152]{1,0:T(8,128)} %get-tuple-element.11, f32[16]{0:T(128)S(1)} %add_sqrt_fusion.1), kind=kLoop, calls=%fused_computation.24 | loop fusion | flops 18432 | bytes 147520 | tf_op jit(solution)/shard_map/div | solution.py:392
  85.7 1.6 %broadcast_divide_fusion = f32[16,1152]{1,0:T(8,128)} fusion(f32[16,1152]{1,0:T(8,128)} %get-tuple-element.12, f32[16]{0:T(128)S(1)} %add_sqrt_fusion), kind=kLoop, calls=%fused_computation.23 | loop fusion | flops 18432 | bytes 147520 | tf_op jit(solution)/shard_map/div | solution.py:392
  (7 shorter events, 0.0 us)
Async XLA Ops:
  41.9 2.8 %copy-start = (bf16[32,16,1152]{2,1,0:T(8,128)(2,1)S(1)}, bf16[32,16,1152]{2,1,0:T(8,128)(2,1)}, u32[]{:S(2)}) copy-start(bf16[32,16,1152]{2,1,0:T(8,128)(2,1)} %get-tuple-element.8) | copy-start | bytes 3538948
  44.7 1.6 %copy-start.1 = (bf16[16,16,1152]{2,1,0:T(8,128)(2,1)S(1)}, bf16[16,16,1152]{2,1,0:T(8,128)(2,1)}, u32[]{:S(2)}) copy-start(bf16[16,16,1152]{2,1,0:T(8,128)(2,1)} %get-tuple-element.9) | copy-start | bytes 1769476

commit v17 on v13

--- a/solution.py
+++ b/solution.py
@@ -90,7 +90,8 @@
     return finish
 
 
-def gather_kernel(image_axes, image_src, text_src, image_out, text_out, image_send, image_recv, text_send, text_recv):
+def gather_kernel(image_axes, image_src, text_src, scale_ref, shift_ref, image_part_out, text_part_out, image_send,
+                  image_recv, text_send, text_recv, image_out, text_out):
     image_count, image_me = group_size(image_axes), linear_index(image_axes)
     count, me, right, left = ring_peers()
     right2 = member(TEXT_AXES, (me + 2) % count)
@@ -132,6 +133,22 @@
     for copy in sends:
         copy.wait_send()
     lax.fori_loop(1, image_count, finish, 0)
+    rows, width = image_src.shape
+    gathered = image_out[...].reshape(image_count * rows, width)
+    seen = text_out[...].reshape(count * rows, width)
+    scale, shift = scale_ref[...], shift_ref[...]
+    shape = (image_count * rows, count * rows)
+    image_ids = lax.broadcasted_iota(jnp.int32, shape, 0)
+    text_ids = lax.broadcasted_iota(jnp.int32, shape, 1)
+    label = ((image_ids // rows == image_me) & (text_ids // rows == me) & (image_ids % rows == text_ids % rows)).astype(
+        jnp.float32)
+    logit = scale * lax.dot_general(gathered, seen, (((1,), (1,)), ((), ())), preferred_element_type=jnp.float32) + shift
+    total = image_count * count * rows
+    loss = jnp.sum(jax.nn.softplus(logit * (1.0 - 2.0 * label)), 1, keepdims=True) / total
+    coef = ((jax.nn.sigmoid(logit) - label) * scale).astype(jnp.bfloat16)
+    image_part_out[:, :width] = jnp.dot(coef, seen, preferred_element_type=jnp.float32)
+    image_part_out[:, width:] = jnp.broadcast_to(loss, (image_count * rows, LOSS_LANES))
+    text_part_out[...] = lax.dot_general(coef, gathered, (((0,), (0,)), ((), ())), preferred_element_type=jnp.float32)
 
 
 def reduce_kernel(image_axes, image_src, text_src, image_out, text_out, image_send, image_recv, text_send, text_recv,
@@ -243,6 +260,31 @@
     )(image_src, text_src)
 
 
+def gather_compute(image_axes, image_src, text_src, scale, shift, tag):
+    image_count, text_count = group_size(image_axes), group_size(TEXT_AXES)
+    rows, width = image_src.shape
+    vmem = pl.BlockSpec(memory_space=pltpu.VMEM)
+    scratch = [
+        pltpu.SemaphoreType.DMA((image_count,)),
+        pltpu.SemaphoreType.DMA((image_count,)),
+        pltpu.SemaphoreType.DMA((text_count,)),
+        pltpu.SemaphoreType.DMA((text_count,)),
+        pltpu.VMEM((image_count,) + image_src.shape, image_src.dtype),
+        pltpu.VMEM((text_count,) + text_src.shape, text_src.dtype),
+    ]
+    return pl.pallas_call(
+        functools.partial(gather_kernel, image_axes),
+        out_shape=(
+            jax.ShapeDtypeStruct((image_count * rows, width + LOSS_LANES), jnp.float32),
+            jax.ShapeDtypeStruct((text_count * rows, width), jnp.float32),
+        ),
+        in_specs=[vmem] * 4,
+        out_specs=(vmem, vmem),
+        scratch_shapes=scratch,
+        compiler_params=pltpu.CompilerParams(collective_id=tag, has_side_effects=True),
+    )(image_src, text_src, scale.reshape(1, 1), shift.reshape(1, 1))
+
+
 def exchange(image_axes, image_src, text_src, scatter, tag):
     image_count, text_count = group_size(image_axes), group_size(TEXT_AXES)
     image_shape = image_src.shape if scatter else (image_count,) + image_src.shape
@@ -352,26 +394,7 @@
     image_count = chips * cores
     text_count = group_size(TEXT_AXES)
     total = image_count * text_count * rows
-    gathered, seen = exchange(CORE_AXES + CHIP_AXES, image_emb, text_emb, False, 0)
-    gathered = gathered.reshape(image_count * rows, width)
-    seen = seen.reshape(text_count * rows, width)
-    image_ids = jnp.arange(image_count * rows, dtype=jnp.int32)[:, None]
-    text_ids = jnp.arange(text_count * rows, dtype=jnp.int32)[None, :]
-    mine_i = linear_index(CORE_AXES + CHIP_AXES)
-    mine_t = linear_index(TEXT_AXES)
-    label = (
-        (image_ids // rows == mine_i) & (text_ids // rows == mine_t) & (image_ids % rows == text_ids % rows)
-    ).astype(jnp.float32)
-    logit = (
-        scale
-        * lax.dot_general(gathered, seen, (((1,), (1,)), ((), ())), preferred_element_type=jnp.float32)
-        + shift
-    )
-    loss = jnp.sum(jax.nn.softplus(logit * (1.0 - 2.0 * label)), 1, keepdims=True) / total
-    coef = ((jax.nn.sigmoid(logit) - label) * scale).astype(jnp.bfloat16)
-    image_part = jnp.dot(coef, seen, preferred_element_type=jnp.float32)
-    text_part = lax.dot_general(coef, gathered, (((0,), (0,)), ((), ())), preferred_element_type=jnp.float32)
-    image_part = jnp.concatenate([image_part, jnp.broadcast_to(loss, (image_count * rows, LOSS_LANES))], 1)
+    image_part, text_part = gather_compute(CORE_AXES + CHIP_AXES, image_emb, text_emb, scale, shift, 0)
     image_in, text_in = merged_reduce(
         CHIP_AXES, image_part.reshape(cores, chips, rows, width + LOSS_LANES), text_part.reshape(text_count, rows, width), 3
     )

time: 87.4 us -> 82.7 us (0.946)
  matrix products: 4.72 us -> 0 us
  Pallas kernels: 70.7 us -> 73.1 us
  other arithmetic: 8.53 us -> 6.57 us
    dot_general x3 -> x0, matrix products: 4.72 us -> none  [the longest x1 2.44 us: local(): lax.dot_general(gathered, seen, (((1,), (1,)), ((), ())), preferred_eleme...]
    pallas_call x1, Pallas kernels: 36.5 us -> 38.9 us  [gather_compute(): pl.pallas_call(functools.partial(gather_kernel, image_axes), out_shape=(j...]
    concatenate x1 -> x0, other arithmetic: 1.7 us -> none  [local(): jnp.concatenate([image_part, jnp.broadcast_to(loss, (image_count * rows,...]
where the time goes in v17:
time: 82.7 us; the launch traced here: 82.3 us
  Pallas kernels  73.1 us (88%)
  other arithmetic  6.57 us (8%)
  between operations  1.98 us (2%)
    pallas_call x1, Pallas kernels, gather_compute(): pl.pallas_call(functools.partial(gather_kernel, image_axes), out_shape=(j...  38.9 us
    pallas_call x1, Pallas kernels, merged_reduce(): pl.pallas_call(functools.partial(merged_reduce_kernel, image_axes), out_s...  34.2 us
    reduce_sum x2, other arithmetic, unit_rows(): norms = jnp.sqrt(jnp.sum(floats * floats, 1, keepdims=True) + 1e-06)  1.79 us

profile of v17, /device:TPU:24, one launch (start us, length us, event | category | flops | bytes accessed | tf_op | source)
XLA Modules:
  0.0 82.3 jit_solution(9118692126146930828)
XLA Ops:
  1.9 0.9 %fusion = f32[16]{0:T(128)S(1)} fusion(bf16[16,1152]{1,0:T(8,128)(2,1)} %param.4), kind=kLoop, calls=%fused_computation.4 | loop fusion | flops 55280 | bytes 36928 | tf_op jit(solution)/shard_map/reduce_sum | solution.py:20
  2.8 0.9 %fusion.1 = f32[16]{0:T(128)S(1)} fusion(bf16[16,1152]{1,0:T(8,128)(2,1)} %param.5), kind=kLoop, calls=%fused_computation.5 | loop fusion | flops 55280 | bytes 36928 | tf_op jit(solution)/shard_map/reduce_sum | solution.py:20
  3.7 1.5 %fusion.2 = (bf16[16,1152]{1,0:T(8,128)(2,1)}, bf16[16,1152]{1,0:T(8,128)(2,1)}) fusion(f32[16]{0:T(128)S(1)} %add_sqrt_fusion.1, bf16[16,1152]{1,0:T(8,128)(2,1)} %param.4, f32[16]{0:T(128)S(1)} %add_sqrt_fusion, bf16[16,1152]{1,0:T(8,128)(2,1)} %param.5), kind=kLoop, calls=%fused_computation.13 | loop fusion | flops 110592 | bytes 147584 | tf_op jit(solution)/shard_map/convert_element_type | solution.py:390
  5.2 38.9 %shard_map.67 = (f32[512,1280]{1,0:T(8,128)}, f32[256,1152]{1,0:T(8,128)}) custom-call(bf16[16,1152]{1,0:T(8,128)(2,1)} %get-tuple-element.11.image_src, bf16[16,1152]{1,0:T(8,128)(2,1)} %get-tuple-element.12.text_src, f32[1,1]{1,0:T(1,128)} %bitcast.4.scale_ref, f32[1,1]{1,0:T(1,128)} %bitcast.5.shift_ref), custom_call_target="tpu_custom_call" | custom-call | tf_op jit(solution)/shard_map/pallas_call | solution.py:275
  44.2 34.2 %shard_map.68 = (f32[16,16,1280]{2,1,0:T(8,128)}, f32[16,1152]{1,0:T(8,128)}) custom-call(f32[2,16,16,1280]{3,2,1,0:T(8,128)} %bitcast.6, f32[16,16,1152]{2,1,0:T(8,128)} %bitcast.7), custom_call_target="tpu_custom_call" | custom-call | tf_op jit(solution)/shard_map/pallas_call | solution.py:253
  78.3 0.0 copy-start
  78.4 0.0 copy-start.1
  78.4 0.0 copy-start.2
  78.4 1.4 %reduce_sum.47 = f32[16,1280]{1,0:T(8,128)S(1)} reduce(f32[16,16,1280]{2,1,0:T(8,128)} %get-tuple-element.9, f32[]{:T(128)} %constant.0.clone.1), dimensions={0}, to_apply=%region_2.0 | reduce | flops 307200 | bytes 1392644 | tf_op jit(solution)/shard_map/reduce_sum | solution.py:401
  79.8 0.0 copy-done
  79.8 0.2 multiply_reduce_fusion.1
  80.0 0.6 slice_reduce_fusion
  80.6 0.7 subtract_divide_fusion.1
  81.4 0.0 copy-done.1
  81.4 0.0 copy-done.2
  81.4 0.2 multiply_reduce_fusion
  81.6 0.7 subtract_divide_fusion
  (2 shorter events, 0.0 us)
Async XLA Ops:
  78.3 1.5 %copy-start = (bf16[16,1152]{1,0:T(8,128)(2,1)S(1)}, bf16[16,1152]{1,0:T(8,128)(2,1)}, u32[]{:S(2)}) copy-start(bf16[16,1152]{1,0:T(8,128)(2,1)} %param.4) | copy-start | bytes 110596
  78.4 3.0 %copy-start.1 = (bf16[16,1152]{1,0:T(8,128)(2,1)S(1)}, bf16[16,1152]{1,0:T(8,128)(2,1)}, u32[]{:S(2)}) copy-start(bf16[16,1152]{1,0:T(8,128)(2,1)} %param.5) | copy-start | bytes 110596
  78.4 3.0 %copy-start.2 = (f32[16,1152]{1,0:T(8,128)S(1)}, f32[16,1152]{1,0:T(8,128)}, u32[]{:S(2)}) copy-start(f32[16,1152]{1,0:T(8,128)} %get-tuple-element.10) | copy-start | bytes 221188

commit v18 on v17

--- a/solution.py
+++ b/solution.py
@@ -90,8 +90,17 @@
     return finish
 
 
-def gather_kernel(image_axes, image_src, text_src, scale_ref, shift_ref, image_part_out, text_part_out, image_send,
-                  image_recv, text_send, text_recv, image_out, text_out):
+def gather_kernel(image_axes, image_raw, text_raw, scale_ref, shift_ref, image_part_out, text_part_out,
+                  image_unit_out, image_norm_out, text_unit_out, text_norm_out, image_send, image_recv, text_send,
+                  text_recv, image_out, text_out, image_src, text_src):
+    for raw, unit_out, norm_out, emb in ((image_raw, image_unit_out, image_norm_out, image_src),
+                                         (text_raw, text_unit_out, text_norm_out, text_src)):
+        floats = raw[...].astype(jnp.float32)
+        norms = jnp.sqrt(jnp.sum(floats * floats, 1, keepdims=True) + 1e-06)
+        units = floats / norms
+        unit_out[...] = units
+        norm_out[...] = jnp.broadcast_to(norms, norm_out.shape)
+        emb[...] = units.astype(jnp.bfloat16)
     image_count, image_me = group_size(image_axes), linear_index(image_axes)
     count, me, right, left = ring_peers()
     right2 = member(TEXT_AXES, (me + 2) % count)
@@ -269,17 +278,23 @@
         pltpu.SemaphoreType.DMA((image_count,)),
         pltpu.SemaphoreType.DMA((text_count,)),
         pltpu.SemaphoreType.DMA((text_count,)),
-        pltpu.VMEM((image_count,) + image_src.shape, image_src.dtype),
-        pltpu.VMEM((text_count,) + text_src.shape, text_src.dtype),
+        pltpu.VMEM((image_count,) + image_src.shape, jnp.bfloat16),
+        pltpu.VMEM((text_count,) + text_src.shape, jnp.bfloat16),
+        pltpu.VMEM(image_src.shape, jnp.bfloat16),
+        pltpu.VMEM(text_src.shape, jnp.bfloat16),
     ]
     return pl.pallas_call(
         functools.partial(gather_kernel, image_axes),
         out_shape=(
             jax.ShapeDtypeStruct((image_count * rows, width + LOSS_LANES), jnp.float32),
             jax.ShapeDtypeStruct((text_count * rows, width), jnp.float32),
+            jax.ShapeDtypeStruct((rows, width), jnp.float32),
+            jax.ShapeDtypeStruct((rows, LOSS_LANES), jnp.float32),
+            jax.ShapeDtypeStruct((rows, width), jnp.float32),
+            jax.ShapeDtypeStruct((rows, LOSS_LANES), jnp.float32),
         ),
         in_specs=[vmem] * 4,
-        out_specs=(vmem, vmem),
+        out_specs=tuple([vmem] * 6),
         scratch_shapes=scratch,
         compiler_params=pltpu.CompilerParams(collective_id=tag, has_side_effects=True),
     )(image_src, text_src, scale.reshape(1, 1), shift.reshape(1, 1))
@@ -385,16 +400,14 @@
 
 def local(images, texts, scale, shift):
     rows, width = images.shape
-    image_unit, image_norm = unit_rows(images)
-    text_unit, text_norm = unit_rows(texts)
-    image_emb = image_unit.astype(jnp.bfloat16)
-    text_emb = text_unit.astype(jnp.bfloat16)
     chips = group_size(CHIP_AXES)
     cores = group_size(CORE_AXES)
-    image_count = chips * cores
     text_count = group_size(TEXT_AXES)
-    total = image_count * text_count * rows
-    image_part, text_part = gather_compute(CORE_AXES + CHIP_AXES, image_emb, text_emb, scale, shift, 0)
+    image_part, text_part, image_unit, image_norm, text_unit, text_norm = gather_compute(
+        CORE_AXES + CHIP_AXES, images, texts, scale, shift, 0
+    )
+    image_norm = image_norm[:, :1]
+    text_norm = text_norm[:, :1]
     image_in, text_in = merged_reduce(
         CHIP_AXES, image_part.reshape(cores, chips, rows, width + LOSS_LANES), text_part.reshape(text_count, rows, width), 3
     )

time: 82.7 us -> 80.7 us (0.976)
  other arithmetic: 6.57 us -> 2.48 us
  Pallas kernels: 73.1 us -> 75.1 us
    reduce_sum x2 -> x0, other arithmetic: 1.79 us -> none  [unit_rows(): norms = jnp.sqrt(jnp.sum(floats * floats, 1, keepdims=True) + 1e-06)]
    pallas_call x1, Pallas kernels: 34.2 us -> 35.7 us  [merged_reduce(): pl.pallas_call(functools.partial(merged_reduce_kernel, image_axes), out_s...]
    convert_element_type x1 -> x0, other arithmetic: 1.5 us -> none  [local(): image_emb = image_unit.astype(jnp.bfloat16)]
where the time goes in v18:
time: 80.7 us; the launch traced here: 80.5 us
  Pallas kernels  75.1 us (93%)
  other arithmetic  2.48 us (3%)
  between operations  1.99 us (2%)
  local copies, waits for them, and re-layouts  0.87 us (1%)
    pallas_call x1, Pallas kernels, gather_compute(): pl.pallas_call(functools.partial(gather_kernel, image_axes), out_shape=(j...  39.4 us
    pallas_call x1, Pallas kernels, merged_reduce(): pl.pallas_call(functools.partial(merged_reduce_kernel, image_axes), out_s...  35.7 us

profile of v18, /device:TPU:24, one launch (start us, length us, event | category | flops | bytes accessed | tf_op | source)
XLA Modules:
  0.0 80.5 jit_solution(10180313158186046558)
XLA Ops:
  1.9 39.4 %shard_map.67 = (f32[512,1280]{1,0:T(8,128)}, f32[256,1152]{1,0:T(8,128)}, f32[16,1152]{1,0:T(8,128)}, f32[16,128]{1,0:T(8,128)}, f32[16,1152]{1,0:T(8,128)}, /*index=5*/f32[16,128]{1,0:T(8,128)}) custom-call(bf16[16,1152]{1,0:T(8,128)(2,1)} %image_raw.1, bf16[16,1152]{1,0:T(8,128)(2,1)} %text_raw.1, f32[1,1]{1,0:T(1,128)} %bitcast.4.scale_ref, ...), custom_call_target="tpu_custom_call" | custom-call | tf_op jit(solution)/shard_map/pallas_call | solution.py:286
  41.4 35.7 %shard_map.68 = (f32[16,16,1280]{2,1,0:T(8,128)}, f32[16,1152]{1,0:T(8,128)}) custom-call(f32[2,16,16,1280]{3,2,1,0:T(8,128)} %bitcast.6, f32[16,16,1152]{2,1,0:T(8,128)} %bitcast.7), custom_call_target="tpu_custom_call" | custom-call | tf_op jit(solution)/shard_map/pallas_call | solution.py:262
  77.1 0.0 copy-start
  77.1 0.0 copy-start.1
  77.1 0.0 copy-start.2
  77.1 0.0 copy-start.4
  77.1 0.0 copy-start.3
  77.1 1.5 %reduce_sum.27 = f32[16,1280]{1,0:T(8,128)S(1)} reduce(f32[16,16,1280]{2,1,0:T(8,128)} %get-tuple-element.13, f32[]{:T(128)} %constant.0.clone.1), dimensions={0}, to_apply=%region_0.0 | reduce | flops 307200 | bytes 1392644 | tf_op jit(solution)/shard_map/reduce_sum | solution.py:414
  78.6 0.0 copy-done
  78.6 0.1 multiply_reduce_fusion.1
  78.7 0.6 slice_reduce_fusion
  79.3 0.0 copy-done.1
  79.4 0.0 copy-done.2
  79.4 0.1 multiply_reduce_fusion
  79.5 0.0 copy-done.4
  79.5 0.1 slice_reduce_fusion.2
  79.6 0.0 copy-done.3
  79.6 0.1 slice_reduce_fusion.1
  79.7 0.8 subtract_divide_fusion
Async XLA Ops:
  77.1 1.5 %copy-start = (f32[16,1152]{1,0:T(8,128)S(1)}, f32[16,1152]{1,0:T(8,128)}, u32[]{:S(2)}) copy-start(f32[16,1152]{1,0:T(8,128)} %get-tuple-element.14) | copy-start | bytes 221188
  77.1 2.3 %copy-start.1 = (f32[16,1152]{1,0:T(8,128)S(1)}, f32[16,1152]{1,0:T(8,128)}, u32[]{:S(2)}) copy-start(f32[16,1152]{1,0:T(8,128)} %get-tuple-element.17) | copy-start | bytes 221188
  77.1 2.3 %copy-start.2 = (f32[16,1152]{1,0:T(8,128)S(1)}, f32[16,1152]{1,0:T(8,128)}, u32[]{:S(2)}) copy-start(f32[16,1152]{1,0:T(8,128)} %get-tuple-element.16) | copy-start | bytes 221188
  77.1 2.4 %copy-start.4 = (f32[16,128]{1,0:T(8,128)S(1)}, f32[16,128]{1,0:T(8,128)}, u32[]{:S(2)}) copy-start(f32[16,128]{1,0:T(8,128)} %get-tuple-element.15) | copy-start | bytes 24580
  77.1 2.5 %copy-start.3 = (f32[16,128]{1,0:T(8,128)S(1)}, f32[16,128]{1,0:T(8,128)}, u32[]{:S(2)}) copy-start(f32[16,128]{1,0:T(8,128)} %get-tuple-element.18) | copy-start | bytes 24580

commit v19 on v18

--- a/solution.py
+++ b/solution.py
@@ -190,8 +190,8 @@
     lax.fori_loop(1, image_count, finish, 0)
 
 
-def merged_reduce_kernel(image_axes, image_src, text_src, image_out, text_out, image_send, image_recv, text_send,
-                         text_recv, inbox, outbox, halfbox, summed, half_sems):
+def merged_reduce_kernel(image_axes, image_src, text_src, image_total, text_out, image_send, image_recv, text_send,
+                         text_recv, inbox, outbox, halfbox, summed, half_sems, image_out):
     image_count, image_me = group_size(image_axes), linear_index(image_axes)
     count, me, right, left = ring_peers()
     right2 = member(TEXT_AXES, (me + 2) % count)
@@ -241,6 +241,7 @@
         copy.wait_send()
     swap.wait_send()
     lax.fori_loop(1, image_count, finish, 0)
+    image_total[...] = jnp.sum(image_out[...], 0)
 
 
 def merged_reduce(image_axes, image_src, text_src, tag):
@@ -258,10 +259,11 @@
         pltpu.VMEM(image_shape, image_src.dtype),
         pltpu.VMEM(image_shape, image_src.dtype),
         pltpu.SemaphoreType.DMA((2,)),
+        pltpu.VMEM(image_shape, image_src.dtype),
     ]
     return pl.pallas_call(
         functools.partial(merged_reduce_kernel, image_axes),
-        out_shape=(jax.ShapeDtypeStruct(image_shape, image_src.dtype), jax.ShapeDtypeStruct(block, text_src.dtype)),
+        out_shape=(jax.ShapeDtypeStruct(image_shape[1:], image_src.dtype), jax.ShapeDtypeStruct(block, text_src.dtype)),
         in_specs=[vmem, vmem],
         out_specs=(vmem, vmem),
         scratch_shapes=scratch,
@@ -411,7 +413,6 @@
     image_in, text_in = merged_reduce(
         CHIP_AXES, image_part.reshape(cores, chips, rows, width + LOSS_LANES), text_part.reshape(text_count, rows, width), 3
     )
-    image_in = jnp.sum(image_in, 0)
     text_sum = text_in
     image_grad = back_rows(image_in[:, :width], image_unit, image_norm)
     text_grad = back_rows(text_sum, text_unit, text_norm)

time: 80.7 us -> 82.4 us (1.021)
  other arithmetic: 2.48 us -> 3.69 us
    reduce_sum x2, other arithmetic: 0.25 us -> 2.02 us  [back_rows(): return (grads - units * jnp.sum(units * grads, 1, keepdims=True)) / norms]
    reduce_sum x1 -> x0, other arithmetic: 1.47 us -> none  [local(): image_in = jnp.sum(image_in, 0)]
    div x1, other arithmetic: 0.76 us -> 1.67 us  [back_rows(): return (grads - units * jnp.sum(units * grads, 1, keepdims=True)) / norms]
where the time goes in v19:
time: 82.4 us; the launch traced here: 82 us
  Pallas kernels  74.7 us (91%)
  other arithmetic  3.69 us (4%)
  between operations  1.98 us (2%)
  local copies, waits for them, and re-layouts  1.57 us (2%)
    pallas_call x1, Pallas kernels, gather_compute(): pl.pallas_call(functools.partial(gather_kernel, image_axes), out_shape=(j...  39.3 us
    pallas_call x1, Pallas kernels, merged_reduce(): pl.pallas_call(functools.partial(merged_reduce_kernel, image_axes), out_s...  35.4 us
    reduce_sum x2, other arithmetic, back_rows(): return (grads - units * jnp.sum(units * grads, 1, keepdims=True)) / norms  2.02 us
    div x1, other arithmetic, back_rows(): return (grads - units * jnp.sum(units * grads, 1, keepdims=True)) / norms  1.67 us

profile of v19, /device:TPU:24, one launch (start us, length us, event | category | flops | bytes accessed | tf_op | source)
XLA Modules:
  0.0 82.0 jit_solution(8125381060200240063)
XLA Ops:
  1.9 39.3 %shard_map.67 = (f32[512,1280]{1,0:T(8,128)}, f32[256,1152]{1,0:T(8,128)}, f32[16,1152]{1,0:T(8,128)}, f32[16,128]{1,0:T(8,128)}, f32[16,1152]{1,0:T(8,128)}, /*index=5*/f32[16,128]{1,0:T(8,128)}) custom-call(bf16[16,1152]{1,0:T(8,128)(2,1)} %image_raw.1, bf16[16,1152]{1,0:T(8,128)(2,1)} %text_raw.1, f32[1,1]{1,0:T(1,128)} %bitcast.4.scale_ref, ...), custom_call_target="tpu_custom_call" | custom-call | tf_op jit(solution)/shard_map/pallas_call | solution.py:288
  41.3 0.0 copy-start.1
  41.3 0.0 copy-start
  41.3 0.0 copy-start.3
  41.3 0.0 copy-start.2
  41.3 35.4 %shard_map.68 = (f32[16,1280]{1,0:T(8,128)}, f32[16,1152]{1,0:T(8,128)}) custom-call(f32[2,16,16,1280]{3,2,1,0:T(8,128)} %bitcast.6, f32[16,16,1152]{2,1,0:T(8,128)} %bitcast.7), custom_call_target="tpu_custom_call" | custom-call | tf_op jit(solution)/shard_map/pallas_call | solution.py:264
  76.7 0.0 copy-done.1
  76.7 1.0 %multiply_reduce_fusion = f32[16]{0:T(128)S(1)} fusion(f32[16,1152]{1,0:T(8,128)S(1)} %copy-done.1, f32[16,1152]{1,0:T(8,128)} %get-tuple-element.16), kind=kLoop, calls=%fused_computation.1 | loop fusion | flops 36848 | bytes 147520 | tf_op jit(solution)/shard_map/reduce_sum | solution.py:25
  77.7 0.0 copy-done
  77.8 1.0 %multiply_reduce_fusion.1 = f32[16]{0:T(128)S(1)} fusion(f32[16,1152]{1,0:T(8,128)S(1)} %copy-done, f32[16,1280]{1,0:T(8,128)} %get-tuple-element.13), kind=kLoop, calls=%fused_computation.3 | loop fusion | flops 36848 | bytes 147520 | tf_op jit(solution)/shard_map/reduce_sum | solution.py:25
  78.8 1.3 %slice_reduce_fusion.2 = f32[16]{0:T(128)} fusion(f32[16,1280]{1,0:T(8,128)} %get-tuple-element.13), kind=kLoop, calls=%fused_computation.6 | loop fusion | bytes 128 | tf_op jit(solution)/shard_map/slice | solution.py:419
  80.1 0.0 copy-done.3
  80.1 0.1 slice_reduce_fusion.1
  80.2 0.0 copy-done.2
  80.2 0.1 slice_reduce_fusion
  80.3 1.7 %subtract_divide_fusion = (f32[16,1152]{1,0:T(8,128)}, f32[16,1152]{1,0:T(8,128)}) fusion(f32[16,1152]{1,0:T(8,128)} %get-tuple-element.16, f32[16,1152]{1,0:T(8,128)S(1)} %copy-done.1, f32[16]{0:T(128)S(1)} %slice_reduce_fusion, f32[16]{0:T(128)S(1)} %multiply_reduce_fusion, f32[16]{0:T(128)S(1)} %slice_reduce_fusion.1, f32[16,1152]{1,0:T(8,128)S(1)} %copy-done, ...), kind=kLoop, calls=%fused_computation | loop fusion | flops 110592 | bytes 442624 | tf_op jit(solution)/shard_map/div | solution.py:25
Async XLA Ops:
  41.3 35.5 %copy-start.1 = (f32[16,1152]{1,0:T(8,128)S(1)}, f32[16,1152]{1,0:T(8,128)}, u32[]{:S(2)}) copy-start(f32[16,1152]{1,0:T(8,128)} %get-tuple-element.17) | copy-start | bytes 221188
  41.3 36.5 %copy-start = (f32[16,1152]{1,0:T(8,128)S(1)}, f32[16,1152]{1,0:T(8,128)}, u32[]{:S(2)}) copy-start(f32[16,1152]{1,0:T(8,128)} %get-tuple-element.14) | copy-start | bytes 221188
  41.3 38.8 %copy-start.3 = (f32[16,128]{1,0:T(8,128)S(1)}, f32[16,128]{1,0:T(8,128)}, u32[]{:S(2)}) copy-start(f32[16,128]{1,0:T(8,128)} %get-tuple-element.15) | copy-start | bytes 24580
  41.3 38.9 %copy-start.2 = (f32[16,128]{1,0:T(8,128)S(1)}, f32[16,128]{1,0:T(8,128)}, u32[]{:S(2)}) copy-start(f32[16,128]{1,0:T(8,128)} %get-tuple-element.18) | copy-start | bytes 24580

commit v20 on v18

--- a/solution.py
+++ b/solution.py
@@ -157,7 +157,14 @@
     coef = ((jax.nn.sigmoid(logit) - label) * scale).astype(jnp.bfloat16)
     image_part_out[:, :width] = jnp.dot(coef, seen, preferred_element_type=jnp.float32)
     image_part_out[:, width:] = jnp.broadcast_to(loss, (image_count * rows, LOSS_LANES))
-    text_part_out[...] = lax.dot_general(coef, gathered, (((0,), (0,)), ((), ())), preferred_element_type=jnp.float32)
+    shape_t = (count * rows, image_count * rows)
+    text_ids_t = lax.broadcasted_iota(jnp.int32, shape_t, 0)
+    image_ids_t = lax.broadcasted_iota(jnp.int32, shape_t, 1)
+    label_t = ((image_ids_t // rows == image_me) & (text_ids_t // rows == me)
+               & (image_ids_t % rows == text_ids_t % rows)).astype(jnp.float32)
+    logit_t = scale * lax.dot_general(seen, gathered, (((1,), (1,)), ((), ())), preferred_element_type=jnp.float32) + shift
+    coef_t = ((jax.nn.sigmoid(logit_t) - label_t) * scale).astype(jnp.bfloat16)
+    text_part_out[...] = jnp.dot(coef_t, gathered, preferred_element_type=jnp.float32)
 
 
 def reduce_kernel(image_axes, image_src, text_src, image_out, text_out, image_send, image_recv, text_send, text_recv,

time: 80.7 us -> 80.9 us (level)
  no operation moved by 1% of the time
where the time goes in v20:
time: 80.9 us; the launch traced here: 80.7 us
  Pallas kernels  75.3 us (93%)
  other arithmetic  2.48 us (3%)
  between operations  1.99 us (2%)
  local copies, waits for them, and re-layouts  0.87 us (1%)
    pallas_call x1, Pallas kernels, gather_compute(): pl.pallas_call(functools.partial(gather_kernel, image_axes), out_shape=(j...  39.7 us
    pallas_call x1, Pallas kernels, merged_reduce(): pl.pallas_call(functools.partial(merged_reduce_kernel, image_axes), out_s...  35.7 us

profile of v20, /device:TPU:24, one launch (start us, length us, event | category | flops | bytes accessed | tf_op | source)
XLA Modules:
  0.0 80.7 jit_solution(4623198278681894059)
XLA Ops:
  1.9 39.7 %shard_map.67 = (f32[512,1280]{1,0:T(8,128)}, f32[256,1152]{1,0:T(8,128)}, f32[16,1152]{1,0:T(8,128)}, f32[16,128]{1,0:T(8,128)}, f32[16,1152]{1,0:T(8,128)}, /*index=5*/f32[16,128]{1,0:T(8,128)}) custom-call(bf16[16,1152]{1,0:T(8,128)(2,1)} %image_raw.1, bf16[16,1152]{1,0:T(8,128)(2,1)} %text_raw.1, f32[1,1]{1,0:T(1,128)} %bitcast.4.scale_ref, ...), custom_call_target="tpu_custom_call" | custom-call | tf_op jit(solution)/shard_map/pallas_call | solution.py:293
  41.6 35.7 %shard_map.68 = (f32[16,16,1280]{2,1,0:T(8,128)}, f32[16,1152]{1,0:T(8,128)}) custom-call(f32[2,16,16,1280]{3,2,1,0:T(8,128)} %bitcast.6, f32[16,16,1152]{2,1,0:T(8,128)} %bitcast.7), custom_call_target="tpu_custom_call" | custom-call | tf_op jit(solution)/shard_map/pallas_call | solution.py:269
  77.3 0.0 copy-start
  77.3 0.0 copy-start.1
  77.3 0.0 copy-start.2
  77.3 0.0 copy-start.4
  77.3 0.0 copy-start.3
  77.3 1.5 %reduce_sum.27 = f32[16,1280]{1,0:T(8,128)S(1)} reduce(f32[16,16,1280]{2,1,0:T(8,128)} %get-tuple-element.13, f32[]{:T(128)} %constant.0.clone.1), dimensions={0}, to_apply=%region_0.0 | reduce | flops 307200 | bytes 1392644 | tf_op jit(solution)/shard_map/reduce_sum | solution.py:421
  78.8 0.0 copy-done
  78.8 0.1 multiply_reduce_fusion.1
  78.9 0.6 slice_reduce_fusion
  79.6 0.0 copy-done.1
  79.6 0.0 copy-done.2
  79.6 0.1 multiply_reduce_fusion
  79.7 0.0 copy-done.4
  79.7 0.1 slice_reduce_fusion.2
  79.8 0.0 copy-done.3
  79.8 0.1 slice_reduce_fusion.1
  79.9 0.8 subtract_divide_fusion
Async XLA Ops:
  77.3 1.5 %copy-start = (f32[16,1152]{1,0:T(8,128)S(1)}, f32[16,1152]{1,0:T(8,128)}, u32[]{:S(2)}) copy-start(f32[16,1152]{1,0:T(8,128)} %get-tuple-element.14) | copy-start | bytes 221188
  77.3 2.3 %copy-start.1 = (f32[16,1152]{1,0:T(8,128)S(1)}, f32[16,1152]{1,0:T(8,128)}, u32[]{:S(2)}) copy-start(f32[16,1152]{1,0:T(8,128)} %get-tuple-element.17) | copy-start | bytes 221188
  77.3 2.3 %copy-start.2 = (f32[16,1152]{1,0:T(8,128)S(1)}, f32[16,1152]{1,0:T(8,128)}, u32[]{:S(2)}) copy-start(f32[16,1152]{1,0:T(8,128)} %get-tuple-element.16) | copy-start | bytes 221188
  77.3 2.4 %copy-start.4 = (f32[16,128]{1,0:T(8,128)S(1)}, f32[16,128]{1,0:T(8,128)}, u32[]{:S(2)}) copy-start(f32[16,128]{1,0:T(8,128)} %get-tuple-element.15) | copy-start | bytes 24580
  77.3 2.5 %copy-start.3 = (f32[16,128]{1,0:T(8,128)S(1)}, f32[16,128]{1,0:T(8,128)}, u32[]{:S(2)}) copy-start(f32[16,128]{1,0:T(8,128)} %get-tuple-element.18) | copy-start | bytes 24580

commit v21 on v20

--- a/solution.py
+++ b/solution.py
@@ -149,8 +149,7 @@
     shape = (image_count * rows, count * rows)
     image_ids = lax.broadcasted_iota(jnp.int32, shape, 0)
     text_ids = lax.broadcasted_iota(jnp.int32, shape, 1)
-    label = ((image_ids // rows == image_me) & (text_ids // rows == me) & (image_ids % rows == text_ids % rows)).astype(
-        jnp.float32)
+    label = ((image_ids - text_ids == (image_me - me) * rows) & (text_ids // rows == me)).astype(jnp.float32)
     logit = scale * lax.dot_general(gathered, seen, (((1,), (1,)), ((), ())), preferred_element_type=jnp.float32) + shift
     total = image_count * count * rows
     loss = jnp.sum(jax.nn.softplus(logit * (1.0 - 2.0 * label)), 1, keepdims=True) / total
@@ -160,8 +159,7 @@
     shape_t = (count * rows, image_count * rows)
     text_ids_t = lax.broadcasted_iota(jnp.int32, shape_t, 0)
     image_ids_t = lax.broadcasted_iota(jnp.int32, shape_t, 1)
-    label_t = ((image_ids_t // rows == image_me) & (text_ids_t // rows == me)
-               & (image_ids_t % rows == text_ids_t % rows)).astype(jnp.float32)
+    label_t = ((image_ids_t - text_ids_t == (image_me - me) * rows) & (text_ids_t // rows == me)).astype(jnp.float32)
     logit_t = scale * lax.dot_general(seen, gathered, (((1,), (1,)), ((), ())), preferred_element_type=jnp.float32) + shift
     coef_t = ((jax.nn.sigmoid(logit_t) - label_t) * scale).astype(jnp.bfloat16)
     text_part_out[...] = jnp.dot(coef_t, gathered, preferred_element_type=jnp.float32)

time: 80.9 us -> 80.9 us (level)
  no operation moved by 1% of the time
where the time goes in v21:
time: 80.9 us; the launch traced here: 80.7 us
  Pallas kernels  75.3 us (93%)
  other arithmetic  2.48 us (3%)
  between operations  1.99 us (2%)
  local copies, waits for them, and re-layouts  0.87 us (1%)
    pallas_call x1, Pallas kernels, gather_compute(): pl.pallas_call(functools.partial(gather_kernel, image_axes), out_shape=(j...  39.7 us
    pallas_call x1, Pallas kernels, merged_reduce(): pl.pallas_call(functools.partial(merged_reduce_kernel, image_axes), out_s...  35.7 us

profile of v21, /device:TPU:24, one launch (start us, length us, event | category | flops | bytes accessed | tf_op | source)
XLA Modules:
  0.0 80.7 jit_solution(18366963562673127167)
XLA Ops:
  1.9 39.7 %shard_map.67 = (f32[512,1280]{1,0:T(8,128)}, f32[256,1152]{1,0:T(8,128)}, f32[16,1152]{1,0:T(8,128)}, f32[16,128]{1,0:T(8,128)}, f32[16,1152]{1,0:T(8,128)}, /*index=5*/f32[16,128]{1,0:T(8,128)}) custom-call(bf16[16,1152]{1,0:T(8,128)(2,1)} %image_raw.1, bf16[16,1152]{1,0:T(8,128)(2,1)} %text_raw.1, f32[1,1]{1,0:T(1,128)} %bitcast.4.scale_ref, ...), custom_call_target="tpu_custom_call" | custom-call | tf_op jit(solution)/shard_map/pallas_call | solution.py:291
  41.6 35.7 %shard_map.68 = (f32[16,16,1280]{2,1,0:T(8,128)}, f32[16,1152]{1,0:T(8,128)}) custom-call(f32[2,16,16,1280]{3,2,1,0:T(8,128)} %bitcast.6, f32[16,16,1152]{2,1,0:T(8,128)} %bitcast.7), custom_call_target="tpu_custom_call" | custom-call | tf_op jit(solution)/shard_map/pallas_call | solution.py:267
  77.3 0.0 copy-start
  77.3 0.0 copy-start.1
  77.3 0.0 copy-start.2
  77.3 0.0 copy-start.4
  77.3 0.0 copy-start.3
  77.3 1.5 %reduce_sum.27 = f32[16,1280]{1,0:T(8,128)S(1)} reduce(f32[16,16,1280]{2,1,0:T(8,128)} %get-tuple-element.13, f32[]{:T(128)} %constant.0.clone.1), dimensions={0}, to_apply=%region_0.0 | reduce | flops 307200 | bytes 1392644 | tf_op jit(solution)/shard_map/reduce_sum | solution.py:419
  78.8 0.0 copy-done
  78.8 0.1 multiply_reduce_fusion.1
  78.9 0.6 slice_reduce_fusion
  79.6 0.0 copy-done.1
  79.6 0.0 copy-done.2
  79.6 0.1 multiply_reduce_fusion
  79.7 0.0 copy-done.4
  79.7 0.1 slice_reduce_fusion.2
  79.8 0.0 copy-done.3
  79.8 0.1 slice_reduce_fusion.1
  79.9 0.8 subtract_divide_fusion
Async XLA Ops:
  77.3 1.5 %copy-start = (f32[16,1152]{1,0:T(8,128)S(1)}, f32[16,1152]{1,0:T(8,128)}, u32[]{:S(2)}) copy-start(f32[16,1152]{1,0:T(8,128)} %get-tuple-element.14) | copy-start | bytes 221188
  77.3 2.3 %copy-start.1 = (f32[16,1152]{1,0:T(8,128)S(1)}, f32[16,1152]{1,0:T(8,128)}, u32[]{:S(2)}) copy-start(f32[16,1152]{1,0:T(8,128)} %get-tuple-element.17) | copy-start | bytes 221188
  77.3 2.3 %copy-start.2 = (f32[16,1152]{1,0:T(8,128)S(1)}, f32[16,1152]{1,0:T(8,128)}, u32[]{:S(2)}) copy-start(f32[16,1152]{1,0:T(8,128)} %get-tuple-element.16) | copy-start | bytes 221188
  77.3 2.4 %copy-start.4 = (f32[16,128]{1,0:T(8,128)S(1)}, f32[16,128]{1,0:T(8,128)}, u32[]{:S(2)}) copy-start(f32[16,128]{1,0:T(8,128)} %get-tuple-element.15) | copy-start | bytes 24580
  77.3 2.5 %copy-start.3 = (f32[16,128]{1,0:T(8,128)S(1)}, f32[16,128]{1,0:T(8,128)}, u32[]{:S(2)}) copy-start(f32[16,128]{1,0:T(8,128)} %get-tuple-element.18) | copy-start | bytes 24580

commit v22 on v20

--- a/solution.py
+++ b/solution.py
@@ -235,11 +235,11 @@
     swap.start()
     step_sends(1)
     step_sends(2)
+    step_sends(3)
     swap.wait_recv()
     summed[...] = image_src[core] + halfbox[...]
     finish = image_direct(image_axes, True, summed, image_out, image_send, image_recv, image_count, image_me)
-    for step in range(3, 5):
-        step_sends(step)
+    step_sends(4)
     finals = (3, 7, 10, 14)
     for slot in finals:
         remote(inbox.at[slot], inbox.at[slot], text_send.at[0], text_recv.at[slot], right).wait_recv()

time: 80.9 us -> 84.5 us (1.044); the launches traced: 80.7 us -> 82.9 us
  Pallas kernels: 75.3 us -> 77.5 us
    pallas_call x1, Pallas kernels: 35.7 us -> 37.9 us  [merged_reduce(): pl.pallas_call(functools.partial(merged_reduce_kernel, image_axes), out_s...]
where the time goes in v22:
time: 84.5 us; the launch traced here: 82.9 us
  Pallas kernels  77.5 us (92%)
  other arithmetic  2.48 us (3%)
  between operations  1.99 us (2%)
  local copies, waits for them, and re-layouts  0.87 us (1%)
    pallas_call x1, Pallas kernels, gather_compute(): pl.pallas_call(functools.partial(gather_kernel, image_axes), out_shape=(j...  39.7 us
    pallas_call x1, Pallas kernels, merged_reduce(): pl.pallas_call(functools.partial(merged_reduce_kernel, image_axes), out_s...  37.9 us

profile of v22, /device:TPU:24, one launch (start us, length us, event | category | flops | bytes accessed | tf_op | source)
XLA Modules:
  0.0 82.9 jit_solution(14261945797539026943)
XLA Ops:
  1.9 39.7 %shard_map.67 = (f32[512,1280]{1,0:T(8,128)}, f32[256,1152]{1,0:T(8,128)}, f32[16,1152]{1,0:T(8,128)}, f32[16,128]{1,0:T(8,128)}, f32[16,1152]{1,0:T(8,128)}, /*index=5*/f32[16,128]{1,0:T(8,128)}) custom-call(bf16[16,1152]{1,0:T(8,128)(2,1)} %image_raw.1, bf16[16,1152]{1,0:T(8,128)(2,1)} %text_raw.1, f32[1,1]{1,0:T(1,128)} %bitcast.4.scale_ref, ...), custom_call_target="tpu_custom_call" | custom-call | tf_op jit(solution)/shard_map/pallas_call | solution.py:293
  41.6 37.9 %shard_map.68 = (f32[16,16,1280]{2,1,0:T(8,128)}, f32[16,1152]{1,0:T(8,128)}) custom-call(f32[2,16,16,1280]{3,2,1,0:T(8,128)} %bitcast.6, f32[16,16,1152]{2,1,0:T(8,128)} %bitcast.7), custom_call_target="tpu_custom_call" | custom-call | tf_op jit(solution)/shard_map/pallas_call | solution.py:269
  79.5 0.0 copy-start
  79.5 0.0 copy-start.1
  79.5 0.0 copy-start.2
  79.5 0.0 copy-start.4
  79.5 0.0 copy-start.3
  79.5 1.5 %reduce_sum.27 = f32[16,1280]{1,0:T(8,128)S(1)} reduce(f32[16,16,1280]{2,1,0:T(8,128)} %get-tuple-element.13, f32[]{:T(128)} %constant.0.clone.1), dimensions={0}, to_apply=%region_0.0 | reduce | flops 307200 | bytes 1392644 | tf_op jit(solution)/shard_map/reduce_sum | solution.py:421
  81.0 0.0 copy-done
  81.0 0.1 multiply_reduce_fusion.1
  81.1 0.6 slice_reduce_fusion
  81.7 0.0 copy-done.1
  81.7 0.0 copy-done.2
  81.7 0.1 multiply_reduce_fusion
  81.9 0.0 copy-done.4
  81.9 0.1 slice_reduce_fusion.2
  82.0 0.0 copy-done.3
  82.0 0.1 slice_reduce_fusion.1
  82.1 0.8 subtract_divide_fusion
Async XLA Ops:
  79.5 1.5 %copy-start = (f32[16,1152]{1,0:T(8,128)S(1)}, f32[16,1152]{1,0:T(8,128)}, u32[]{:S(2)}) copy-start(f32[16,1152]{1,0:T(8,128)} %get-tuple-element.14) | copy-start | bytes 221188
  79.5 2.3 %copy-start.1 = (f32[16,1152]{1,0:T(8,128)S(1)}, f32[16,1152]{1,0:T(8,128)}, u32[]{:S(2)}) copy-start(f32[16,1152]{1,0:T(8,128)} %get-tuple-element.17) | copy-start | bytes 221188
  79.5 2.3 %copy-start.2 = (f32[16,1152]{1,0:T(8,128)S(1)}, f32[16,1152]{1,0:T(8,128)}, u32[]{:S(2)}) copy-start(f32[16,1152]{1,0:T(8,128)} %get-tuple-element.16) | copy-start | bytes 221188
  79.5 2.4 %copy-start.4 = (f32[16,128]{1,0:T(8,128)S(1)}, f32[16,128]{1,0:T(8,128)}, u32[]{:S(2)}) copy-start(f32[16,128]{1,0:T(8,128)} %get-tuple-element.15) | copy-start | bytes 24580
  79.5 2.5 %copy-start.3 = (f32[16,128]{1,0:T(8,128)S(1)}, f32[16,128]{1,0:T(8,128)}, u32[]{:S(2)}) copy-start(f32[16,128]{1,0:T(8,128)} %get-tuple-element.18) | copy-start | bytes 24580

commit v23 on v20

--- a/solution.py
+++ b/solution.py
@@ -106,7 +106,6 @@
     right2 = member(TEXT_AXES, (me + 2) % count)
     left2 = member(TEXT_AXES, (me + count - 2) % count)
     greet_all(image_axes, pltpu.get_barrier_semaphore(), image_count, image_me, right, left, (right2, left2))
-    finish = image_direct(image_axes, False, image_src, image_out, image_send, image_recv, image_count, image_me)
     sends = []
 
     def send(src, origin, device, slot):
@@ -121,6 +120,7 @@
     for slot, device in ((0, right), (1, right2), (half, left), (half + 1, left2)):
         send(text_src, me, device, slot)
     text_out[me] = text_src[...]
+    finish = image_direct(image_axes, False, image_src, image_out, image_send, image_recv, image_count, image_me)
     slot_right, slot_left = 2, half + 2
     for step in range(2, half // 2 + 1):
         for distance in (2 * step - 3, 2 * step - 2):

time: 80.9 us -> 79.7 us (0.985)
  Pallas kernels: 75.3 us -> 74.1 us
where the time goes in v23:
time: 79.7 us; the launch traced here: 79.5 us
  Pallas kernels  74.1 us (93%)
  other arithmetic  2.48 us (3%)
  between operations  1.99 us (2%)
  local copies, waits for them, and re-layouts  0.87 us (1%)
    pallas_call x1, Pallas kernels, gather_compute(): pl.pallas_call(functools.partial(gather_kernel, image_axes), out_shape=(j...  39 us
    pallas_call x1, Pallas kernels, merged_reduce(): pl.pallas_call(functools.partial(merged_reduce_kernel, image_axes), out_s...  35.1 us

profile of v23, /device:TPU:24, one launch (start us, length us, event | category | flops | bytes accessed | tf_op | source)
XLA Modules:
  0.0 79.5 jit_solution(16961340621124937236)
XLA Ops:
  1.9 39.0 %shard_map.67 = (f32[512,1280]{1,0:T(8,128)}, f32[256,1152]{1,0:T(8,128)}, f32[16,1152]{1,0:T(8,128)}, f32[16,128]{1,0:T(8,128)}, f32[16,1152]{1,0:T(8,128)}, /*index=5*/f32[16,128]{1,0:T(8,128)}) custom-call(bf16[16,1152]{1,0:T(8,128)(2,1)} %image_raw.1, bf16[16,1152]{1,0:T(8,128)(2,1)} %text_raw.1, f32[1,1]{1,0:T(1,128)} %bitcast.4.scale_ref, ...), custom_call_target="tpu_custom_call" | custom-call | tf_op jit(solution)/shard_map/pallas_call | solution.py:293
  40.9 35.1 %shard_map.68 = (f32[16,16,1280]{2,1,0:T(8,128)}, f32[16,1152]{1,0:T(8,128)}) custom-call(f32[2,16,16,1280]{3,2,1,0:T(8,128)} %bitcast.6, f32[16,16,1152]{2,1,0:T(8,128)} %bitcast.7), custom_call_target="tpu_custom_call" | custom-call | tf_op jit(solution)/shard_map/pallas_call | solution.py:269
  76.1 0.0 copy-start
  76.1 0.0 copy-start.1
  76.1 0.0 copy-start.2
  76.1 0.0 copy-start.4
  76.1 0.0 copy-start.3
  76.1 1.5 %reduce_sum.27 = f32[16,1280]{1,0:T(8,128)S(1)} reduce(f32[16,16,1280]{2,1,0:T(8,128)} %get-tuple-element.13, f32[]{:T(128)} %constant.0.clone.1), dimensions={0}, to_apply=%region_0.0 | reduce | flops 307200 | bytes 1392644 | tf_op jit(solution)/shard_map/reduce_sum | solution.py:421
  77.6 0.0 copy-done
  77.6 0.1 multiply_reduce_fusion.1
  77.7 0.6 slice_reduce_fusion
  78.3 0.0 copy-done.1
  78.4 0.0 copy-done.2
  78.4 0.1 multiply_reduce_fusion
  78.5 0.0 copy-done.4
  78.5 0.1 slice_reduce_fusion.2
  78.6 0.0 copy-done.3
  78.6 0.1 slice_reduce_fusion.1
  78.7 0.8 subtract_divide_fusion
Async XLA Ops:
  76.1 1.5 %copy-start = (f32[16,1152]{1,0:T(8,128)S(1)}, f32[16,1152]{1,0:T(8,128)}, u32[]{:S(2)}) copy-start(f32[16,1152]{1,0:T(8,128)} %get-tuple-element.14) | copy-start | bytes 221188
  76.1 2.3 %copy-start.1 = (f32[16,1152]{1,0:T(8,128)S(1)}, f32[16,1152]{1,0:T(8,128)}, u32[]{:S(2)}) copy-start(f32[16,1152]{1,0:T(8,128)} %get-tuple-element.17) | copy-start | bytes 221188
  76.1 2.3 %copy-start.2 = (f32[16,1152]{1,0:T(8,128)S(1)}, f32[16,1152]{1,0:T(8,128)}, u32[]{:S(2)}) copy-start(f32[16,1152]{1,0:T(8,128)} %get-tuple-element.16) | copy-start | bytes 221188
  76.1 2.4 %copy-start.4 = (f32[16,128]{1,0:T(8,128)S(1)}, f32[16,128]{1,0:T(8,128)}, u32[]{:S(2)}) copy-start(f32[16,128]{1,0:T(8,128)} %get-tuple-element.15) | copy-start | bytes 24580
  76.1 2.5 %copy-start.3 = (f32[16,128]{1,0:T(8,128)S(1)}, f32[16,128]{1,0:T(8,128)}, u32[]{:S(2)}) copy-start(f32[16,128]{1,0:T(8,128)} %get-tuple-element.18) | copy-start | bytes 24580

commit v24 on v23

--- a/solution.py
+++ b/solution.py
@@ -231,9 +231,9 @@
             copy.start()
             sends.append(copy)
 
+    step_sends(1)
     swap = remote(image_src.at[1 - core], halfbox, half_sems.at[0], half_sems.at[1], partner)
     swap.start()
-    step_sends(1)
     step_sends(2)
     swap.wait_recv()
     summed[...] = image_src[core] + halfbox[...]

time: 79.7 us -> 79.7 us (level)
  no operation moved by 1% of the time
where the time goes in v24:
time: 79.7 us; the launch traced here: 79.5 us
  Pallas kernels  74.1 us (93%)
  other arithmetic  2.48 us (3%)
  between operations  1.99 us (2%)
  local copies, waits for them, and re-layouts  0.87 us (1%)
    pallas_call x1, Pallas kernels, gather_compute(): pl.pallas_call(functools.partial(gather_kernel, image_axes), out_shape=(j...  39 us
    pallas_call x1, Pallas kernels, merged_reduce(): pl.pallas_call(functools.partial(merged_reduce_kernel, image_axes), out_s...  35.1 us

profile of v24, /device:TPU:24, one launch (start us, length us, event | category | flops | bytes accessed | tf_op | source)
XLA Modules:
  0.0 79.5 jit_solution(9585671515026556784)
XLA Ops:
  1.9 39.0 %shard_map.67 = (f32[512,1280]{1,0:T(8,128)}, f32[256,1152]{1,0:T(8,128)}, f32[16,1152]{1,0:T(8,128)}, f32[16,128]{1,0:T(8,128)}, f32[16,1152]{1,0:T(8,128)}, /*index=5*/f32[16,128]{1,0:T(8,128)}) custom-call(bf16[16,1152]{1,0:T(8,128)(2,1)} %image_raw.1, bf16[16,1152]{1,0:T(8,128)(2,1)} %text_raw.1, f32[1,1]{1,0:T(1,128)} %bitcast.4.scale_ref, ...), custom_call_target="tpu_custom_call" | custom-call | tf_op jit(solution)/shard_map/pallas_call | solution.py:293
  40.9 35.1 %shard_map.68 = (f32[16,16,1280]{2,1,0:T(8,128)}, f32[16,1152]{1,0:T(8,128)}) custom-call(f32[2,16,16,1280]{3,2,1,0:T(8,128)} %bitcast.6, f32[16,16,1152]{2,1,0:T(8,128)} %bitcast.7), custom_call_target="tpu_custom_call" | custom-call | tf_op jit(solution)/shard_map/pallas_call | solution.py:269
  76.1 0.0 copy-start
  76.1 0.0 copy-start.1
  76.1 0.0 copy-start.2
  76.1 0.0 copy-start.4
  76.1 0.0 copy-start.3
  76.1 1.5 %reduce_sum.27 = f32[16,1280]{1,0:T(8,128)S(1)} reduce(f32[16,16,1280]{2,1,0:T(8,128)} %get-tuple-element.13, f32[]{:T(128)} %constant.0.clone.1), dimensions={0}, to_apply=%region_0.0 | reduce | flops 307200 | bytes 1392644 | tf_op jit(solution)/shard_map/reduce_sum | solution.py:421
  77.6 0.0 copy-done
  77.6 0.1 multiply_reduce_fusion.1
  77.7 0.6 slice_reduce_fusion
  78.3 0.0 copy-done.1
  78.4 0.0 copy-done.2
  78.4 0.1 multiply_reduce_fusion
  78.5 0.0 copy-done.4
  78.5 0.1 slice_reduce_fusion.2
  78.6 0.0 copy-done.3
  78.6 0.1 slice_reduce_fusion.1
  78.7 0.8 subtract_divide_fusion
Async XLA Ops:
  76.1 1.5 %copy-start = (f32[16,1152]{1,0:T(8,128)S(1)}, f32[16,1152]{1,0:T(8,128)}, u32[]{:S(2)}) copy-start(f32[16,1152]{1,0:T(8,128)} %get-tuple-element.14) | copy-start | bytes 221188
  76.1 2.3 %copy-start.1 = (f32[16,1152]{1,0:T(8,128)S(1)}, f32[16,1152]{1,0:T(8,128)}, u32[]{:S(2)}) copy-start(f32[16,1152]{1,0:T(8,128)} %get-tuple-element.17) | copy-start | bytes 221188
  76.1 2.3 %copy-start.2 = (f32[16,1152]{1,0:T(8,128)S(1)}, f32[16,1152]{1,0:T(8,128)}, u32[]{:S(2)}) copy-start(f32[16,1152]{1,0:T(8,128)} %get-tuple-element.16) | copy-start | bytes 221188
  76.1 2.4 %copy-start.4 = (f32[16,128]{1,0:T(8,128)S(1)}, f32[16,128]{1,0:T(8,128)}, u32[]{:S(2)}) copy-start(f32[16,128]{1,0:T(8,128)} %get-tuple-element.15) | copy-start | bytes 24580
  76.1 2.5 %copy-start.3 = (f32[16,128]{1,0:T(8,128)S(1)}, f32[16,128]{1,0:T(8,128)}, u32[]{:S(2)}) copy-start(f32[16,128]{1,0:T(8,128)} %get-tuple-element.18) | copy-start | bytes 24580
